TPU v7x, 128 devices: a whole 4x4x4 slice. The times are simulated.
128 devices in a mesh: cuts: 4 (over z), tile: 32 (over x, y, core).
Axes of the slice: x: 4, y: 4, z: 4, core: 2. Of those that a mesh axis runs over, the one named last changes fastest.
Arguments:
- probe_wave: float32 [2, 256, 256], replicated, may hold values from -6 to 6
- transmission: float32 [4, 2, 4096, 8192], P('cuts', None, None, 'tile'), may hold values from -1 to 1, as said below
- kernel_phase: float32 [256, 256], replicated, may hold values from -3.140625 to 3.140625
- measured: bfloat16 [32, 6, 256, 256], P('tile'), may hold values from 0 to 4
- counts: int32 [32], P('tile'), may hold values from 1 to 6, as said below
- positions: int32 [32, 6, 2], P('tile'), may hold values from 0 to 3840, as said below
- widths: int32 [32, 2], P('tile'), may hold values from 32 to 128
Outputs:
- adjoint_wave: float32 [4, 32, 6, 2, 256, 256], P('cuts', 'tile')
- object_grad: float32 [4, 2, 4096, 8192], P('cuts', None, None, 'tile')
Inputs may be any that keep to these rules, and one draw needn't show every extreme that they name: Every entry has magnitude at most 1; each pair is a complex transmission. Tile t uses its first counts[t] slots; some tile uses all 6 slots. `positions`: rows lie in 0 to 3840 and columns in 0 to 256; column 0 of a tile's extended patch is 128 columns left of its first own column.
All inputs are finite; a program needn't handle non-finite values.
Results may differ from a plain program's by a relative error of at most 0.0003.
Values sent between devices are 32-bit elements; how exact they have to be, the bound alone decides.
No kernel may reach another device: no remote copies, remote signals or barrier semaphores. Data moves between devices by JAX's collectives and lax.ppermute only.
A program may use at most 256 MiB of HBM per device.

v0:
```python
import math

import jax
import jax.numpy as jnp
from jax import lax
from jax.sharding import PartitionSpec as P

RIM = 128


def extended(value, sides, width):
    for axis, dim in sides:
        count, length = (lax.axis_size(axis), value.shape[dim])
        up = [(i, (i + 1) % count) for i in range(count - 1)]
        down = [(j, i) for i, j in up]
        last = lax.slice_in_dim(value, length - width, length, axis=dim)
        initial = lax.slice_in_dim(value, 0, width, axis=dim)
        before = lax.ppermute(last, axis, up)
        after = lax.ppermute(initial, axis, down)
        value = jnp.concatenate([before, value, after], axis=dim)
    return value


def from_behind(value, axis, by):
    count = lax.axis_size(axis)
    pairs = [(i, i + by) for i in range(count) if 0 <= i + by < count]
    return lax.ppermute(value, axis, pairs)


def make_tables(extent):
    indices = jnp.arange(extent, dtype=jnp.int32)
    product = indices[:, None] * indices[None, :] % extent
    angles = product.astype(jnp.float32) * (2.0 * math.pi / extent)
    cosine = jnp.cos(angles) / math.sqrt(extent)
    sine_part = jnp.sin(angles) / math.sqrt(extent)
    forward = jnp.concatenate(
        [jnp.concatenate([cosine, sine_part], 1), jnp.concatenate([-sine_part, cosine], 1)], 0
    )
    inverse = jnp.concatenate(
        [jnp.concatenate([cosine, -sine_part], 1), jnp.concatenate([sine_part, cosine], 1)], 0
    )
    return (forward, inverse)


def transform(fields, matrix):
    number = fields.shape[0]
    extent = fields.shape[-1]
    stacked = fields.reshape(number, 2 * extent, extent)
    halfway = jnp.einsum("ab,pbc->pac", matrix, stacked, precision=lax.Precision.HIGHEST)
    halfway = halfway.reshape(number, 2, extent, extent)
    quadrant = matrix.reshape(2, extent, 2, extent)
    return jnp.einsum("psik,rjsk->prij", halfway, quadrant, precision=lax.Precision.HIGHEST)


def complex_mul(first_op, second_op):
    first_re, first_im = (first_op[..., 0, :, :], first_op[..., 1, :, :])
    second_re, second_im = (second_op[..., 0, :, :], second_op[..., 1, :, :])
    return jnp.stack(
        [first_re * second_re - first_im * second_im, first_re * second_im + first_im * second_re],
        axis=-3,
    )


def conj_mul(first_op, second_op):
    first_re, first_im = (first_op[..., 0, :, :], first_op[..., 1, :, :])
    second_re, second_im = (second_op[..., 0, :, :], second_op[..., 1, :, :])
    return jnp.stack(
        [first_re * second_re + first_im * second_im, first_re * second_im - first_im * second_re],
        axis=-3,
    )


def propagate(fields, kernel, tables):
    spectrum = transform(fields, tables[0])
    return transform(complex_mul(kernel, spectrum), tables[1])


def keep_columns(tile_at, width_pair, tiles_total, owned_cols, margin):
    columns = jnp.arange(owned_cols + 2 * margin, dtype=jnp.int32)
    globally = tile_at * owned_cols - margin + columns
    inside = (globally >= 0) & (globally < tiles_total * owned_cols)
    middle = (columns >= margin) & (columns < margin + owned_cols)
    left_ok = (columns < margin) & (margin - columns <= width_pair[0])
    right_ok = (columns >= margin + owned_cols) & (
        columns - margin - owned_cols + 1 <= width_pair[1]
    )
    return inside & (middle | left_ok | right_ok)


def cut_windows(grad_plane, places, extent):
    anchor = jnp.zeros((), jnp.int32)

    def single(corner):
        return lax.dynamic_slice(grad_plane, (anchor, corner[0], corner[1]), (2, extent, extent))

    return jax.vmap(single)(places)


def add_windows(grad_plane, places, contrib, extent):
    anchor = jnp.zeros((), jnp.int32)
    corner_at = (anchor, places[0, 0], places[0, 1])
    current = lax.dynamic_slice(grad_plane, corner_at, (2, extent, extent))
    grad_plane = lax.dynamic_update_slice(grad_plane, current + contrib[0], corner_at)
    return grad_plane


def on_device(probe_wave, transmission, kernel_phase, measured, counts, positions, widths):
    slices_here = transmission.shape[0]
    owned_cols = transmission.shape[3]
    extent = probe_wave.shape[-1]
    margin = RIM
    sections = lax.axis_size("cuts")
    section_at = lax.axis_index("cuts")
    tile_at = lax.axis_index("tile")
    tiles_total = lax.axis_size("tile")
    capacity = positions.shape[1]
    last_section = sections - 1
    tables = make_tables(extent)
    kernel = jnp.stack([jnp.cos(kernel_phase), jnp.sin(kernel_phase)], 0)
    kernel_conj = jnp.stack([jnp.cos(kernel_phase), -jnp.sin(kernel_phase)], 0)
    vacuum = jnp.array([1.0, 0.0], dtype=jnp.float32)[:, None, None]
    object_patch = extended(transmission, (("tile", 3),), margin)
    keep_mask = keep_columns(tile_at, widths[0], tiles_total, owned_cols, margin)
    object_patch = jnp.where(keep_mask, object_patch, vacuum)
    places = positions[0]
    live_slots = (jnp.arange(capacity, dtype=jnp.int32) < counts[0]).astype(jnp.float32)
    entering = probe_wave[None] * live_slots[:, None, None, None]
    members = capacity // capacity
    rounds = capacity + sections - 1
    wave_shape = (members, 2, extent, extent)

    def run_forward(fields, spot_rows):
        windows = cut_windows(object_patch[0], spot_rows, extent)
        inputs = [fields]
        fields = propagate(complex_mul(windows, fields), kernel, tables)
        return (jnp.stack(inputs, 0), fields)

    def skip_forward(fields, spot_rows):
        return (
            jnp.zeros((slices_here,) + wave_shape, jnp.float32),
            jnp.zeros(wave_shape, jnp.float32),
        )

    saved_waves = jnp.zeros((capacity + 1, slices_here) + wave_shape, jnp.float32)
    exit_waves = jnp.zeros((capacity + 1,) + wave_shape, jnp.float32)
    arriving = jnp.zeros(wave_shape, jnp.float32)
    for round_at in range(rounds):
        batch_at = round_at - section_at
        is_valid = (batch_at >= 0) & (batch_at < capacity)
        slot_at = jnp.where(is_valid, batch_at, capacity)
        first_row = jnp.clip(batch_at, 0, capacity - 1) * members
        fields = jnp.where(
            section_at == 0, lax.dynamic_slice_in_dim(entering, first_row, members, 0), arriving
        )
        spot_rows = lax.dynamic_slice_in_dim(places, first_row, members, 0)
        inputs, leaving = lax.cond(is_valid, run_forward, skip_forward, fields, spot_rows)
        saved_waves = lax.dynamic_update_slice_in_dim(saved_waves, inputs[None], slot_at, 0)
        exit_waves = lax.dynamic_update_slice_in_dim(exit_waves, leaving[None], slot_at, 0)
        if round_at + 1 < rounds:
            arriving = from_behind(leaving, "cuts", 1)

    def run_adjoint(grad_ext, fields, inputs, spot_rows):
        for slice_at in reversed(range(slices_here)):
            turned = propagate(fields, kernel_conj, tables)
            contrib = conj_mul(inputs[slice_at], turned)
            grad_plane = add_windows(grad_ext[slice_at], spot_rows, contrib, extent)
            grad_ext = grad_ext.at[slice_at].set(grad_plane)
            windows = cut_windows(object_patch[slice_at], spot_rows, extent)
            fields = conj_mul(windows, turned)
        return (grad_ext, fields)

    def skip_adjoint(grad_ext, fields, inputs, spot_rows):
        return (grad_ext, jnp.zeros(wave_shape, jnp.float32))

    def far_adjoint(fields, observed):
        far_field = transform(fields, tables[0])
        intensity = far_field[:, 0] * far_field[:, 0] + far_field[:, 1] * far_field[:, 1]
        residual = intensity - observed.astype(jnp.float32)
        return transform(far_field * residual[:, None], tables[1])

    def skip_far(fields, observed):
        return jnp.zeros(wave_shape, jnp.float32)

    grad_ext = jnp.zeros(object_patch.shape, jnp.float32)
    adjoints = jnp.zeros((capacity + 1,) + wave_shape, jnp.float32)
    arriving = jnp.zeros(wave_shape, jnp.float32)
    for round_at in range(rounds):
        batch_at = round_at - (last_section - section_at)
        is_valid = (batch_at >= 0) & (batch_at < capacity)
        slot_at = jnp.where(is_valid, batch_at, capacity)
        clipped = jnp.clip(batch_at, 0, capacity - 1)
        first_row = clipped * members
        spot_rows = lax.dynamic_slice_in_dim(places, first_row, members, 0)
        observed = lax.dynamic_slice_in_dim(measured[0], first_row, members, 0)
        exit_now = lax.dynamic_index_in_dim(exit_waves, clipped, 0, keepdims=False)
        starting = lax.cond(
            is_valid & (section_at == last_section), far_adjoint, skip_far, exit_now, observed
        )
        fields = jnp.where(section_at == last_section, starting, arriving)
        inputs = lax.dynamic_index_in_dim(saved_waves, clipped, 0, keepdims=False)
        grad_ext, backward = lax.cond(
            is_valid, run_adjoint, skip_adjoint, grad_ext, fields, inputs, spot_rows
        )
        adjoints = lax.dynamic_update_slice_in_dim(adjoints, backward[None], slot_at, 0)
        if round_at + 1 < rounds:
            arriving = from_behind(backward, "cuts", -1)
    adjoint_wave = adjoints[:capacity].reshape((capacity, 2, extent, extent))[None, None]
    grad_ext = jnp.where(keep_mask, grad_ext, 0.0)
    rim_pair = jnp.concatenate([grad_ext[..., :margin], grad_ext[..., margin + owned_cols :]], 3)
    widened = extended(rim_pair, (("tile", 3),), margin)
    center = grad_ext[..., margin : margin + owned_cols]
    center = center.at[..., :margin].add(widened[..., :margin])
    center = center.at[..., owned_cols - margin :].add(widened[..., 3 * margin :])
    return (adjoint_wave, center)


def solution(mesh):
    return jax.shard_map(
        on_device,
        mesh=mesh,
        in_specs=(
            P(),
            P("cuts", None, None, "tile"),
            P(),
            P("tile", None, None, None),
            P("tile"),
            P("tile", None, None),
            P("tile", None),
        ),
        out_specs=(P("cuts", "tile", None, None, None, None), P("cuts", None, None, "tile")),
        check_vma=False,
    )
```

profile of v0, /device:TPU:30, one launch (start us, length us, event | category | flops | bytes accessed | tf_op | source)
XLA Modules:
  0.0 1022.0 jit_solution(3378046043266242784)
XLA Ops:
  0.6 7.4 fusion.146
  22.4 34.2 %collective-permute-done.1 = f32[1,2,4096,128]{3,2,1,0:T(8,128)} collective-permute-done((f32[1,2,4096,128]{3,2,1,0:T(8,128)}, f32[1,2,4096,128]{3,2,1,0:T(8,128)}, u32[]{:S(2)}, u32[]{:S(2)}) %collective-permute-start.1) | collective-permute-done | bytes 4194336 | tf_op jit(solution)/shard_map/ppermute | solution.py:19
  60.4 12.0 %maximum_select_fusion = f32[1,2,4096,512]{3,2,1,0:T(8,128)} fusion(f32[1,2,4096,128]{3,2,1,0:T(8,128)} %collective-permute-done.1, f32[1,2,4096,256]{3,2,1,0:T(8,128)} %param.85, f32[1,2,4096,128]{3,2,1,0:T(8,128)} %collective-permute-done, f32[2]{0:T(128)S(1)} %copy-done.20, pred[512]{0:T(512)(128)(4,1)S(1)} %fusion.121), kind=kLoop, calls=%fused_computation.450 | loop fusion | flops 12582912 | bytes 33554952 | tf_op jit(solution)/shard_map/jit(_where)/select_n | solution.py:124
  73.3 28.2 %conditional.27 = (f32[1,2,256,256]{3,2,1,0:T(8,128)}, f32[1,1,1,2,256,256]{5,4,3,2,1,0:T(8,128)S(1)}, f32[1,1,2,256,256]{4,3,2,1,0:T(8,128)}) conditional(s32[]{:T(128)} %convert_element_type.187, () %tuple.413, (f32[1,2,4096,512]{3,2,1,0:T(8,128)}, s32[]{:T(128)}, s32[1,6,2]{1,2,0:T(2,128)S(1)}, f32[6,2,256,256]{3,2,1,0:T(8,128)}, ...), branch_computations={%region_0.1_spmd, %region_1.2_spmd} | conditional | flops 3222405120 | bytes 26870092 | solution.py:156
  103.6 11.7 %collective-permute-done.2 = f32[1,2,256,256]{3,2,1,0:T(8,128)} collective-permute-done((f32[1,2,256,256]{3,2,1,0:T(8,128)}, f32[1,2,256,256]{3,2,1,0:T(8,128)}, u32[]{:S(2)}, u32[]{:S(2)}) %collective-permute-start.2) | collective-permute-done | bytes 524320 | tf_op jit(solution)/shard_map/ppermute | solution.py:27
  115.3 28.8 %conditional.28 = (f32[1,2,256,256]{3,2,1,0:T(8,128)}, f32[1,1,1,2,256,256]{5,4,3,2,1,0:T(8,128)}, f32[1,1,2,256,256]{4,3,2,1,0:T(8,128)}) conditional(s32[]{:T(128)} %convert_element_type.190, () %tuple.415, (f32[1,2,4096,512]{3,2,1,0:T(8,128)}, s32[]{:T(128)}, s32[1,6,2]{1,2,0:T(2,128)S(1)}, f32[6,2,256,256]{3,2,1,0:T(8,128)}, ...), branch_computations={%region_2.3_spmd, %region_3.4_spmd} | conditional | flops 3222405120 | bytes 22675732 | solution.py:156
  149.3 10.5 %collective-permute-done.3 = f32[1,2,256,256]{3,2,1,0:T(8,128)} collective-permute-done((f32[1,2,256,256]{3,2,1,0:T(8,128)}, f32[1,2,256,256]{3,2,1,0:T(8,128)}, u32[]{:S(2)}, u32[]{:S(2)}) %collective-permute-start.3) | collective-permute-done | bytes 524320 | tf_op jit(solution)/shard_map/ppermute | solution.py:27
  159.8 28.4 %conditional.29 = (f32[1,2,256,256]{3,2,1,0:T(8,128)}, f32[1,1,1,2,256,256]{5,4,3,2,1,0:T(8,128)}, f32[1,1,2,256,256]{4,3,2,1,0:T(8,128)}) conditional(s32[]{:T(128)} %convert_element_type.191, () %tuple.417, (f32[1,2,4096,512]{3,2,1,0:T(8,128)}, s32[]{:T(128)}, s32[1,6,2]{1,2,0:T(2,128)S(1)}, f32[6,2,256,256]{3,2,1,0:T(8,128)}, ...), branch_computations={%region_4.5_spmd, %region_5.6_spmd} | conditional | flops 3222405120 | bytes 22675732 | solution.py:156
  193.6 9.2 collective-permute-done.4
  202.8 28.3 %conditional.30 = (f32[1,2,256,256]{3,2,1,0:T(8,128)}, f32[1,1,1,2,256,256]{5,4,3,2,1,0:T(8,128)}, f32[1,1,2,256,256]{4,3,2,1,0:T(8,128)}) conditional(s32[]{:T(128)} %convert_element_type.192, () %tuple.419, (f32[1,2,4096,512]{3,2,1,0:T(8,128)}, s32[]{:T(128)}, s32[1,6,2]{1,2,0:T(2,128)S(1)}, f32[6,2,256,256]{3,2,1,0:T(8,128)}, ...), branch_computations={%region_6.7_spmd, %region_7.8_spmd} | conditional | flops 3222405120 | bytes 22675732 | solution.py:156
  236.6 8.4 collective-permute-done.5
  245.0 28.5 %conditional.31 = (f32[1,2,256,256]{3,2,1,0:T(8,128)}, f32[1,1,1,2,256,256]{5,4,3,2,1,0:T(8,128)}, f32[1,1,2,256,256]{4,3,2,1,0:T(8,128)}) conditional(s32[]{:T(128)} %convert_element_type.193, () %tuple.421, (f32[1,2,4096,512]{3,2,1,0:T(8,128)}, s32[]{:T(128)}, s32[1,6,2]{1,2,0:T(2,128)S(1)}, f32[6,2,256,256]{3,2,1,0:T(8,128)}, ...), branch_computations={%region_8.9_spmd, %region_9.10_spmd} | conditional | flops 3222405120 | bytes 22675732 | solution.py:156
  286.5 28.4 %conditional.32 = (f32[1,2,256,256]{3,2,1,0:T(8,128)}, f32[1,1,1,2,256,256]{5,4,3,2,1,0:T(8,128)S(1)}, f32[1,1,2,256,256]{4,3,2,1,0:T(8,128)}) conditional(s32[]{:T(128)} %convert_element_type.194, () %tuple.423, (f32[1,2,4096,512]{3,2,1,0:T(8,128)}, s32[]{:T(128)}, s32[1,6,2]{1,2,0:T(2,128)S(1)}, f32[6,2,256,256]{3,2,1,0:T(8,128)}, ...), branch_computations={%region_10.11_spmd, %region_11.12_spmd} | conditional | flops 3222405120 | bytes 28967272 | solution.py:156
  330.2 30.0 %collective-permute-start.8 = (f32[1,2,256,256]{3,2,1,0:T(8,128)}, f32[1,2,256,256]{3,2,1,0:T(8,128)}, u32[]{:S(2)}, u32[]{:S(2)}) collective-permute-start(f32[1,2,256,256]{3,2,1,0:T(8,128)} %get-tuple-element.2297), channel_id=1, source_target_pairs={{0,32},{32,64},{64,96},{1,33},{33,65},{65,97},{2,34},{34,66},{66,9... | collective-permute-start | bytes 1572872 | tf_op jit(solution)/shard_map/ppermute | solution.py:27
  387.9 9.8 conditional.37
  387.9 7.9 broadcast_in_dim.421
  403.5 30.7 %collective-permute-done.10 = f32[1,2,256,256]{3,2,1,0:T(8,128)} collective-permute-done((f32[1,2,256,256]{3,2,1,0:T(8,128)}, f32[1,2,256,256]{3,2,1,0:T(8,128)}, u32[]{:S(2)}, u32[]{:S(2)}) %collective-permute-start.10) | collective-permute-done | bytes 524320 | tf_op jit(solution)/shard_map/ppermute | solution.py:27
  451.1 11.0 %conditional.42 = (f32[1,2,256,256]{3,2,1,0:T(8,128)S(1)}) conditional(s32[]{:T(128)} %convert_element_type.204, () %tuple.440, (f32[7,1,2,256,256]{4,3,2,0,1:T(8,128)}, s32[]{:T(128)}, f32[512,512]{1,0:T(8,128)S(1)}, bf16[1,6,256,256]{3,2,1,0:T(8,128)(2,1)}, f32[512,512]{1,0:T(8,128)S(1)}) %tuple.441), branch_computations={%region_30.31_spmd, %region_31.32_spmd} | conditional | flops 3221684224 | bytes 17956880 | solution.py:196
  462.1 149.8 %collective-permute-done.12 = f32[1,2,256,256]{3,2,1,0:T(8,128)} collective-permute-done((f32[1,2,256,256]{3,2,1,0:T(8,128)}, f32[1,2,256,256]{3,2,1,0:T(8,128)}, u32[]{:S(2)}, u32[]{:S(2)}) %collective-permute-start.12) | collective-permute-done | bytes 524320 | tf_op jit(solution)/shard_map/ppermute | solution.py:27
  612.0 39.3 %conditional.43 = (f32[1,2,4096,512]{3,2,1,0:T(8,128)}, f32[1,2,256,256]{3,2,1,0:T(8,128)}, f32[1,1,2,256,256]{4,3,2,1,0:T(8,128)}) conditional(s32[]{:T(128)} %convert_element_type.203, f32[1,2,4096,512]{3,2,1,0:T(8,128)} %get-tuple-element.2317, (s32[1,6,2]{1,2,0:T(2,128)S(1)}, s32[]{:T(128)}, f32[1,2,4096,512]{3,2,1,0:T(8,128)}, ...), branch_computations={%region_32.33_spmd, %region_33.34_spmd} | conditional | flops 3223060480 | bytes 27394376 | solution.py:201
  659.6 10.9 %collective-permute-done.13 = f32[1,2,256,256]{3,2,1,0:T(8,128)} collective-permute-done((f32[1,2,256,256]{3,2,1,0:T(8,128)}, f32[1,2,256,256]{3,2,1,0:T(8,128)}, u32[]{:S(2)}, u32[]{:S(2)}) %collective-permute-start.13) | collective-permute-done | bytes 524320 | tf_op jit(solution)/shard_map/ppermute | solution.py:27
  670.5 39.3 %conditional.45 = (f32[1,2,4096,512]{3,2,1,0:T(8,128)}, f32[1,2,256,256]{3,2,1,0:T(8,128)}, f32[1,1,2,256,256]{4,3,2,1,0:T(8,128)}) conditional(s32[]{:T(128)} %convert_element_type.205, f32[1,2,4096,512]{3,2,1,0:T(8,128)} %get-tuple-element.2320, (s32[1,6,2]{1,2,0:T(2,128)S(1)}, s32[]{:T(128)}, f32[1,2,4096,512]{3,2,1,0:T(8,128)}, ...), branch_computations={%region_36.37_spmd, %region_37.38_spmd} | conditional | flops 3223060480 | bytes 27394376 | solution.py:201
  718.0 11.2 %collective-permute-done.14 = f32[1,2,256,256]{3,2,1,0:T(8,128)} collective-permute-done((f32[1,2,256,256]{3,2,1,0:T(8,128)}, f32[1,2,256,256]{3,2,1,0:T(8,128)}, u32[]{:S(2)}, u32[]{:S(2)}) %collective-permute-start.14) | collective-permute-done | bytes 524320 | tf_op jit(solution)/shard_map/ppermute | solution.py:27
  729.3 39.3 %conditional.47 = (f32[1,2,4096,512]{3,2,1,0:T(8,128)}, f32[1,2,256,256]{3,2,1,0:T(8,128)}, f32[1,1,2,256,256]{4,3,2,1,0:T(8,128)}) conditional(s32[]{:T(128)} %convert_element_type.207, f32[1,2,4096,512]{3,2,1,0:T(8,128)} %get-tuple-element.2323, (s32[1,6,2]{1,2,0:T(2,128)S(1)}, s32[]{:T(128)}, f32[1,2,4096,512]{3,2,1,0:T(8,128)}, ...), branch_computations={%region_40.41_spmd, %region_41.42_spmd} | conditional | flops 3223060480 | bytes 27394376 | solution.py:201
  770.4 18.4 %collective-permute-done.15 = f32[1,2,256,256]{3,2,1,0:T(8,128)} collective-permute-done((f32[1,2,256,256]{3,2,1,0:T(8,128)}, f32[1,2,256,256]{3,2,1,0:T(8,128)}, u32[]{:S(2)}, u32[]{:S(2)}) %collective-permute-start.15) | collective-permute-done | bytes 524320 | tf_op jit(solution)/shard_map/ppermute | solution.py:27
  788.7 39.7 %conditional.49 = (f32[1,2,4096,512]{3,2,1,0:T(8,128)}, f32[1,2,256,256]{3,2,1,0:T(8,128)}, f32[1,1,2,256,256]{4,3,2,1,0:T(8,128)}) conditional(s32[]{:T(128)} %convert_element_type.209, f32[1,2,4096,512]{3,2,1,0:T(8,128)} %get-tuple-element.2326, (s32[1,6,2]{1,2,0:T(2,128)S(1)}, s32[]{:T(128)}, f32[1,2,4096,512]{3,2,1,0:T(8,128)}, ...), branch_computations={%region_44.45_spmd, %region_45.46_spmd} | conditional | flops 3223060480 | bytes 27394376 | solution.py:201
  830.0 18.1 %collective-permute-done.16 = f32[1,2,256,256]{3,2,1,0:T(8,128)} collective-permute-done((f32[1,2,256,256]{3,2,1,0:T(8,128)}, f32[1,2,256,256]{3,2,1,0:T(8,128)}, u32[]{:S(2)}, u32[]{:S(2)}) %collective-permute-start.16) | collective-permute-done | bytes 524320 | tf_op jit(solution)/shard_map/ppermute | solution.py:27
  848.0 39.8 %conditional.51 = (f32[1,2,4096,512]{3,2,1,0:T(8,128)}, f32[1,2,256,256]{3,2,1,0:T(8,128)}, f32[1,1,2,256,256]{4,3,2,1,0:T(8,128)}) conditional(s32[]{:T(128)} %convert_element_type.211, f32[1,2,4096,512]{3,2,1,0:T(8,128)} %get-tuple-element.2329, (s32[1,6,2]{1,2,0:T(2,128)S(1)}, s32[]{:T(128)}, f32[1,2,4096,512]{3,2,1,0:T(8,128)}, ...), branch_computations={%region_48.49_spmd, %region_49.50_spmd} | conditional | flops 3223060480 | bytes 27394376 | solution.py:201
  889.6 23.2 %collective-permute-done.17 = f32[1,2,256,256]{3,2,1,0:T(8,128)} collective-permute-done((f32[1,2,256,256]{3,2,1,0:T(8,128)}, f32[1,2,256,256]{3,2,1,0:T(8,128)}, u32[]{:S(2)}, u32[]{:S(2)}) %collective-permute-start.17) | collective-permute-done | bytes 524320 | tf_op jit(solution)/shard_map/ppermute | solution.py:27
  912.8 31.6 %conditional.53 = (f32[1,2,4096,512]{3,2,1,0:T(8,128)}, f32[1,1,2,256,256]{4,3,2,1,0:T(8,128)S(1)}) conditional(s32[]{:T(128)} %convert_element_type.213, f32[1,2,4096,512]{3,2,1,0:T(8,128)} %get-tuple-element.2332, (s32[1,6,2]{1,2,0:T(2,128)S(1)}, s32[]{:T(128)}, f32[1,2,4096,512]{3,2,1,0:T(8,128)}, f32[7,1,1,2,256,256]{5,4,3,2,1,0:T(8,128)}, ...), branch_computations={%region_52.53_spmd, %region_53.54_spmd} | conditional | flops 3223060480 | bytes 26345792 | solution.py:201
  944.3 7.1 broadcast_select_fusion
  977.9 33.5 %collective-permute-done.18 = f32[1,2,4096,128]{3,2,1,0:T(8,128)} collective-permute-done((f32[1,2,4096,128]{3,2,1,0:T(8,128)}, f32[1,2,4096,128]{3,2,1,0:T(8,128)}, u32[]{:S(2)}, u32[]{:S(2)}) %collective-permute-start.18) | collective-permute-done | bytes 4194336 | tf_op jit(solution)/shard_map/ppermute | solution.py:18
  (360 shorter events, 515.1 us)
Async XLA Ops:
  0.6 14.5 %copy-start.19 = (s32[1,2]{1,0:T(1,128)S(1)}, s32[1,2]{1,0:T(1,128)}, u32[]{:S(2)}) copy-start(s32[1,2]{1,0:T(1,128)} %param.90) | copy-start | bytes 28
  8.0 11.3 %copy-start.16 = (f32[256,256]{1,0:T(8,128)S(1)}, f32[256,256]{1,0:T(8,128)}, u32[]{:S(2)}) copy-start(f32[256,256]{1,0:T(8,128)} %param.86) | copy-start | bytes 786436
  8.0 12.3 %copy-start.14 = (f32[2,256,256]{2,1,0:T(8,128)S(1)}, f32[2,256,256]{2,1,0:T(8,128)}, u32[]{:S(2)}) copy-start(f32[2,256,256]{2,1,0:T(8,128)} %param.84) | copy-start | bytes 1572868
  8.0 48.5 %collective-permute-start.1 = (f32[1,2,4096,128]{3,2,1,0:T(8,128)}, f32[1,2,4096,128]{3,2,1,0:T(8,128)}, u32[]{:S(2)}, u32[]{:S(2)}) collective-permute-start(f32[1,2,4096,128]{3,2,1,0:T(8,128)} %get-tuple-element.2939), channel_id=1, source_target_pairs={{1,0},{2,1},{3,2},{4,3},{5,4},{6,5},{7,6},{8,7},{9,8},{10,9},{11,1... | collective-permute-start | bytes 12582920 | tf_op jit(solution)/shard_map/ppermute | solution.py:19
  10.3 50.1 %collective-permute-start = (f32[1,2,4096,128]{3,2,1,0:T(8,128)}, f32[1,2,4096,128]{3,2,1,0:T(8,128)}, u32[]{:S(2)}, u32[]{:S(2)}) collective-permute-start(f32[1,2,4096,128]{3,2,1,0:T(8,128)} %get-tuple-element.2938), channel_id=1, source_target_pairs={{0,1},{1,2},{2,3},{3,4},{4,5},{5,6},{6,7},{7,8},{8,9},{9,10},{10,1... | collective-permute-start | bytes 12582920 | tf_op jit(solution)/shard_map/ppermute | solution.py:18
  17.1 43.4 %copy-start.17 = (pred[512]{0:T(512)(128)(4,1)}, pred[512]{0:T(512)(128)(4,1)S(1)}, u32[]{:S(2)}) copy-start(pred[512]{0:T(512)(128)(4,1)S(1)} %fusion.121) | copy-start | bytes 1540
  19.1 41.3 %copy-start.20 = (f32[2]{0:T(128)S(1)}, f32[2]{0:T(128)}, u32[]{:S(2)}) copy-start(f32[2]{0:T(128)} %constant.1123.clone) | copy-start | bytes 28
  22.4 50.9 %copy-start.15 = (s32[1,6,2]{1,2,0:T(2,128)S(1)}, s32[1,6,2]{1,2,0:T(2,128)}, u32[]{:S(2)}) copy-start(s32[1,6,2]{1,2,0:T(2,128)} %param.89) | copy-start | bytes 148
  74.9 12.5 %copy-start.4 = (f32[1,2,256,256]{3,2,1,0:T(8,128)}, f32[1,2,256,256]{3,2,1,0:T(8,128)S(1)}, u32[]{:S(2)}) copy-start(f32[1,2,256,256]{3,2,1,0:T(8,128)S(1)} %dynamic-slice_select_fusion) | copy-start | bytes 1572868 | tf_op jit(solution)/shard_map/cond
  92.6 8.9 copy-start.5
  101.5 13.8 %collective-permute-start.2 = (f32[1,2,256,256]{3,2,1,0:T(8,128)}, f32[1,2,256,256]{3,2,1,0:T(8,128)}, u32[]{:S(2)}, u32[]{:S(2)}) collective-permute-start(f32[1,2,256,256]{3,2,1,0:T(8,128)} %get-tuple-element.2285), channel_id=1, source_target_pairs={{0,32},{32,64},{64,96},{1,33},{33,65},{65,97},{2,34},{34,66},{66,9... | collective-permute-start | bytes 1572872 | tf_op jit(solution)/shard_map/ppermute | solution.py:27
  144.1 15.7 %collective-permute-start.3 = (f32[1,2,256,256]{3,2,1,0:T(8,128)}, f32[1,2,256,256]{3,2,1,0:T(8,128)}, u32[]{:S(2)}, u32[]{:S(2)}) collective-permute-start(f32[1,2,256,256]{3,2,1,0:T(8,128)} %get-tuple-element.2287), channel_id=1, source_target_pairs={{0,32},{32,64},{64,96},{1,33},{33,65},{65,97},{2,34},{34,66},{66,9... | collective-permute-start | bytes 1572872 | tf_op jit(solution)/shard_map/ppermute | solution.py:27
  188.2 14.6 %collective-permute-start.4 = (f32[1,2,256,256]{3,2,1,0:T(8,128)}, f32[1,2,256,256]{3,2,1,0:T(8,128)}, u32[]{:S(2)}, u32[]{:S(2)}) collective-permute-start(f32[1,2,256,256]{3,2,1,0:T(8,128)} %get-tuple-element.2289), channel_id=1, source_target_pairs={{0,32},{32,64},{64,96},{1,33},{33,65},{65,97},{2,34},{34,66},{66,9... | collective-permute-start | bytes 1572872 | tf_op jit(solution)/shard_map/ppermute | solution.py:27
  231.1 13.9 %collective-permute-start.5 = (f32[1,2,256,256]{3,2,1,0:T(8,128)}, f32[1,2,256,256]{3,2,1,0:T(8,128)}, u32[]{:S(2)}, u32[]{:S(2)}) collective-permute-start(f32[1,2,256,256]{3,2,1,0:T(8,128)} %get-tuple-element.2291), channel_id=1, source_target_pairs={{0,32},{32,64},{64,96},{1,33},{33,65},{65,97},{2,34},{34,66},{66,9... | collective-permute-start | bytes 1572872 | tf_op jit(solution)/shard_map/ppermute | solution.py:27
  273.5 12.9 %collective-permute-start.6 = (f32[1,2,256,256]{3,2,1,0:T(8,128)}, f32[1,2,256,256]{3,2,1,0:T(8,128)S(1)}, u32[]{:S(2)}, u32[]{:S(2)}) collective-permute-start(f32[1,2,256,256]{3,2,1,0:T(8,128)} %get-tuple-element.2293), channel_id=1, source_target_pairs={{0,32},{32,64},{64,96},{1,33},{33,65},{65,97},{2,34},{34,66},{66,9... | collective-permute-start | bytes 1572872 | tf_op jit(solution)/shard_map/ppermute | solution.py:27
  288.6 12.1 %copy-start.6 = (f32[1,2,256,256]{3,2,1,0:T(8,128)}, f32[1,2,256,256]{3,2,1,0:T(8,128)S(1)}, u32[]{:S(2)}) copy-start(f32[1,2,256,256]{3,2,1,0:T(8,128)S(1)} %dynamic-slice_select_fusion.5) | copy-start | bytes 1572868 | tf_op jit(solution)/shard_map/cond
  305.9 9.0 copy-start.7
  314.9 12.6 %collective-permute-start.7 = (f32[1,2,256,256]{3,2,1,0:T(8,128)}, f32[1,2,256,256]{3,2,1,0:T(8,128)}, u32[]{:S(2)}, u32[]{:S(2)}) collective-permute-start(f32[1,2,256,256]{3,2,1,0:T(8,128)} %get-tuple-element.2295), channel_id=1, source_target_pairs={{0,32},{32,64},{64,96},{1,33},{33,65},{65,97},{2,34},{34,66},{66,9... | collective-permute-start | bytes 1572872 | tf_op jit(solution)/shard_map/ppermute | solution.py:27
  330.2 36.4 %collective-permute-start.8 = (f32[1,2,256,256]{3,2,1,0:T(8,128)}, f32[1,2,256,256]{3,2,1,0:T(8,128)}, u32[]{:S(2)}, u32[]{:S(2)}) collective-permute-start(f32[1,2,256,256]{3,2,1,0:T(8,128)} %get-tuple-element.2297), channel_id=1, source_target_pairs={{0,32},{32,64},{64,96},{1,33},{33,65},{65,97},{2,34},{34,66},{66,9... | collective-permute-start | bytes 1572872 | tf_op jit(solution)/shard_map/ppermute | solution.py:27
  368.5 11.4 %collective-permute-start.9 = (f32[1,2,256,256]{3,2,1,0:T(8,128)}, f32[1,2,256,256]{3,2,1,0:T(8,128)}, u32[]{:S(2)}, u32[]{:S(2)}) collective-permute-start(f32[1,2,256,256]{3,2,1,0:T(8,128)} %get-tuple-element.2299), channel_id=1, source_target_pairs={{0,32},{32,64},{64,96},{1,33},{33,65},{65,97},{2,34},{34,66},{66,9... | collective-permute-start | bytes 1572872 | tf_op jit(solution)/shard_map/ppermute | solution.py:27
  397.7 36.5 %collective-permute-start.10 = (f32[1,2,256,256]{3,2,1,0:T(8,128)}, f32[1,2,256,256]{3,2,1,0:T(8,128)}, u32[]{:S(2)}, u32[]{:S(2)}) collective-permute-start(f32[1,2,256,256]{3,2,1,0:T(8,128)} %get-tuple-element.2312), channel_id=1, source_target_pairs={{32,0},{64,32},{96,64},{33,1},{65,33},{97,65},{34,2},{66,34},{98,6... | collective-permute-start | bytes 1572872 | tf_op jit(solution)/shard_map/ppermute | solution.py:27
  436.1 11.9 %collective-permute-start.11 = (f32[1,2,256,256]{3,2,1,0:T(8,128)}, f32[1,2,256,256]{3,2,1,0:T(8,128)}, u32[]{:S(2)}, u32[]{:S(2)}) collective-permute-start(f32[1,2,256,256]{3,2,1,0:T(8,128)} %get-tuple-element.2315), channel_id=1, source_target_pairs={{32,0},{64,32},{96,64},{33,1},{65,33},{97,65},{34,2},{66,34},{98,6... | collective-permute-start | bytes 1572872 | tf_op jit(solution)/shard_map/ppermute | solution.py:27
  449.8 162.2 %collective-permute-start.12 = (f32[1,2,256,256]{3,2,1,0:T(8,128)}, f32[1,2,256,256]{3,2,1,0:T(8,128)}, u32[]{:S(2)}, u32[]{:S(2)}) collective-permute-start(f32[1,2,256,256]{3,2,1,0:T(8,128)} %get-tuple-element.2318), channel_id=1, source_target_pairs={{32,0},{64,32},{96,64},{33,1},{65,33},{97,65},{34,2},{66,34},{98,6... | collective-permute-start | bytes 1572872 | tf_op jit(solution)/shard_map/ppermute | solution.py:27
  651.3 19.3 %collective-permute-start.13 = (f32[1,2,256,256]{3,2,1,0:T(8,128)}, f32[1,2,256,256]{3,2,1,0:T(8,128)}, u32[]{:S(2)}, u32[]{:S(2)}) collective-permute-start(f32[1,2,256,256]{3,2,1,0:T(8,128)} %get-tuple-element.2321), channel_id=1, source_target_pairs={{32,0},{64,32},{96,64},{33,1},{65,33},{97,65},{34,2},{66,34},{98,6... | collective-permute-start | bytes 1572872 | tf_op jit(solution)/shard_map/ppermute | solution.py:27
  709.8 19.4 %collective-permute-start.14 = (f32[1,2,256,256]{3,2,1,0:T(8,128)}, f32[1,2,256,256]{3,2,1,0:T(8,128)}, u32[]{:S(2)}, u32[]{:S(2)}) collective-permute-start(f32[1,2,256,256]{3,2,1,0:T(8,128)} %get-tuple-element.2324), channel_id=1, source_target_pairs={{32,0},{64,32},{96,64},{33,1},{65,33},{97,65},{34,2},{66,34},{98,6... | collective-permute-start | bytes 1572872 | tf_op jit(solution)/shard_map/ppermute | solution.py:27
  768.5 20.2 %collective-permute-start.15 = (f32[1,2,256,256]{3,2,1,0:T(8,128)}, f32[1,2,256,256]{3,2,1,0:T(8,128)}, u32[]{:S(2)}, u32[]{:S(2)}) collective-permute-start(f32[1,2,256,256]{3,2,1,0:T(8,128)} %get-tuple-element.2327), channel_id=1, source_target_pairs={{32,0},{64,32},{96,64},{33,1},{65,33},{97,65},{34,2},{66,34},{98,6... | collective-permute-start | bytes 1572872 | tf_op jit(solution)/shard_map/ppermute | solution.py:27
  828.4 19.6 %collective-permute-start.16 = (f32[1,2,256,256]{3,2,1,0:T(8,128)}, f32[1,2,256,256]{3,2,1,0:T(8,128)}, u32[]{:S(2)}, u32[]{:S(2)}) collective-permute-start(f32[1,2,256,256]{3,2,1,0:T(8,128)} %get-tuple-element.2330), channel_id=1, source_target_pairs={{32,0},{64,32},{96,64},{33,1},{65,33},{97,65},{34,2},{66,34},{98,6... | collective-permute-start | bytes 1572872 | tf_op jit(solution)/shard_map/ppermute | solution.py:27
  887.8 25.0 %collective-permute-start.17 = (f32[1,2,256,256]{3,2,1,0:T(8,128)}, f32[1,2,256,256]{3,2,1,0:T(8,128)}, u32[]{:S(2)}, u32[]{:S(2)}) collective-permute-start(f32[1,2,256,256]{3,2,1,0:T(8,128)} %get-tuple-element.2333), channel_id=1, source_target_pairs={{32,0},{64,32},{96,64},{33,1},{65,33},{97,65},{34,2},{66,34},{98,6... | collective-permute-start | bytes 1572872 | tf_op jit(solution)/shard_map/ppermute | solution.py:27
  912.8 31.6 %copy-start.18 = (pred[512]{0:T(512)(128)(4,1)S(1)}, pred[512]{0:T(512)(128)(4,1)}, u32[]{:S(2)}) copy-start(pred[512]{0:T(512)(128)(4,1)} %copy-done.17) | copy-start | bytes 1540
  961.3 50.1 %collective-permute-start.18 = (f32[1,2,4096,128]{3,2,1,0:T(8,128)}, f32[1,2,4096,128]{3,2,1,0:T(8,128)}, u32[]{:S(2)}, u32[]{:S(2)}) collective-permute-start(f32[1,2,4096,128]{3,2,1,0:T(8,128)} %get-tuple-element.2937), channel_id=1, source_target_pairs={{0,1},{1,2},{2,3},{3,4},{4,5},{5,6},{6,7},{7,8},{8,9},{9,10},{10,1... | collective-permute-start | bytes 12582920 | tf_op jit(solution)/shard_map/ppermute | solution.py:18
  963.2 52.2 %collective-permute-start.19 = (f32[1,2,4096,128]{3,2,1,0:T(8,128)}, f32[1,2,4096,128]{3,2,1,0:T(8,128)}, u32[]{:S(2)}, u32[]{:S(2)}) collective-permute-start(f32[1,2,4096,128]{3,2,1,0:T(8,128)} %get-tuple-element.2936), channel_id=1, source_target_pairs={{1,0},{2,1},{3,2},{4,3},{5,4},{6,5},{7,6},{8,7},{9,8},{10,9},{11,1... | collective-permute-start | bytes 12582920 | tf_op jit(solution)/shard_map/ppermute | solution.py:19
  975.9 35.5 %slice-start = ((f32[1,2,4096,512]{3,2,1,0:T(8,128)}), f32[1,2,4096,256]{3,2,1,0:T(8,128)S(1)}, s32[]{:S(2)}) async-start(f32[1,2,4096,512]{3,2,1,0:T(8,128)} %copy-done), calls=%async_computation | async-start | bytes 16777216 | tf_op jit(solution)/shard_map/slice | solution.py:211
  (6 other events, 23.0 us)
where the time goes:
time: 1030 us; the launch traced here: 1020 us
  waiting for transfers between devices  383 us (37%)
  local copies, waits for them, and re-layouts  234 us (23%)
  matrix products  124 us (12%)
  loops' own time  108 us (10%)
  other arithmetic  85.8 us (8%)
  starting transfers between devices  85.3 us (8%)
    ppermute x16, waiting for transfers between devices, from_behind(): return lax.ppermute(value, axis, pairs)  312 us
    ppermute x16, starting transfers between devices, from_behind(): return lax.ppermute(value, axis, pairs)  73.3 us
    dot_general x24, matrix products, transform(): jnp.einsum('ab,pbc->pac', matrix, stacked, precision=lax.Precision.HIGHEST)  63.2 us
    dot_general x24, matrix products, transform(): jnp.einsum('psik,rjsk->prij', halfway, quadrant, precision=lax.Precision....  60.3 us
    another operation x53, local copies, waits for them, and re-layouts  46.4 us
    another operation x9, loops' own time, on_device(): lax.cond(is_valid, run_adjoint, skip_adjoint, grad_ext, fields, inputs, s...  45.9 us
    scatter x6, local copies, waits for them, and re-layouts, run_adjoint(): grad_ext = grad_ext.at[slice_at].set(grad_plane)  39.8 us
    another operation x9, loops' own time, on_device(): lax.cond(is_valid & (section_at == last_section), far_adjoint, skip_far,...  38.4 us
  transfers between devices with their start and end apart: 20, of which 16 were waited for; matrix products, arithmetic and copies ran while one was open for 5% of the time, Pallas kernels for 0%

commit v1 on v0

v1 whole, which is shorter than its diff:
```python
import math

import jax
import jax.numpy as jnp
import ml_dtypes
import numpy as np
from jax import lax
from jax.experimental import pallas as pl
from jax.experimental.pallas import tpu as pltpu
from jax.sharding import PartitionSpec as P

RIM = 128
HALF = 128
W = 256
F32 = jnp.float32
BF16 = jnp.bfloat16
VMEM_BYTES = 56 * 1024 * 1024

ANY_SPEC = pl.BlockSpec(memory_space=pl.ANY)
SMEM_SPEC = pl.BlockSpec(memory_space=pltpu.SMEM)
VMEM_SPEC = pl.BlockSpec(memory_space=pltpu.VMEM)


def split_table(table):
    high = table.astype(ml_dtypes.bfloat16)
    low = (table - high.astype(np.float64)).astype(ml_dtypes.bfloat16)
    return high, low


def make_tables():
    freq = np.arange(HALF)[:, None]
    place = np.arange(HALF)[None, :]
    out = []
    for odd in (0, 1):
        angle = 2.0 * math.pi * (((2 * freq + odd) * place) % W) / W
        re, im = np.cos(angle) / math.sqrt(W), -np.sin(angle) / math.sqrt(W)
        real = np.block([[re, -im], [im, re]])
        out += [*split_table(real), *split_table(real.T)]
    return np.stack(out)


def make_order():
    order = np.concatenate([np.arange(0, W, 2), np.arange(1, W, 2)])
    hot = np.zeros((W, W), np.float32)
    hot[np.arange(W), order] = 1.0
    return hot


TABLES = make_tables()
ORDER = make_order()


def dot(first, second):
    return jnp.dot(first, second, preferred_element_type=F32)


def split(value):
    high = value.astype(BF16)
    return high, (value - high.astype(F32)).astype(BF16)


def table_left(tab, at, value):
    high, low = split(value)
    return dot(tab[at], high) + dot(tab[at], low) + dot(tab[at + 1], high)


def table_right(value, tab, at):
    high, low = split(value)
    return dot(high, tab[at]) + dot(low, tab[at]) + dot(high, tab[at + 1])


def to_spectrum(re, im, tab):
    h = HALF
    total = jnp.concatenate([re[:h] + re[h:], im[:h] + im[h:]], 0)
    diff = jnp.concatenate([re[:h] - re[h:], im[:h] - im[h:]], 0)
    even = table_left(tab, 0, total)
    odd = table_left(tab, 4, diff)
    yr = jnp.concatenate([even[:h], odd[:h]], 0)
    yi = jnp.concatenate([even[h:], odd[h:]], 0)
    total = jnp.concatenate([yr[:, :h] + yr[:, h:], yi[:, :h] + yi[:, h:]], 1)
    diff = jnp.concatenate([yr[:, :h] - yr[:, h:], yi[:, :h] - yi[:, h:]], 1)
    return table_right(total, tab, 2), table_right(diff, tab, 6)


def from_spectrum(even, odd, tab):
    h = HALF
    a = table_right(even, tab, 0)
    b = table_right(odd, tab, 4)
    yr = jnp.concatenate([a[:, :h] + b[:, :h], a[:, :h] - b[:, :h]], 1)
    yi = jnp.concatenate([a[:, h:] + b[:, h:], a[:, h:] - b[:, h:]], 1)
    p = table_left(tab, 2, jnp.concatenate([yr[:h], yi[:h]], 0))
    q = table_left(tab, 6, jnp.concatenate([yr[h:], yi[h:]], 0))
    re = jnp.concatenate([p[:h] + q[:h], p[:h] - q[:h]], 0)
    im = jnp.concatenate([p[h:] + q[h:], p[h:] - q[h:]], 0)
    return re, im


def turn(spectrum, cosine, sine):
    h = HALF
    re, im = spectrum[:, :h], spectrum[:, h:]
    return jnp.concatenate([re * cosine - im * sine, re * sine + im * cosine], 1)


def propagate(re, im, kern, tab, sign):
    h = HALF
    even, odd = to_spectrum(re, im, tab)
    cosine, sine = kern[0], sign * kern[1]
    even = turn(even, cosine[:, :h], sine[:, :h])
    odd = turn(odd, cosine[:, h:], sine[:, h:])
    return from_spectrum(even, odd, tab)


def row_base(row):
    base = pl.multiple_of((row // 8) * 8, 8)
    extra = pl.multiple_of(jnp.minimum(base + W, 4096 - 8), 8)
    return base, extra, row - base


def rows_below(delta, shape):
    return lax.broadcasted_iota(jnp.int32, shape, len(shape) - 2) < delta


def cut_rims(cap):
    def kernel(pos_left, pos_right, image, to_left, to_right, extra, sems):
        copies = []
        for s in range(cap):
            for side, (pos, out, first) in enumerate(
                ((pos_left, to_left, 0), (pos_right, to_right, HALF))
            ):
                base, more, _ = row_base(pos[s, 0])
                cols = pl.ds(first, HALF)
                copies.append((
                    pltpu.make_async_copy(
                        image.at[:, pl.ds(base, W), cols], out.at[s], sems.at[2 * s + side, 0]
                    ),
                    pltpu.make_async_copy(
                        image.at[:, pl.ds(more, 8), cols],
                        extra.at[2 * s + side],
                        sems.at[2 * s + side, 1],
                    ),
                ))
        for pair in copies:
            for copy in pair:
                copy.start()
        for s in range(cap):
            for side, (pos, out) in enumerate(((pos_left, to_left), (pos_right, to_right))):
                for copy in copies[2 * s + side]:
                    copy.wait()
                delta = pos[s, 0] % 8
                mask = rows_below(delta, (2, 8, HALF))
                out[s, :, 0:8, :] = jnp.where(mask, extra[2 * s + side], out[s, :, 0:8, :])

    strips = jax.ShapeDtypeStruct((cap, 2, W, HALF), F32)
    return pl.pallas_call(
        kernel,
        out_shape=(strips, strips),
        in_specs=[SMEM_SPEC, SMEM_SPEC, ANY_SPEC],
        out_specs=(VMEM_SPEC, VMEM_SPEC),
        scratch_shapes=[
            pltpu.VMEM((2 * cap, 2, 8, HALF), F32),
            pltpu.SemaphoreType.DMA((2 * cap, 2)),
        ],
        compiler_params=pltpu.CompilerParams(vmem_limit_bytes=VMEM_BYTES),
        name="cut_rims",
    )


def slot_of(owner, second):
    return 4 + owner // 2 if second else owner


def make_windows():
    def kernel(meta, pos, image, from_left, from_right, *rest):
        outs, (extra, sems, rim_buf) = rest[:8], rest[8:]
        group, tile, parity = meta[0], meta[1], meta[2]
        wide_left, wide_right, tiles = meta[4], meta[5], meta[6]

        def job(at):
            second, k = divmod(at, 4)
            owner = (group + k) % 4
            valid = (owner % 2 == parity) if second else (owner >= 0)
            return slot_of(owner, second), valid

        def transfers(at, s):
            base, more, _ = row_base(pos[s, 0])
            return (
                pltpu.make_async_copy(image.at[:, pl.ds(base, W), :], outs[at], sems.at[at, 0]),
                pltpu.make_async_copy(
                    image.at[:, pl.ds(more, 8), :], extra.at[at], sems.at[at, 1]
                ),
                pltpu.make_async_copy(from_left.at[s], rim_buf.at[at, 0], sems.at[at, 2]),
                pltpu.make_async_copy(from_right.at[s], rim_buf.at[at, 1], sems.at[at, 3]),
            )

        for at in range(8):
            s, valid = job(at)

            @pl.when(valid)
            def _(at=at, s=s):
                for copy in transfers(at, s):
                    copy.start()

        for at in range(8):
            s, valid = job(at)

            @pl.when(valid)
            def _(at=at, s=s):
                for copy in transfers(at, s):
                    copy.wait()
                delta = pos[s, 0] % 8
                edge = pos[s, 1] - RIM
                out = outs[at]
                mask = rows_below(delta, (2, 8, W))
                out[:, 0:8, :] = jnp.where(mask, extra[at], out[:, 0:8, :])
                lane = lax.broadcasted_iota(jnp.int32, (W, HALF), 1)

                @pl.when(edge > 0)
                def _():
                    rim = lane < edge
                    kept = (lane < wide_right) & (tile < tiles - 1)
                    for part in range(2):
                        value = jnp.where(kept, rim_buf[at, 1, part], 1.0 - part)
                        out[part, :, :HALF] = jnp.where(rim, value, out[part, :, :HALF])

                @pl.when(edge < 0)
                def _():
                    rim = lane + HALF >= W + edge
                    kept = (lane + HALF >= W - wide_left) & (tile > 0)
                    for part in range(2):
                        value = jnp.where(kept, rim_buf[at, 0, part], 1.0 - part)
                        out[part, :, HALF:] = jnp.where(rim, value, out[part, :, HALF:])

    window = jax.ShapeDtypeStruct((2, W, W), F32)
    return pl.pallas_call(
        kernel,
        out_shape=(window,) * 8,
        in_specs=[SMEM_SPEC, SMEM_SPEC, ANY_SPEC, ANY_SPEC, ANY_SPEC],
        out_specs=(VMEM_SPEC,) * 8,
        scratch_shapes=[
            pltpu.VMEM((8, 2, 8, W), F32),
            pltpu.SemaphoreType.DMA((8, 4)),
            pltpu.VMEM((8, 2, 2, W, HALF), F32),
        ],
        compiler_params=pltpu.CompilerParams(vmem_limit_bytes=VMEM_BYTES),
        name="make_windows",
    )


def forward_slot(second):
    def kernel(meta, pos, probe, measured, kern, tab, order, order_t, *rest):
        wins, inputs, back = rest[:4], rest[4:8], rest[8]
        win_buf, in_buf, seen, sems = rest[9:]
        group, parity, live = meta[0], meta[2], meta[3]
        s = slot_of(group, second)
        valid = (group % 2 == parity) if second else (group >= 0)

        @pl.when(valid)
        def _():
            loads = []
            for k in range(4):
                n = (group - k) % 4
                loads.append(pltpu.make_async_copy(wins[k], win_buf.at[n], sems.at[k]))
            seeing = pltpu.make_async_copy(measured.at[s], seen, sems.at[4])
            for copy in loads:
                copy.start()
            seeing.start()
            down = pos[s, 0] % 8
            across = (pos[s, 1] - RIM) % W
            scale = jnp.where(s < live, 1.0, 0.0)
            for part in range(2):
                rolled = pltpu.roll(probe[part], across, 1)
                in_buf[0, part] = pltpu.roll(rolled, down, 0) * scale
            for copy in loads:
                copy.wait()

            def step(n, carry):
                re, im = in_buf[n, 0], in_buf[n, 1]
                wr, wi = win_buf[n, 0], win_buf[n, 1]
                re, im = wr * re - wi * im, wr * im + wi * re
                re, im = propagate(re, im, kern, tab, 1.0)
                in_buf[n + 1, 0] = re
                in_buf[n + 1, 1] = im
                return carry

            lax.fori_loop(0, 4, step, 0)
            stores = []
            for k in range(4):
                n = (group + k) % 4
                stores.append(pltpu.make_async_copy(in_buf.at[n], inputs[k], sems.at[5 + k]))
            for copy in stores:
                copy.start()
            seeing.wait()
            half_seen = dot(order[...], seen[...]).astype(BF16)
            target = dot(half_seen, order_t[...])
            spectra = to_spectrum(in_buf[4, 0], in_buf[4, 1], tab)
            chis = []
            for odd in range(2):
                re, im = spectra[odd][:, :HALF], spectra[odd][:, HALF:]
                rest_of = re * re + im * im - target[:, odd * HALF : (odd + 1) * HALF]
                chis.append(jnp.concatenate([re * rest_of, im * rest_of], 1))
            re, im = from_spectrum(chis[0], chis[1], tab)
            back[0] = re
            back[1] = im
            for copy in stores:
                copy.wait()

    field = jax.ShapeDtypeStruct((2, W, W), F32)
    return pl.pallas_call(
        kernel,
        out_shape=(field,) * 5,
        in_specs=[SMEM_SPEC, SMEM_SPEC, VMEM_SPEC, ANY_SPEC]
        + [VMEM_SPEC] * 4
        + [ANY_SPEC] * 4,
        out_specs=(ANY_SPEC,) * 4 + (VMEM_SPEC,),
        scratch_shapes=[
            pltpu.VMEM((4, 2, W, W), F32),
            pltpu.VMEM((5, 2, W, W), F32),
            pltpu.VMEM((W, W), BF16),
            pltpu.SemaphoreType.DMA((9,)),
        ],
        compiler_params=pltpu.CompilerParams(vmem_limit_bytes=VMEM_BYTES),
        name="forward_second" if second else "forward_first",
    )


def backward_slot(second):
    def kernel(meta, back, kern, tab, *rest):
        wins, turned = rest[:4], rest[4:8]
        win_buf, turned_buf, back_buf, sems = rest[8:]
        group, parity = meta[0], meta[2]
        valid = (group % 2 == parity) if second else (group >= 0)

        @pl.when(valid)
        def _():
            loads = []
            for k in range(4):
                n = (group - k) % 4
                loads.append(pltpu.make_async_copy(wins[k], win_buf.at[n], sems.at[k]))
            for copy in loads:
                copy.start()
            back_buf[...] = back[...]
            for copy in loads:
                copy.wait()

            def step(at, carry):
                n = 3 - at
                re, im = propagate(back_buf[0], back_buf[1], kern, tab, -1.0)
                turned_buf[n, 0] = re
                turned_buf[n, 1] = im
                wr, wi = win_buf[n, 0], win_buf[n, 1]
                back_buf[0] = wr * re + wi * im
                back_buf[1] = wr * im - wi * re
                return carry

            lax.fori_loop(0, 4, step, 0)
            stores = []
            for k in range(4):
                n = (group + k) % 4
                stores.append(pltpu.make_async_copy(turned_buf.at[n], turned[k], sems.at[4 + k]))
            for copy in stores:
                copy.start()
            for copy in stores:
                copy.wait()

    field = jax.ShapeDtypeStruct((2, W, W), F32)
    return pl.pallas_call(
        kernel,
        out_shape=(field,) * 4,
        in_specs=[SMEM_SPEC] + [VMEM_SPEC] * 3 + [ANY_SPEC] * 4,
        out_specs=(ANY_SPEC,) * 4,
        scratch_shapes=[
            pltpu.VMEM((4, 2, W, W), F32),
            pltpu.VMEM((4, 2, W, W), F32),
            pltpu.VMEM((2, W, W), F32),
            pltpu.SemaphoreType.DMA((8,)),
        ],
        compiler_params=pltpu.CompilerParams(vmem_limit_bytes=VMEM_BYTES),
        name="backward_second" if second else "backward_first",
    )


def slice_terms(second, cap):
    count = 2 if second else 4
    first = 4 if second else 0

    def kernel(meta, pos, probe, *rest):
        if second:
            rest = rest[1:]
        turned, inputs, wins = rest[:4], rest[4:8], rest[8:12]
        adjoint, own, to_left, to_right = rest[12:16]
        t_buf, i_buf, w_buf, a_buf, sems = rest[16:]
        group, tile, parity, live = meta[0], meta[1], meta[2], meta[3]
        wide_left, wide_right, tiles = meta[4], meta[5], meta[6]

        def job(j):
            owner = (group - j) % 4
            valid = (owner % 2 == parity) if second else (owner >= 0)
            return slot_of(owner, second), valid

        def loads(j):
            return (
                pltpu.make_async_copy(turned[j], t_buf.at[j], sems.at[j, 0]),
                pltpu.make_async_copy(inputs[j], i_buf.at[j], sems.at[j, 1]),
                pltpu.make_async_copy(wins[(4 - j) % 4], w_buf.at[j], sems.at[j, 2]),
            )

        def store(j, s):
            return pltpu.make_async_copy(a_buf.at[j], adjoint.at[s], sems.at[j, 3])

        for j in range(4):
            s, valid = job(j)

            @pl.when(valid)
            def _(j=j):
                for copy in loads(j):
                    copy.start()

        for j in range(4):
            s, valid = job(j)

            @pl.when(valid)
            def _(j=j, s=s):
                for copy in loads(j):
                    copy.wait()
                down = pos[s, 0] % 8
                edge = pos[s, 1] - RIM
                across = edge % W

                @pl.when(group == 0)
                def _():
                    scale = jnp.where(s < live, 1.0, 0.0)
                    for part in range(2):
                        rolled = pltpu.roll(probe[part], across, 1)
                        i_buf[j, part] = pltpu.roll(rolled, down, 0) * scale

                re, im = t_buf[j, 0], t_buf[j, 1]
                wr, wi = w_buf[j, 0], w_buf[j, 1]
                for part, value in enumerate((wr * re + wi * im, wr * im - wi * re)):
                    rolled = pltpu.roll(value, (W - across) % W, 1)
                    a_buf[j, part] = pltpu.roll(rolled, (W - down) % W, 0)
                store(j, s).start()
                lane = lax.broadcasted_iota(jnp.int32, (W, W), 1)
                rim_left = lane >= W + edge
                rim_right = lane < edge
                half = lax.broadcasted_iota(jnp.int32, (W, HALF), 1)
                sent_left = (half + HALF >= W + edge) & (half + HALF >= W - wide_left) & (tile > 0)
                sent_right = (half < edge) & (half < wide_right) & (tile < tiles - 1)
                ir, ii = i_buf[j, 0], i_buf[j, 1]
                at = s - first
                for part, value in enumerate((ir * re + ii * im, ir * im - ii * re)):
                    own[at, part] = jnp.where(rim_left | rim_right, 0.0, value)
                    to_left[at, part] = jnp.where(sent_left, value[:, HALF:], 0.0)
                    to_right[at, part] = jnp.where(sent_right, value[:, :HALF], 0.0)

        for j in range(4):
            s, valid = job(j)

            @pl.when(valid)
            def _(j=j, s=s):
                store(j, s).wait()

    waves = jax.ShapeDtypeStruct((cap, 2, W, W), F32)
    own = jax.ShapeDtypeStruct((count, 2, W, W), F32)
    strips = jax.ShapeDtypeStruct((count, 2, W, HALF), F32)
    extra = [ANY_SPEC] if second else []
    return pl.pallas_call(
        kernel,
        out_shape=(waves, own, strips, strips),
        in_specs=[SMEM_SPEC, SMEM_SPEC, VMEM_SPEC] + extra + [ANY_SPEC] * 12,
        out_specs=(ANY_SPEC, VMEM_SPEC, VMEM_SPEC, VMEM_SPEC),
        scratch_shapes=[pltpu.VMEM((4, 2, W, W), F32)] * 4 + [pltpu.SemaphoreType.DMA((4, 4))],
        input_output_aliases={3: 0} if second else {},
        compiler_params=pltpu.CompilerParams(vmem_limit_bytes=VMEM_BYTES),
        name="terms_second" if second else "terms_first",
    )


def add_terms(cap, rows):
    def kernel(pos, pos_left, pos_right, own1, own2, left1, left2, right1, right2, out):
        out[...] = jnp.zeros_like(out)

        def add(row, value, cols):
            base, more, delta = row_base(row)
            width = value.shape[-1]
            below = rows_below(delta, (W, width))
            few = rows_below(delta, (8, width))
            for part in range(2):
                out[part, pl.ds(base, W), cols] += jnp.where(below, 0.0, value[part])
                out[part, pl.ds(more, 8), cols] += jnp.where(few, value[part, :8], 0.0)

        for s in range(cap):
            pick = (lambda one, two: one[s] if s < 4 else two[s - 4])
            add(pos[s, 0], pick(own1, own2), slice(0, W))
            add(pos_left[s, 0], pick(left1, left2), slice(0, HALF))
            add(pos_right[s, 0], pick(right1, right2), slice(HALF, W))

    return pl.pallas_call(
        kernel,
        out_shape=jax.ShapeDtypeStruct((2, rows, W), F32),
        in_specs=[SMEM_SPEC] * 3 + [VMEM_SPEC] * 6,
        out_specs=VMEM_SPEC,
        compiler_params=pltpu.CompilerParams(vmem_limit_bytes=VMEM_BYTES),
        name="add_terms",
    )


def on_device(probe_wave, transmission, kernel_phase, measured, counts, positions, widths):
    groups, tiles = lax.axis_size("cuts"), lax.axis_size("tile")
    group, tile = lax.axis_index("cuts"), lax.axis_index("tile")
    cap = positions.shape[1]
    rows = transmission.shape[2]
    image, pos = transmission[0], positions[0]
    up = [(i, i + 1) for i in range(tiles - 1)]
    down = [(i + 1, i) for i in range(tiles - 1)]

    def to_up(value):
        return lax.ppermute(value, "tile", up)

    def to_down(value):
        return lax.ppermute(value, "tile", down)

    def shift(value, by, keep):
        pairs = [
            (g * tiles + t, (g + by) % groups * tiles + t)
            for g in range(groups)
            for t in range(tiles)
            if keep(g, (g + by) % groups, t % 2)
        ]
        return lax.ppermute(value, ("cuts", "tile"), pairs)

    meta = jnp.stack(
        [group, tile, tile % 2, counts[0], widths[0, 0], widths[0, 1], jnp.int32(tiles)]
    ).astype(jnp.int32)
    pos_left, pos_right = to_up(pos), to_down(pos)
    rims_left, rims_right = cut_rims(cap)(pos_left, pos_right, image)
    from_right, from_left = to_down(rims_left), to_up(rims_right)
    wins = make_windows()(meta, pos, image, from_left, from_right)

    order = jnp.asarray(ORDER)
    exact = lax.Precision.HIGHEST
    phase = jnp.dot(jnp.dot(order, kernel_phase, precision=exact), order.T, precision=exact)
    kern = jnp.stack([jnp.cos(phase), jnp.sin(phase)])
    tab = jnp.asarray(TABLES)
    hot, hot_t = order.astype(BF16), order.T.astype(BF16)

    def shifted(values, keep):
        return [values[0]] + [shift(values[k], k, keep) for k in range(1, 4)]

    all_pairs = lambda src, dst, parity: True
    to_owner = lambda src, dst, parity: dst % 2 == parity
    inner = lambda src, dst, parity: dst != 0
    inner_owned = lambda src, dst, parity: dst != 0 and src % 2 == parity
    owned = lambda src, dst, parity: src % 2 == parity

    got1 = shifted(wins[:4], all_pairs)
    got2 = shifted(wins[4:], to_owner)
    *in1, back1 = forward_slot(0)(meta, pos, probe_wave, measured[0], kern, tab, hot, hot_t, *got1)
    in1 = shifted(in1, inner)
    turned1 = shifted(backward_slot(0)(meta, back1, kern, tab, *got1), all_pairs)
    *in2, back2 = forward_slot(1)(meta, pos, probe_wave, measured[0], kern, tab, hot, hot_t, *got2)
    in2 = shifted(in2, inner_owned)
    turned2 = shifted(backward_slot(1)(meta, back2, kern, tab, *got2), owned)

    adjoint, own1, left1, right1 = slice_terms(0, cap)(
        meta, pos, probe_wave, *turned1, *in1, *wins[:4]
    )
    right1, left1 = to_down(left1), to_up(right1)
    adjoint, own2, left2, right2 = slice_terms(1, cap)(
        meta, pos, probe_wave, adjoint, *turned2, *in2, *wins[4:]
    )
    right2, left2 = to_down(left2), to_up(right2)
    grad = add_terms(cap, rows)(
        pos, pos_left, pos_right, own1, own2, left1, left2, right1, right2
    )
    return adjoint[None, None], grad[None]


def solution(mesh):
    return jax.shard_map(
        on_device,
        mesh=mesh,
        in_specs=(
            P(),
            P("cuts", None, None, "tile"),
            P(),
            P("tile", None, None, None),
            P("tile"),
            P("tile", None, None),
            P("tile", None),
        ),
        out_specs=(P("cuts", "tile", None, None, None, None), P("cuts", None, None, "tile")),
        check_vma=False,
    )
```

time: 1030 us -> 212 us (0.21)
  the two profiles are of different devices: /device:TPU:30 before, /device:TPU:57 now
where the time goes in v1:
time: 212 us; the launch traced here: 210 us
  Pallas kernels  75 us (35%)
  starting transfers between devices  66.5 us (31%)
  waiting for transfers between devices  55.4 us (26%)
  local copies, waits for them, and re-layouts  8.64 us (4%)
    ppermute x18, starting transfers between devices, shift(): return lax.ppermute(value, ('cuts', 'tile'), pairs)  45.4 us
    ppermute x18, waiting for transfers between devices, shift(): return lax.ppermute(value, ('cuts', 'tile'), pairs)  20.8 us
    ppermute x4, waiting for transfers between devices, to_down(): return lax.ppermute(value, 'tile', down)  17.9 us
    ppermute x4, waiting for transfers between devices, to_up(): return lax.ppermute(value, 'tile', up)  16.7 us
    ppermute x4, starting transfers between devices, to_up(): return lax.ppermute(value, 'tile', up)  12.5 us
    pallas_call x1, Pallas kernels, on_device(): forward_slot(0)  11.4 us
    pallas_call x1, Pallas kernels, on_device(): forward_slot(1)  11.4 us
    pallas_call x1, Pallas kernels, on_device(): turned2 = shifted(backward_slot(1)(meta, back2, kern, tab, *got2), owned)  10.5 us
  transfers between devices with their start and end apart: 26, of which 7 were waited for; matrix products, arithmetic and copies ran while one was open for 3% of the time, Pallas kernels for 27%

profile of v1, /device:TPU:57, one launch (start us, length us, event | category | flops | bytes accessed | tf_op | source)
XLA Modules:
  0.0 210.5 jit_solution(12858276093941235770)
XLA Ops:
  1.5 3.3 %collective-permute-start = (s32[6,2]{1,0:T(8,128)S(1)}, s32[6,2]{1,0:T(8,128)S(1)}, u32[]{:S(2)}, u32[]{:S(2)}) collective-permute-start(s32[6,2]{1,0:T(8,128)S(1)} %copy.18.pos), channel_id=1, source_target_pairs={{0,1},{1,2},{2,3},{3,4},{4,5},{5,6},{6,7},{7,8},{8,9},{9,10},{10,1... | collective-permute-start | bytes 152 | tf_op jit(solution)/shard_map/ppermute | solution.py:517
  4.8 1.9 collective-permute-start.1
  6.7 5.1 %collective-permute-done.1.pos_right = s32[6,2]{1,0:T(8,128)S(1)} collective-permute-done((s32[6,2]{1,0:T(8,128)S(1)}, s32[6,2]{1,0:T(8,128)S(1)}, u32[]{:S(2)}, u32[]{:S(2)}) %collective-permute-start.1) | collective-permute-done | bytes 80 | tf_op jit(solution)/shard_map/ppermute | solution.py:520
  12.4 4.8 %cut_rims.1 = (f32[6,2,256,128]{3,2,1,0:T(8,128)}, f32[6,2,256,128]{3,2,1,0:T(8,128)}) custom-call(s32[6,2]{1,0:T(8,128)} %copy-done.28, s32[6,2]{1,0:T(8,128)} %copy-done.29, f32[2,4096,256]{2,1,0:T(8,128)} %bitcast.18), custom_call_target="tpu_custom_call" | custom-call | tf_op jit(solution)/shard_map/cut_rims/pallas_call | solution.py:535
  17.2 1.9 collective-permute-start.2
  19.2 2.4 %collective-permute-start.3 = (f32[6,2,256,128]{3,2,1,0:T(8,128)}, f32[6,2,256,128]{3,2,1,0:T(8,128)S(1)}, u32[]{:S(2)}, u32[]{:S(2)}) collective-permute-start(f32[6,2,256,128]{3,2,1,0:T(8,128)} %get-tuple-element.39), channel_id=1, source_target_pairs={{1,0},{2,1},{3,2},{4,3},{5,4},{6,5},{7,6},{8,7},{9,8},{10,9},{11,1... | collective-permute-start | bytes 4718600 | tf_op jit(solution)/shard_map/ppermute | solution.py:520
  24.6 12.2 %collective-permute-done.2.from_left = f32[6,2,256,128]{3,2,1,0:T(8,128)S(1)} collective-permute-done((f32[6,2,256,128]{3,2,1,0:T(8,128)}, f32[6,2,256,128]{3,2,1,0:T(8,128)S(1)}, u32[]{:S(2)}, u32[]{:S(2)}) %collective-permute-start.2) | collective-permute-done | bytes 1572896 | tf_op jit(solution)/shard_map/ppermute | solution.py:517
  36.9 6.4 %collective-permute-done.3.from_right = f32[6,2,256,128]{3,2,1,0:T(8,128)S(1)} collective-permute-done((f32[6,2,256,128]{3,2,1,0:T(8,128)}, f32[6,2,256,128]{3,2,1,0:T(8,128)S(1)}, u32[]{:S(2)}, u32[]{:S(2)}) %collective-permute-start.3) | collective-permute-done | bytes 1572896 | tf_op jit(solution)/shard_map/ppermute | solution.py:520
  44.4 5.9 %make_windows.1 = (f32[2,256,256]{2,1,0:T(8,128)}, f32[2,256,256]{2,1,0:T(8,128)}, f32[2,256,256]{2,1,0:T(8,128)}, f32[2,256,256]{2,1,0:T(8,128)}, f32[2,256,256...) custom-call(s32[7]{0:T(128)} %stack.24.meta, s32[6,2]{1,0:T(8,128)} %copy-done.27, ...), custom_call_target="tpu_custom_call" | custom-call | tf_op jit(solution)/shard_map/make_windows/pallas_call | solution.py:537
  53.2 2.0 collective-permute-start.6
  56.4 1.9 collective-permute-start.14
  61.3 19.7 %collective-permute-done.4.rest_1_ = f32[2,256,256]{2,1,0:T(8,128)S(1)} collective-permute-done((f32[2,256,256]{2,1,0:T(8,128)}, f32[2,256,256]{2,1,0:T(8,128)S(1)}, u32[]{:S(2)}, u32[]{:S(2)}) %collective-permute-start.4) | collective-permute-done | bytes 524320 | tf_op jit(solution)/shard_map/ppermute | solution.py:529
  83.3 11.4 %forward_first.1 = (f32[2,256,256]{2,1,0:T(8,128)}, f32[2,256,256]{2,1,0:T(8,128)}, f32[2,256,256]{2,1,0:T(8,128)}, f32[2,256,256]{2,1,0:T(8,128)}, f32[2,256,256]{2,1,0:T(8,128)}) custom-call(s32[7]{0:T(128)} %stack.24.meta, s32[6,2]{1,0:T(8,128)} %copy-done.27, f32[2,256,256]{2,1,0:T(8,128)} %probe.7, bf16[6,256,256]{2,1,0:T(8,128)(2,1)} %bitcast.21, ...), custom_call_target="tpu_custom_call" | custom-call | tf_op jit(solution)/shard_map/forward_first/pallas_call | solution.py:557
  94.8 10.3 %backward_first.1 = (f32[2,256,256]{2,1,0:T(8,128)}, f32[2,256,256]{2,1,0:T(8,128)}, f32[2,256,256]{2,1,0:T(8,128)}, f32[2,256,256]{2,1,0:T(8,128)}) custom-call(s32[7]{0:T(128)} %stack.24.meta, f32[2,256,256]{2,1,0:T(8,128)} %get-tuple-element.44.back, f32[2,256,256]{2,1,0:T(8,128)} %pad_maximum_fusion.kern, bf16[8,256,256]{2,1,0:T(8,128)(2,1)} %constant.29.clone.tab, ...), custom_call_target="tpu_custom_call" | custom-call | tf_op jit(solution)/shard_map/backward_first/pallas_call | solution.py:559
  105.1 2.2 %collective-permute-start.7 = (f32[2,256,256]{2,1,0:T(8,128)}, f32[2,256,256]{2,1,0:T(8,128)S(1)}, u32[]{:S(2)}, u32[]{:S(2)}) collective-permute-start(f32[2,256,256]{2,1,0:T(8,128)} %get-tuple-element.46), channel_id=1, source_target_pairs={{0,32},{1,33},{2,34},{3,35},{4,36},{5,37},{6,38},{7,39},{8,40},{9,... | collective-permute-start | bytes 1572872 | tf_op jit(solution)/shard_map/ppermute | solution.py:529
  109.2 3.0 %collective-permute-start.10 = (f32[2,256,256]{2,1,0:T(8,128)}, f32[2,256,256]{2,1,0:T(8,128)S(1)}, u32[]{:S(2)}, u32[]{:S(2)}) collective-permute-start(f32[2,256,256]{2,1,0:T(8,128)} %get-tuple-element.50), channel_id=1, source_target_pairs={{0,32},{1,33},{2,34},{3,35},{4,36},{5,37},{6,38},{7,39},{8,40},{9,... | collective-permute-start | bytes 1572872 | tf_op jit(solution)/shard_map/ppermute | solution.py:529
  112.2 1.9 collective-permute-start.11
  114.1 11.4 %forward_second.1 = (f32[2,256,256]{2,1,0:T(8,128)}, f32[2,256,256]{2,1,0:T(8,128)}, f32[2,256,256]{2,1,0:T(8,128)}, f32[2,256,256]{2,1,0:T(8,128)}, f32[2,256,256]{2,1,0:T(8,128)}) custom-call(s32[7]{0:T(128)} %stack.24.meta, s32[6,2]{1,0:T(8,128)} %copy-done.27, f32[2,256,256]{2,1,0:T(8,128)} %probe.7, bf16[6,256,256]{2,1,0:T(8,128)(2,1)} %bitcast.22, ...), custom_call_target="tpu_custom_call" | custom-call | tf_op jit(solution)/shard_map/forward_second/pallas_call | solution.py:560
  125.6 10.5 %backward_second.1 = (f32[2,256,256]{2,1,0:T(8,128)}, f32[2,256,256]{2,1,0:T(8,128)}, f32[2,256,256]{2,1,0:T(8,128)}, f32[2,256,256]{2,1,0:T(8,128)}) custom-call(s32[7]{0:T(128)} %stack.24.meta, f32[2,256,256]{2,1,0:T(8,128)} %get-tuple-element.58.back, f32[2,256,256]{2,1,0:T(8,128)} %pad_maximum_fusion.kern, bf16[8,256,256]{2,1,0:T(8,128)(2,1)} %constant.29.clone.tab, ...), custom_call_target="tpu_custom_call" | custom-call | tf_op jit(solution)/shard_map/backward_second/pallas_call | solution.py:562
  137.5 4.0 %collective-permute-start.16 = (f32[2,256,256]{2,1,0:T(8,128)}, f32[2,256,256]{2,1,0:T(8,128)S(1)}, u32[]{:S(2)}, u32[]{:S(2)}) collective-permute-start(f32[2,256,256]{2,1,0:T(8,128)} %get-tuple-element.60), channel_id=1, source_target_pairs={{0,32},{2,34},{4,36},{6,38},{8,40},{10,42},{12,44},{14,46},{16,48}... | collective-permute-start | bytes 1572872 | tf_op jit(solution)/shard_map/ppermute | solution.py:529
  141.6 6.1 %collective-permute-start.17 = (f32[2,256,256]{2,1,0:T(8,128)}, f32[2,256,256]{2,1,0:T(8,128)S(1)}, u32[]{:S(2)}, u32[]{:S(2)}) collective-permute-start(f32[2,256,256]{2,1,0:T(8,128)} %get-tuple-element.61), channel_id=1, source_target_pairs={{0,64},{2,66},{4,68},{6,70},{8,72},{10,74},{12,76},{14,78},{16,80}... | collective-permute-start | bytes 1572872 | tf_op jit(solution)/shard_map/ppermute | solution.py:529
  149.1 7.6 %collective-permute-start.19 = (f32[2,256,256]{2,1,0:T(8,128)S(1)}, f32[2,256,256]{2,1,0:T(8,128)S(1)}, u32[]{:S(2)}, u32[]{:S(2)}) collective-permute-start(f32[2,256,256]{2,1,0:T(8,128)S(1)} %copy-done.33), channel_id=1, source_target_pairs={{0,32},{2,34},{4,36},{6,38},{8,40},{10,42},{12,44},{14,46},{16,48}... | collective-permute-start | bytes 1572872 | tf_op jit(solution)/shard_map/ppermute | solution.py:529
  157.7 6.1 %collective-permute-start.20 = (f32[2,256,256]{2,1,0:T(8,128)S(1)}, f32[2,256,256]{2,1,0:T(8,128)S(1)}, u32[]{:S(2)}, u32[]{:S(2)}) collective-permute-start(f32[2,256,256]{2,1,0:T(8,128)S(1)} %copy-done.32), channel_id=1, source_target_pairs={{0,64},{2,66},{4,68},{6,70},{8,72},{10,74},{12,76},{14,78},{16,80}... | collective-permute-start | bytes 1572872 | tf_op jit(solution)/shard_map/ppermute | solution.py:529
  164.6 7.3 %terms_first.1 = (f32[6,2,256,256]{3,2,1,0:T(8,128)}, f32[4,2,256,256]{3,2,1,0:T(8,128)}, f32[4,2,256,128]{3,2,1,0:T(8,128)}, f32[4,2,256,128]{3,2,1,0:T(8,128)}) custom-call(s32[7]{0:T(128)} %stack.24.meta, s32[6,2]{1,0:T(8,128)} %copy-done.27, f32[2,256,256]{2,1,0:T(8,128)} %probe.7, f32[2,256,256]{2,1,0:T(8,128)} %get-tuple-element.45.rest_0_, ...), custom_call_target="tpu_custom_call" | custom-call | tf_op jit(solution)/shard_map/terms_first/pallas_call | solution.py:564
  172.0 1.9 collective-permute-start.22
  173.9 2.4 %collective-permute-start.24 = (f32[4,2,256,128]{3,2,1,0:T(8,128)}, f32[4,2,256,128]{3,2,1,0:T(8,128)S(1)}, u32[]{:S(2)}, u32[]{:S(2)}) collective-permute-start(f32[4,2,256,128]{3,2,1,0:T(8,128)} %get-tuple-element.72), channel_id=1, source_target_pairs={{1,0},{2,1},{3,2},{4,3},{5,4},{6,5},{7,6},{8,7},{9,8},{10,9},{11,1... | collective-permute-start | bytes 3145736 | tf_op jit(solution)/shard_map/ppermute | solution.py:520
  177.5 5.5 %terms_second.1 = (f32[6,2,256,256]{3,2,1,0:T(8,128)}, f32[2,2,256,256]{3,2,1,0:T(8,128)}, f32[2,2,256,128]{3,2,1,0:T(8,128)}, f32[2,2,256,128]{3,2,1,0:T(8,128)}) custom-call(s32[7]{0:T(128)} %stack.24.meta, s32[6,2]{1,0:T(8,128)} %copy-done.27, f32[2,256,256]{2,1,0:T(8,128)} %probe.7, ...), custom_call_target="tpu_custom_call", output_to_operand_aliasing={{0}: (3, {})} | custom-call | tf_op jit(solution)/shard_map/terms_second/pallas_call | solution.py:568
  183.0 5.3 %collective-permute-start.23 = (f32[2,2,256,128]{3,2,1,0:T(8,128)}, f32[2,2,256,128]{3,2,1,0:T(8,128)S(1)}, u32[]{:S(2)}, u32[]{:S(2)}) collective-permute-start(f32[2,2,256,128]{3,2,1,0:T(8,128)} %get-tuple-element.71), channel_id=1, source_target_pairs={{0,1},{1,2},{2,3},{3,4},{4,5},{5,6},{6,7},{7,8},{8,9},{9,10},{10,1... | collective-permute-start | bytes 1572872 | tf_op jit(solution)/shard_map/ppermute | solution.py:517
  188.3 1.9 collective-permute-start.25
  190.2 4.5 %collective-permute-done.23.left2 = f32[2,2,256,128]{3,2,1,0:T(8,128)S(1)} collective-permute-done((f32[2,2,256,128]{3,2,1,0:T(8,128)}, f32[2,2,256,128]{3,2,1,0:T(8,128)S(1)}, u32[]{:S(2)}, u32[]{:S(2)}) %collective-permute-start.23) | collective-permute-done | bytes 524320 | tf_op jit(solution)/shard_map/ppermute | solution.py:517
  194.7 6.4 %collective-permute-done.25.right2 = f32[2,2,256,128]{3,2,1,0:T(8,128)S(1)} collective-permute-done((f32[2,2,256,128]{3,2,1,0:T(8,128)}, f32[2,2,256,128]{3,2,1,0:T(8,128)S(1)}, u32[]{:S(2)}, u32[]{:S(2)}) %collective-permute-start.25) | collective-permute-done | bytes 524320 | tf_op jit(solution)/shard_map/ppermute | solution.py:520
  202.7 7.8 %add_terms.1 = f32[2,4096,256]{2,1,0:T(8,128)} custom-call(s32[6,2]{1,0:T(8,128)} %copy-done.27, s32[6,2]{1,0:T(8,128)} %copy-done.28, s32[6,2]{1,0:T(8,128)} %copy-done.29, f32[4,2,256,256]{3,2,1,0:T(8,128)} %get-tuple-element.68.own1, f32[2,2,256,256]{3,2,1,0:T(8,128)} %get-tuple-element.69.own2, f32[4,2,256,128]{3,2,1,0:T(8,128)} %copy-done.10, ...), custom_call_target="tpu_custom_call" | custom-call | tf_op jit(solution)/shard_map/add_terms/pallas_call | solution.py:572
  (107 shorter events, 23.2 us)
Async XLA Ops:
  0.6 57.7 %copy-start = (f32[256,256]{1,0:T(8,128)S(1)}, f32[256,256]{1,0:T(8,128)}, u32[]{:S(2)}) copy-start(f32[256,256]{1,0:T(8,128)} %param.11) | copy-start | bytes 786436
  1.5 5.3 %collective-permute-start = (s32[6,2]{1,0:T(8,128)S(1)}, s32[6,2]{1,0:T(8,128)S(1)}, u32[]{:S(2)}, u32[]{:S(2)}) collective-permute-start(s32[6,2]{1,0:T(8,128)S(1)} %copy.18.pos), channel_id=1, source_target_pairs={{0,1},{1,2},{2,3},{3,4},{4,5},{5,6},{6,7},{7,8},{8,9},{9,10},{10,1... | collective-permute-start | bytes 152 | tf_op jit(solution)/shard_map/ppermute | solution.py:517
  4.8 7.0 %collective-permute-start.1 = (s32[6,2]{1,0:T(8,128)S(1)}, s32[6,2]{1,0:T(8,128)S(1)}, u32[]{:S(2)}, u32[]{:S(2)}) collective-permute-start(s32[6,2]{1,0:T(8,128)S(1)} %copy.18.pos), channel_id=1, source_target_pairs={{1,0},{2,1},{3,2},{4,3},{5,4},{6,5},{7,6},{8,7},{9,8},{10,9},{11,1... | collective-permute-start | bytes 152 | tf_op jit(solution)/shard_map/ppermute | solution.py:520
  17.2 19.6 %collective-permute-start.2 = (f32[6,2,256,128]{3,2,1,0:T(8,128)}, f32[6,2,256,128]{3,2,1,0:T(8,128)S(1)}, u32[]{:S(2)}, u32[]{:S(2)}) collective-permute-start(f32[6,2,256,128]{3,2,1,0:T(8,128)} %get-tuple-element.38), channel_id=1, source_target_pairs={{0,1},{1,2},{2,3},{3,4},{4,5},{5,6},{6,7},{7,8},{8,9},{9,10},{10,1... | collective-permute-start | bytes 4718600 | tf_op jit(solution)/shard_map/ppermute | solution.py:517
  19.2 24.1 %collective-permute-start.3 = (f32[6,2,256,128]{3,2,1,0:T(8,128)}, f32[6,2,256,128]{3,2,1,0:T(8,128)S(1)}, u32[]{:S(2)}, u32[]{:S(2)}) collective-permute-start(f32[6,2,256,128]{3,2,1,0:T(8,128)} %get-tuple-element.39), channel_id=1, source_target_pairs={{1,0},{2,1},{3,2},{4,3},{5,4},{6,5},{7,6},{8,7},{9,8},{10,9},{11,1... | collective-permute-start | bytes 4718600 | tf_op jit(solution)/shard_map/ppermute | solution.py:520
  24.6 33.7 %copy-start.9 = (f32[256,256]{1,0:T(8,128)S(1)}, f32[256,256]{1,0:T(8,128)}, u32[]{:S(2)}) copy-start(f32[256,256]{1,0:T(8,128)} %constant.28.clone) | copy-start | bytes 786436
  50.3 30.7 %copy-start.12 = (f32[2,256,256]{2,1,0:T(8,128)S(1)}, f32[2,256,256]{2,1,0:T(8,128)}, u32[]{:S(2)}) copy-start(f32[2,256,256]{2,1,0:T(8,128)} %get-tuple-element.57.rest_12_) | copy-start | bytes 1572868
  50.3 30.7 %collective-permute-start.4 = (f32[2,256,256]{2,1,0:T(8,128)}, f32[2,256,256]{2,1,0:T(8,128)S(1)}, u32[]{:S(2)}, u32[]{:S(2)}) collective-permute-start(f32[2,256,256]{2,1,0:T(8,128)} %get-tuple-element.41.rest_9_), channel_id=1, source_target_pairs={{0,32},{1,33},{2,34},{3,35},{4,36},{5,37},{6,38},{7,39},{8,40},{9,... | collective-permute-start | bytes 1572872 | tf_op jit(solution)/shard_map/ppermute | solution.py:529
  52.0 30.3 %collective-permute-start.5 = (f32[2,256,256]{2,1,0:T(8,128)}, f32[2,256,256]{2,1,0:T(8,128)S(1)}, u32[]{:S(2)}, u32[]{:S(2)}) collective-permute-start(f32[2,256,256]{2,1,0:T(8,128)} %get-tuple-element.42.rest_10_), channel_id=1, source_target_pairs={{0,64},{1,65},{2,66},{3,67},{4,68},{5,69},{6,70},{7,71},{8,72},{9,... | collective-permute-start | bytes 1572872 | tf_op jit(solution)/shard_map/ppermute | solution.py:529
  53.2 29.1 %collective-permute-start.6 = (f32[2,256,256]{2,1,0:T(8,128)}, f32[2,256,256]{2,1,0:T(8,128)S(1)}, u32[]{:S(2)}, u32[]{:S(2)}) collective-permute-start(f32[2,256,256]{2,1,0:T(8,128)} %get-tuple-element.43.rest_11_), channel_id=1, source_target_pairs={{0,96},{1,97},{2,98},{3,99},{4,100},{5,101},{6,102},{7,103},{8,104... | collective-permute-start | bytes 1572872 | tf_op jit(solution)/shard_map/ppermute | solution.py:529
  55.1 53.6 %collective-permute-start.13 = (f32[2,256,256]{2,1,0:T(8,128)}, f32[2,256,256]{2,1,0:T(8,128)S(1)}, u32[]{:S(2)}, u32[]{:S(2)}) collective-permute-start(f32[2,256,256]{2,1,0:T(8,128)} %get-tuple-element.55.rest_10_), channel_id=1, source_target_pairs={{1,33},{3,35},{5,37},{7,39},{9,41},{11,43},{13,45},{15,47},{17,49}... | collective-permute-start | bytes 1572872 | tf_op jit(solution)/shard_map/ppermute | solution.py:529
  56.4 52.7 %collective-permute-start.14 = (f32[2,256,256]{2,1,0:T(8,128)}, f32[2,256,256]{2,1,0:T(8,128)S(1)}, u32[]{:S(2)}, u32[]{:S(2)}) collective-permute-start(f32[2,256,256]{2,1,0:T(8,128)} %get-tuple-element.56.rest_11_), channel_id=1, source_target_pairs={{0,64},{2,66},{4,68},{6,70},{8,72},{10,74},{12,76},{14,78},{16,80}... | collective-permute-start | bytes 1572872 | tf_op jit(solution)/shard_map/ppermute | solution.py:529
  81.0 31.2 %collective-permute-start.15 = (f32[2,256,256]{2,1,0:T(8,128)S(1)}, f32[2,256,256]{2,1,0:T(8,128)S(1)}, u32[]{:S(2)}, u32[]{:S(2)}) collective-permute-start(f32[2,256,256]{2,1,0:T(8,128)S(1)} %copy-done.12), channel_id=1, source_target_pairs={{1,97},{3,99},{5,101},{7,103},{9,105},{11,107},{13,109},{15,111},{... | collective-permute-start | bytes 1572872 | tf_op jit(solution)/shard_map/ppermute | solution.py:529
  105.1 31.1 %collective-permute-start.7 = (f32[2,256,256]{2,1,0:T(8,128)}, f32[2,256,256]{2,1,0:T(8,128)S(1)}, u32[]{:S(2)}, u32[]{:S(2)}) collective-permute-start(f32[2,256,256]{2,1,0:T(8,128)} %get-tuple-element.46), channel_id=1, source_target_pairs={{0,32},{1,33},{2,34},{3,35},{4,36},{5,37},{6,38},{7,39},{8,40},{9,... | collective-permute-start | bytes 1572872 | tf_op jit(solution)/shard_map/ppermute | solution.py:529
  107.3 30.2 %collective-permute-start.8 = (f32[2,256,256]{2,1,0:T(8,128)}, f32[2,256,256]{2,1,0:T(8,128)S(1)}, u32[]{:S(2)}, u32[]{:S(2)}) collective-permute-start(f32[2,256,256]{2,1,0:T(8,128)} %get-tuple-element.47), channel_id=1, source_target_pairs={{0,64},{1,65},{2,66},{3,67},{4,68},{5,69},{6,70},{7,71},{8,72},{9,... | collective-permute-start | bytes 1572872 | tf_op jit(solution)/shard_map/ppermute | solution.py:529
  108.8 32.8 %collective-permute-start.9 = (f32[2,256,256]{2,1,0:T(8,128)}, f32[2,256,256]{2,1,0:T(8,128)S(1)}, u32[]{:S(2)}, u32[]{:S(2)}) collective-permute-start(f32[2,256,256]{2,1,0:T(8,128)} %get-tuple-element.48), channel_id=1, source_target_pairs={{0,96},{1,97},{2,98},{3,99},{4,100},{5,101},{6,102},{7,103},{8,104... | collective-permute-start | bytes 1572872 | tf_op jit(solution)/shard_map/ppermute | solution.py:529
  109.2 38.5 %collective-permute-start.10 = (f32[2,256,256]{2,1,0:T(8,128)}, f32[2,256,256]{2,1,0:T(8,128)S(1)}, u32[]{:S(2)}, u32[]{:S(2)}) collective-permute-start(f32[2,256,256]{2,1,0:T(8,128)} %get-tuple-element.50), channel_id=1, source_target_pairs={{0,32},{1,33},{2,34},{3,35},{4,36},{5,37},{6,38},{7,39},{8,40},{9,... | collective-permute-start | bytes 1572872 | tf_op jit(solution)/shard_map/ppermute | solution.py:529
  112.2 36.8 %collective-permute-start.11 = (f32[2,256,256]{2,1,0:T(8,128)S(1)}, f32[2,256,256]{2,1,0:T(8,128)S(1)}, u32[]{:S(2)}, u32[]{:S(2)}) collective-permute-start(f32[2,256,256]{2,1,0:T(8,128)S(1)} %copy-done.35), channel_id=1, source_target_pairs={{0,64},{1,65},{2,66},{3,67},{4,68},{5,69},{6,70},{7,71},{8,72},{9,... | collective-permute-start | bytes 1572872 | tf_op jit(solution)/shard_map/ppermute | solution.py:529
  125.6 32.1 %copy-start.32 = (f32[2,256,256]{2,1,0:T(8,128)S(1)}, f32[2,256,256]{2,1,0:T(8,128)}, u32[]{:S(2)}) copy-start(f32[2,256,256]{2,1,0:T(8,128)} %get-tuple-element.65) | copy-start | bytes 1572868
  125.6 38.2 %copy-start.31 = (f32[2,256,256]{2,1,0:T(8,128)S(1)}, f32[2,256,256]{2,1,0:T(8,128)}, u32[]{:S(2)}) copy-start(f32[2,256,256]{2,1,0:T(8,128)} %get-tuple-element.66) | copy-start | bytes 1572868
  136.2 28.4 %copy-start.13 = (f32[2,256,256]{2,1,0:T(8,128)}, f32[2,256,256]{2,1,0:T(8,128)S(1)}, u32[]{:S(2)}) copy-start(f32[2,256,256]{2,1,0:T(8,128)S(1)} %collective-permute-done.7.rest_1_) | copy-start | bytes 1572868
  136.2 21.5 %collective-permute-start.12 = (f32[2,256,256]{2,1,0:T(8,128)S(1)}, f32[2,256,256]{2,1,0:T(8,128)S(1)}, u32[]{:S(2)}, u32[]{:S(2)}) collective-permute-start(f32[2,256,256]{2,1,0:T(8,128)S(1)} %copy-done.34), channel_id=1, source_target_pairs={{0,96},{1,97},{2,98},{3,99},{4,100},{5,101},{6,102},{7,103},{8,104... | collective-permute-start | bytes 1572872 | tf_op jit(solution)/shard_map/ppermute | solution.py:529
  137.5 26.3 %collective-permute-start.16 = (f32[2,256,256]{2,1,0:T(8,128)}, f32[2,256,256]{2,1,0:T(8,128)S(1)}, u32[]{:S(2)}, u32[]{:S(2)}) collective-permute-start(f32[2,256,256]{2,1,0:T(8,128)} %get-tuple-element.60), channel_id=1, source_target_pairs={{0,32},{2,34},{4,36},{6,38},{8,40},{10,42},{12,44},{14,46},{16,48}... | collective-permute-start | bytes 1572872 | tf_op jit(solution)/shard_map/ppermute | solution.py:529
  141.6 30.4 %collective-permute-start.17 = (f32[2,256,256]{2,1,0:T(8,128)}, f32[2,256,256]{2,1,0:T(8,128)S(1)}, u32[]{:S(2)}, u32[]{:S(2)}) collective-permute-start(f32[2,256,256]{2,1,0:T(8,128)} %get-tuple-element.61), channel_id=1, source_target_pairs={{0,64},{2,66},{4,68},{6,70},{8,72},{10,74},{12,76},{14,78},{16,80}... | collective-permute-start | bytes 1572872 | tf_op jit(solution)/shard_map/ppermute | solution.py:529
  147.7 26.2 %collective-permute-start.18 = (f32[2,256,256]{2,1,0:T(8,128)}, f32[2,256,256]{2,1,0:T(8,128)S(1)}, u32[]{:S(2)}, u32[]{:S(2)}) collective-permute-start(f32[2,256,256]{2,1,0:T(8,128)} %get-tuple-element.62), channel_id=1, source_target_pairs={{0,96},{2,98},{4,100},{6,102},{8,104},{10,106},{12,108},{14,110},{... | collective-permute-start | bytes 1572872 | tf_op jit(solution)/shard_map/ppermute | solution.py:529
  149.1 27.3 %collective-permute-start.19 = (f32[2,256,256]{2,1,0:T(8,128)S(1)}, f32[2,256,256]{2,1,0:T(8,128)S(1)}, u32[]{:S(2)}, u32[]{:S(2)}) collective-permute-start(f32[2,256,256]{2,1,0:T(8,128)S(1)} %copy-done.33), channel_id=1, source_target_pairs={{0,32},{2,34},{4,36},{6,38},{8,40},{10,42},{12,44},{14,46},{16,48}... | collective-permute-start | bytes 1572872 | tf_op jit(solution)/shard_map/ppermute | solution.py:529
  157.7 18.7 %collective-permute-start.20 = (f32[2,256,256]{2,1,0:T(8,128)S(1)}, f32[2,256,256]{2,1,0:T(8,128)S(1)}, u32[]{:S(2)}, u32[]{:S(2)}) collective-permute-start(f32[2,256,256]{2,1,0:T(8,128)S(1)} %copy-done.32), channel_id=1, source_target_pairs={{0,64},{2,66},{4,68},{6,70},{8,72},{10,74},{12,76},{14,78},{16,80}... | collective-permute-start | bytes 1572872 | tf_op jit(solution)/shard_map/ppermute | solution.py:529
  163.8 12.6 %collective-permute-start.21 = (f32[2,256,256]{2,1,0:T(8,128)S(1)}, f32[2,256,256]{2,1,0:T(8,128)S(1)}, u32[]{:S(2)}, u32[]{:S(2)}) collective-permute-start(f32[2,256,256]{2,1,0:T(8,128)S(1)} %copy-done.31), channel_id=1, source_target_pairs={{0,96},{2,98},{4,100},{6,102},{8,104},{10,106},{12,108},{14,110},{... | collective-permute-start | bytes 1572872 | tf_op jit(solution)/shard_map/ppermute | solution.py:529
  172.0 29.2 %collective-permute-start.22 = (f32[4,2,256,128]{3,2,1,0:T(8,128)}, f32[4,2,256,128]{3,2,1,0:T(8,128)S(1)}, u32[]{:S(2)}, u32[]{:S(2)}) collective-permute-start(f32[4,2,256,128]{3,2,1,0:T(8,128)} %get-tuple-element.70), channel_id=1, source_target_pairs={{0,1},{1,2},{2,3},{3,4},{4,5},{5,6},{6,7},{7,8},{8,9},{9,10},{10,1... | collective-permute-start | bytes 3145736 | tf_op jit(solution)/shard_map/ppermute | solution.py:517
  173.9 27.2 %collective-permute-start.24 = (f32[4,2,256,128]{3,2,1,0:T(8,128)}, f32[4,2,256,128]{3,2,1,0:T(8,128)S(1)}, u32[]{:S(2)}, u32[]{:S(2)}) collective-permute-start(f32[4,2,256,128]{3,2,1,0:T(8,128)} %get-tuple-element.72), channel_id=1, source_target_pairs={{1,0},{2,1},{3,2},{4,3},{5,4},{6,5},{7,6},{8,7},{9,8},{10,9},{11,1... | collective-permute-start | bytes 3145736 | tf_op jit(solution)/shard_map/ppermute | solution.py:520
  183.0 11.7 %collective-permute-start.23 = (f32[2,2,256,128]{3,2,1,0:T(8,128)}, f32[2,2,256,128]{3,2,1,0:T(8,128)S(1)}, u32[]{:S(2)}, u32[]{:S(2)}) collective-permute-start(f32[2,2,256,128]{3,2,1,0:T(8,128)} %get-tuple-element.71), channel_id=1, source_target_pairs={{0,1},{1,2},{2,3},{3,4},{4,5},{5,6},{6,7},{7,8},{8,9},{9,10},{10,1... | collective-permute-start | bytes 1572872 | tf_op jit(solution)/shard_map/ppermute | solution.py:517
  188.3 12.8 %collective-permute-start.25 = (f32[2,2,256,128]{3,2,1,0:T(8,128)}, f32[2,2,256,128]{3,2,1,0:T(8,128)S(1)}, u32[]{:S(2)}, u32[]{:S(2)}) collective-permute-start(f32[2,2,256,128]{3,2,1,0:T(8,128)} %get-tuple-element.73), channel_id=1, source_target_pairs={{1,0},{2,1},{3,2},{4,3},{5,4},{6,5},{7,6},{8,7},{9,8},{10,9},{11,1... | collective-permute-start | bytes 1572872 | tf_op jit(solution)/shard_map/ppermute | solution.py:520
  (30 other events, 223.0 us)

commit v2 on v1

v2 whole, which is shorter than its diff:
```python
import math

import jax
import jax.numpy as jnp
import ml_dtypes
import numpy as np
from jax import lax
from jax.experimental import pallas as pl
from jax.experimental.pallas import tpu as pltpu
from jax.sharding import PartitionSpec as P

RIM = 128
HALF = 128
W = 256
F32 = jnp.float32
BF16 = jnp.bfloat16
VMEM_BYTES = 56 * 1024 * 1024

ANY_SPEC = pl.BlockSpec(memory_space=pl.ANY)
SMEM_SPEC = pl.BlockSpec(memory_space=pltpu.SMEM)
VMEM_SPEC = pl.BlockSpec(memory_space=pltpu.VMEM)


def split_table(table):
    high = table.astype(ml_dtypes.bfloat16)
    low = (table - high.astype(np.float64)).astype(ml_dtypes.bfloat16)
    return high, low


def make_tables():
    freq = np.arange(HALF)[:, None]
    place = np.arange(HALF)[None, :]
    out = []
    for odd in (0, 1):
        angle = 2.0 * math.pi * (((2 * freq + odd) * place) % W) / W
        re, im = np.cos(angle) / math.sqrt(W), -np.sin(angle) / math.sqrt(W)
        real = np.block([[re, -im], [im, re]])
        out += [*split_table(real), *split_table(real.T)]
    return np.stack(out)


def make_order():
    order = np.concatenate([np.arange(0, W, 2), np.arange(1, W, 2)])
    hot = np.zeros((W, W), np.float32)
    hot[np.arange(W), order] = 1.0
    return hot


TABLES = make_tables()
ORDER = make_order()


def dot(first, second):
    return jnp.dot(first, second, preferred_element_type=F32)


def split(value):
    high = value.astype(BF16)
    return high, (value - high.astype(F32)).astype(BF16)


def table_left(tab, at, value):
    high, low = split(value)
    return dot(tab[at], high) + dot(tab[at], low) + dot(tab[at + 1], high)


def table_right(value, tab, at):
    high, low = split(value)
    return dot(high, tab[at]) + dot(low, tab[at]) + dot(high, tab[at + 1])


def to_spectrum(re, im, tab):
    h = HALF
    total = jnp.concatenate([re[:h] + re[h:], im[:h] + im[h:]], 0)
    diff = jnp.concatenate([re[:h] - re[h:], im[:h] - im[h:]], 0)
    even = table_left(tab, 0, total)
    odd = table_left(tab, 4, diff)
    yr = jnp.concatenate([even[:h], odd[:h]], 0)
    yi = jnp.concatenate([even[h:], odd[h:]], 0)
    total = jnp.concatenate([yr[:, :h] + yr[:, h:], yi[:, :h] + yi[:, h:]], 1)
    diff = jnp.concatenate([yr[:, :h] - yr[:, h:], yi[:, :h] - yi[:, h:]], 1)
    return table_right(total, tab, 2), table_right(diff, tab, 6)


def from_spectrum(even, odd, tab):
    h = HALF
    a = table_right(even, tab, 0)
    b = table_right(odd, tab, 4)
    yr = jnp.concatenate([a[:, :h] + b[:, :h], a[:, :h] - b[:, :h]], 1)
    yi = jnp.concatenate([a[:, h:] + b[:, h:], a[:, h:] - b[:, h:]], 1)
    p = table_left(tab, 2, jnp.concatenate([yr[:h], yi[:h]], 0))
    q = table_left(tab, 6, jnp.concatenate([yr[h:], yi[h:]], 0))
    re = jnp.concatenate([p[:h] + q[:h], p[:h] - q[:h]], 0)
    im = jnp.concatenate([p[h:] + q[h:], p[h:] - q[h:]], 0)
    return re, im


def turn(spectrum, cosine, sine):
    h = HALF
    re, im = spectrum[:, :h], spectrum[:, h:]
    return jnp.concatenate([re * cosine - im * sine, re * sine + im * cosine], 1)


def propagate(re, im, kern, tab, sign):
    h = HALF
    even, odd = to_spectrum(re, im, tab)
    cosine, sine = kern[0], sign * kern[1]
    even = turn(even, cosine[:, :h], sine[:, :h])
    odd = turn(odd, cosine[:, h:], sine[:, h:])
    return from_spectrum(even, odd, tab)


def cost(us):
    return pl.CostEstimate(flops=0, transcendentals=0, bytes_accessed=int(us * 3.3e6))


def params():
    return pltpu.CompilerParams(vmem_limit_bytes=VMEM_BYTES)


def row_base(row):
    base = pl.multiple_of((row // 8) * 8, 8)
    extra = pl.multiple_of(jnp.where(base + W < 4096, base + W, base - 8), 8)
    return base, extra, row - base


def rows_below(delta, shape):
    return lax.broadcasted_iota(jnp.int32, shape, len(shape) - 2) < delta


def aligned(cols):
    return pl.ds(pl.multiple_of(cols, HALF), HALF)


def slot_of(owner, second):
    return 4 + owner // 2 if second else owner


def is_owner(owner, second):
    return owner % 2 == lax.axis_index("tile") % 2 if second else owner >= 0


STRIP = jax.ShapeDtypeStruct((2, W, HALF), F32)
FIELD = jax.ShapeDtypeStruct((2, W, W), F32)


class Cut:
    def __init__(self, image, row, cols, out, extra, sems):
        base, more, self.delta = row_base(row)
        self.out, self.extra = out, extra
        cols = aligned(cols)
        self.copies = (
            pltpu.make_async_copy(image.at[:, pl.ds(base, W), cols], out, sems.at[0]),
            pltpu.make_async_copy(image.at[:, pl.ds(more, 8), cols], extra, sems.at[1]),
        )

    def start(self):
        for copy in self.copies:
            copy.start()

    def finish(self):
        for copy in self.copies:
            copy.wait()
        mask = rows_below(self.delta, (2, 8, HALF))
        self.out[:, 0:8, :] = jnp.where(mask, self.extra[...], self.out[:, 0:8, :])


def cut_rims(cap):
    def kernel(pos_left, pos_right, image, *rest):
        outs, (buf, extra, sems, put_sems) = rest[:2], rest[2:]
        cuts, puts = [], []
        for s in range(cap):
            for side, pos in enumerate((pos_left, pos_right)):
                at = 2 * s + side
                cuts.append(
                    Cut(image, pos[s, 0], side * HALF, buf.at[at], extra.at[at], sems.at[at])
                )
                puts.append(pltpu.make_async_copy(buf.at[at], outs[side].at[s], put_sems.at[at]))
        for cut in cuts:
            cut.start()
        for cut, put in zip(cuts, puts):
            cut.finish()
            put.start()
        for put in puts:
            put.wait()

    strips = jax.ShapeDtypeStruct((cap, 2, W, HALF), F32)
    return pl.pallas_call(
        kernel,
        out_shape=(strips, strips),
        in_specs=[SMEM_SPEC, SMEM_SPEC, ANY_SPEC],
        out_specs=(ANY_SPEC, ANY_SPEC),
        scratch_shapes=[
            pltpu.VMEM((2 * cap, 2, W, HALF), F32),
            pltpu.VMEM((2 * cap, 2, 8, HALF), F32),
            pltpu.SemaphoreType.DMA((2 * cap, 2)),
            pltpu.SemaphoreType.DMA((2 * cap,)),
        ],
        compiler_params=params(),
        cost_estimate=cost(4),
        name="cut_rims",
    )


def pure_halves():
    def kernel(pos, image, *rest):
        outs, (extra, sems) = rest[:4], rest[4:]
        group = lax.axis_index("cuts")
        cuts = []
        for k in range(4):
            s = slot_of((group + k) % 4, 0)
            cols = jnp.where(pos[s, 1] > RIM, HALF, 0)
            cuts.append(Cut(image, pos[s, 0], cols, outs[k], extra.at[k], sems.at[k]))
        for cut in cuts:
            cut.start()
        for cut in cuts:
            cut.finish()

    return pl.pallas_call(
        kernel,
        out_shape=(STRIP,) * 4,
        in_specs=[SMEM_SPEC, ANY_SPEC],
        out_specs=(VMEM_SPEC,) * 4,
        scratch_shapes=[
            pltpu.VMEM((4, 2, 8, HALF), F32),
            pltpu.SemaphoreType.DMA((4, 2)),
        ],
        compiler_params=params(),
        cost_estimate=cost(3),
        name="pure_halves",
    )


def mixed_windows():
    def kernel(pos, widths, image, from_left, from_right, *rest):
        outs, bufs, (extra, rim, sems) = rest[:8], rest[8:16], rest[16:]
        group, tile = lax.axis_index("cuts"), lax.axis_index("tile")
        tiles = lax.axis_size("tile")

        def transfers(at, s):
            base, more, _ = row_base(pos[s, 0])
            cols = pl.ds(0, W) if at >= 4 else aligned(jnp.where(pos[s, 1] > RIM, 0, HALF))
            few = extra.at[at] if at >= 4 else extra.at[at, :, :, pl.ds(0, HALF)]
            return (
                pltpu.make_async_copy(image.at[:, pl.ds(base, W), cols], bufs[at], sems.at[at, 0]),
                pltpu.make_async_copy(image.at[:, pl.ds(more, 8), cols], few, sems.at[at, 1]),
            )

        def rim_copy(at, s, source):
            return pltpu.make_async_copy(source.at[s], rim.at[at], sems.at[at, 2])

        def put(at, s):
            return pltpu.make_async_copy(bufs[at], outs[at], sems.at[at, 3])

        def each(job):
            for at in range(8):
                second, k = divmod(at, 4)
                owner = (group + k) % 4
                pl.when(is_owner(owner, second))(
                    lambda at=at, owner=owner, second=second: job(at, slot_of(owner, second))
                )

        def begin(at, s):
            for copy in transfers(at, s):
                copy.start()

            @pl.when(pos[s, 1] > RIM)
            def _():
                rim_copy(at, s, from_right).start()

            @pl.when(pos[s, 1] <= RIM)
            def _():
                rim_copy(at, s, from_left).start()

        def work(at, s):
            for copy in transfers(at, s):
                copy.wait()
            edge = pos[s, 1] - RIM
            out = bufs[at]
            width = out.shape[-1]
            mask = rows_below(pos[s, 0] % 8, (2, 8, width))
            out[:, 0:8, :] = jnp.where(mask, extra[at, :, :, :width], out[:, 0:8, :])
            lane = lax.broadcasted_iota(jnp.int32, (W, HALF), 1)
            low, high = slice(0, HALF), slice(width - HALF, width)

            @pl.when(edge > 0)
            def _():
                rim_copy(at, s, from_right).wait()
                kept = (lane < widths[0, 1]) & (tile < tiles - 1)
                for part in range(2):
                    value = jnp.where(kept, rim[at, part], 1.0 - part)
                    out[part, :, low] = jnp.where(lane < edge, value, out[part, :, low])

            @pl.when(edge <= 0)
            def _():
                rim_copy(at, s, from_left).wait()
                kept = (lane >= HALF - widths[0, 0]) & (tile > 0)
                for part in range(2):
                    value = jnp.where(kept, rim[at, part], 1.0 - part)
                    out[part, :, high] = jnp.where(lane >= HALF + edge, value, out[part, :, high])

            put(at, s).start()

        each(begin)
        each(work)
        each(lambda at, s: put(at, s).wait())

    return pl.pallas_call(
        kernel,
        out_shape=(STRIP,) * 4 + (FIELD,) * 4,
        in_specs=[SMEM_SPEC, SMEM_SPEC, ANY_SPEC, ANY_SPEC, ANY_SPEC],
        out_specs=(ANY_SPEC,) * 8,
        scratch_shapes=[pltpu.VMEM((2, W, HALF), F32)] * 4
        + [pltpu.VMEM((2, W, W), F32)] * 4
        + [
            pltpu.VMEM((8, 2, 8, W), F32),
            pltpu.VMEM((8, 2, W, HALF), F32),
            pltpu.SemaphoreType.DMA((8, 4)),
        ],
        compiler_params=params(),
        cost_estimate=cost(5),
        name="mixed_windows",
    )


class Windows:
    def __init__(self, refs, buf, right, sems):
        self.refs, self.buf, self.sems = refs, buf, sems
        self.at = jnp.where(right, HALF, 0)

    def copies(self, k, n):
        out = self.buf.at[n]
        if len(self.refs) == 4:
            return [pltpu.make_async_copy(self.refs[k], out, self.sems.at[n, 0])]
        pure, mixed = self.refs[k], self.refs[4 + k]
        return [
            pltpu.make_async_copy(pure, out.at[:, :, aligned(self.at)], self.sems.at[n, 0]),
            pltpu.make_async_copy(mixed, out.at[:, :, aligned(HALF - self.at)], self.sems.at[n, 1]),
        ]

    def start(self):
        for k in range(4):
            for copy in self.copies(k, (lax.axis_index("cuts") - k) % 4):
                copy.start()

    def wait(self, n):
        for copy in self.copies(0, n):
            copy.wait()


class Loads:
    def __init__(self, refs, bufs, sems):
        self.copies = [
            pltpu.make_async_copy(ref, buf, sems.at[at])
            for at, (ref, buf) in enumerate(zip(refs, bufs))
        ]
        for copy in self.copies:
            copy.start()

    def wait(self, *which):
        for at in which:
            self.copies[at].wait()


CONSTANTS = [
    pltpu.VMEM((2, W, W), F32),
    pltpu.VMEM((8, W, W), BF16),
    pltpu.VMEM((2, W, W), F32),
    pltpu.VMEM((W, W), BF16),
    pltpu.VMEM((W, W), BF16),
    pltpu.SemaphoreType.DMA((5,)),
]


def place_probe(probe, row, col, scale, out):
    for part in range(2):
        rolled = pltpu.roll(probe[part], (col - RIM) % W, 1)
        out[part] = pltpu.roll(rolled, row % 8, 0) * scale


def forward_steps(wins, in_buf, kern, tab):
    def step(n, carry):
        wins.wait(n)
        re, im = in_buf[n, 0], in_buf[n, 1]
        wr, wi = wins.buf[n, 0], wins.buf[n, 1]
        re, im = wr * re - wi * im, wr * im + wi * re
        re, im = propagate(re, im, kern, tab, 1.0)
        in_buf[n + 1, 0] = re
        in_buf[n + 1, 1] = im
        return carry

    lax.fori_loop(0, 4, step, 0)


def far_step(in_buf, seen, order, order_t, tab, back):
    half_seen = dot(order[...], seen[...]).astype(BF16)
    target = dot(half_seen, order_t[...])
    spectra = to_spectrum(in_buf[4, 0], in_buf[4, 1], tab)
    chis = []
    for odd in range(2):
        re, im = spectra[odd][:, :HALF], spectra[odd][:, HALF:]
        excess = re * re + im * im - target[:, odd * HALF : (odd + 1) * HALF]
        chis.append(jnp.concatenate([re * excess, im * excess], 1))
    re, im = from_spectrum(chis[0], chis[1], tab)
    back[0] = re
    back[1] = im


def backward_steps(wins, turned_buf, back, kern, tab, store):
    def step(at, carry):
        n = 3 - at
        re, im = propagate(back[0], back[1], kern, tab, -1.0)
        turned_buf[n, 0] = re
        turned_buf[n, 1] = im
        for k in range(4):
            pl.when((lax.axis_index("cuts") + k) % 4 == n)(lambda k=k: store(k, n).start())
        wr, wi = wins.buf[n, 0], wins.buf[n, 1]
        back[0] = wr * re + wi * im
        back[1] = wr * im - wi * re
        return carry

    lax.fori_loop(0, 4, step, 0)


def forward_first():
    def kernel(pos, counts, probe, measured, kern, tab, order, order_t, *rest):
        refs, inputs, back = rest[:8], rest[8:12], rest[12]
        win_buf, in_buf, seen, load_sems, sems, *held = rest[13:]
        group = lax.axis_index("cuts")
        s = slot_of(group, 0)
        *bufs, const_sems = held
        consts = Loads((probe, tab, kern, order, order_t), bufs, const_sems)
        probe, tab, kern, order, order_t = bufs
        wins = Windows(refs, win_buf, pos[s, 1] > RIM, load_sems)
        wins.start()
        seeing = pltpu.make_async_copy(measured.at[s], seen, sems.at[4])
        seeing.start()
        consts.wait(0)
        place_probe(probe, pos[s, 0], pos[s, 1], jnp.where(s < counts[0], 1.0, 0.0), in_buf.at[0])
        consts.wait(1, 2)
        forward_steps(wins, in_buf, kern, tab)
        stores = [
            pltpu.make_async_copy(in_buf.at[(group + k) % 4], inputs[k], sems.at[k])
            for k in range(4)
        ]
        for copy in stores:
            copy.start()
        seeing.wait()
        consts.wait(3, 4)
        far_step(in_buf, seen, order, order_t, tab, back)
        for copy in stores:
            copy.wait()

    return pl.pallas_call(
        kernel,
        out_shape=(FIELD,) * 5,
        in_specs=[SMEM_SPEC, SMEM_SPEC] + [ANY_SPEC] * 14,
        out_specs=(ANY_SPEC,) * 4 + (VMEM_SPEC,),
        scratch_shapes=[
            pltpu.VMEM((4, 2, W, W), F32),
            pltpu.VMEM((5, 2, W, W), F32),
            pltpu.VMEM((W, W), BF16),
            pltpu.SemaphoreType.DMA((4, 2)),
            pltpu.SemaphoreType.DMA((5,)),
            *CONSTANTS,
        ],
        compiler_params=params(),
        cost_estimate=cost(9),
        name="forward_first",
    )


def backward_first():
    def kernel(pos, back, kern, tab, *rest):
        refs, turned = rest[:8], rest[8:12]
        win_buf, turned_buf, back_buf, load_sems, sems, *held = rest[12:]
        s = slot_of(lax.axis_index("cuts"), 0)
        *bufs, const_sems = held
        consts = Loads((back, tab, kern), (back_buf, *bufs), const_sems)
        tab, kern = bufs
        wins = Windows(refs, win_buf, pos[s, 1] > RIM, load_sems)
        wins.start()
        consts.wait(0, 1, 2)


        def store(k, n):
            return pltpu.make_async_copy(turned_buf.at[n], turned[k], sems.at[k])

        for n in range(4):
            wins.wait(n)
        backward_steps(wins, turned_buf, back_buf, kern, tab, store)
        for k in range(4):
            store(k, 0).wait()

    return pl.pallas_call(
        kernel,
        out_shape=(FIELD,) * 4,
        in_specs=[SMEM_SPEC] + [ANY_SPEC] * 11,
        out_specs=(ANY_SPEC,) * 4,
        scratch_shapes=[
            pltpu.VMEM((4, 2, W, W), F32),
            pltpu.VMEM((4, 2, W, W), F32),
            pltpu.VMEM((2, W, W), F32),
            pltpu.SemaphoreType.DMA((4, 2)),
            pltpu.SemaphoreType.DMA((4,)),
            pltpu.VMEM((8, W, W), BF16),
            pltpu.VMEM((2, W, W), F32),
            pltpu.SemaphoreType.DMA((3,)),
        ],
        compiler_params=params(),
        cost_estimate=cost(7),
        name="backward_first",
    )


def both_ways(second):
    count = 4 if second else 8

    def kernel(pos, counts, probe, measured, kern, tab, order, order_t, *rest):
        refs, outs = rest[:count], rest[count : count + 4]
        win_buf, in_buf, turned_buf, back_buf, seen, load_sems, sems, *held = rest[count + 4 :]
        group = lax.axis_index("cuts")
        s = slot_of(group, second)

        def store(k, n):
            return pltpu.make_async_copy(turned_buf.at[n], outs[k].at[1], sems.at[4 + k])

        @pl.when(is_owner(group, second))
        def _():
            *bufs, const_sems = held
            consts = Loads((probe, tab, kern, order, order_t), bufs, const_sems)
            probe_buf, tab_buf, kern_buf, order_buf, order_t_buf = bufs
            wins = Windows(refs, win_buf, pos[s, 1] > RIM, load_sems)
            wins.start()
            seeing = pltpu.make_async_copy(measured.at[s], seen, sems.at[8])
            seeing.start()
            scale = jnp.where(s < counts[0], 1.0, 0.0)
            consts.wait(0)
            place_probe(probe_buf, pos[s, 0], pos[s, 1], scale, in_buf.at[0])
            consts.wait(1, 2)
            forward_steps(wins, in_buf, kern_buf, tab_buf)
            stores = [
                pltpu.make_async_copy(in_buf.at[(group + k) % 4], outs[k].at[0], sems.at[k])
                for k in range(4)
            ]
            for copy in stores:
                copy.start()
            seeing.wait()
            consts.wait(3, 4)
            far_step(in_buf, seen, order_buf, order_t_buf, tab_buf, back_buf)
            backward_steps(wins, turned_buf, back_buf, kern_buf, tab_buf, store)
            for copy in stores:
                copy.wait()
            for k in range(4):
                store(k, 0).wait()

    pair = jax.ShapeDtypeStruct((2, 2, W, W), F32)
    return pl.pallas_call(
        kernel,
        out_shape=(pair,) * 4,
        in_specs=[SMEM_SPEC, SMEM_SPEC] + [ANY_SPEC] * (6 + count),
        out_specs=(ANY_SPEC,) * 4,
        scratch_shapes=[
            pltpu.VMEM((4, 2, W, W), F32),
            pltpu.VMEM((5, 2, W, W), F32),
            pltpu.VMEM((4, 2, W, W), F32),
            pltpu.VMEM((2, W, W), F32),
            pltpu.VMEM((W, W), BF16),
            pltpu.SemaphoreType.DMA((4, 2)),
            pltpu.SemaphoreType.DMA((9,)),
            *CONSTANTS,
        ],
        compiler_params=params(),
        cost_estimate=cost(14),
        name="both_second" if second else "both_first",
    )


def each_owner(second, job):
    for j in range(4):
        owner = (lax.axis_index("cuts") - j) % 4
        pl.when(is_owner(owner, second))(lambda j=j, owner=owner: job(j, slot_of(owner, second)))


def adjoint_of(t_buf, w_buf, pos, s, out):
    re, im = t_buf[0], t_buf[1]
    wr, wi = w_buf[0], w_buf[1]
    for part, value in enumerate((wr * re + wi * im, wr * im - wi * re)):
        rolled = pltpu.roll(value, (W + RIM - pos[s, 1]) % W, 1)
        out[part] = pltpu.roll(rolled, (W - pos[s, 0] % 8) % W, 0)


def conj_terms(i_buf, t_buf, half):
    ir, ii = i_buf[0, :, half], i_buf[1, :, half]
    re, im = t_buf[0, :, half], t_buf[1, :, half]
    return ir * re + ii * im, ir * im - ii * re


LOW, HIGH = slice(0, HALF), slice(HALF, W)


def lanes():
    return lax.broadcasted_iota(jnp.int32, (W, HALF), 1)


def rim_terms(i_buf, t_buf, edge, widths, to_left, to_right):
    tile, tiles = lax.axis_index("tile"), lax.axis_size("tile")
    lane = lanes()
    sent_left = (lane >= HALF + edge) & (lane >= HALF - widths[0, 0]) & (tile > 0)
    sent_right = (lane < edge) & (lane < widths[0, 1]) & (tile < tiles - 1)

    @pl.when(edge > 0)
    def _():
        for part, value in enumerate(conj_terms(i_buf, t_buf, LOW)):
            to_right[part] = jnp.where(sent_right, value, 0.0)
            to_left[part] = jnp.zeros_like(value)

    @pl.when(edge <= 0)
    def _():
        for part, value in enumerate(conj_terms(i_buf, t_buf, HIGH)):
            to_left[part] = jnp.where(sent_left, value, 0.0)
            to_right[part] = jnp.zeros_like(value)


def own_terms(i_buf, t_buf, edge):
    lane = lanes()
    low = [jnp.where(lane < edge, 0.0, value) for value in conj_terms(i_buf, t_buf, LOW)]
    high = [jnp.where(lane >= HALF + edge, 0.0, value) for value in conj_terms(i_buf, t_buf, HIGH)]
    return low, high


def terms_first(cap):
    def kernel(pos, counts, widths, probe, *rest):
        inputs, turned, pure, mixed = rest[:4], rest[4:8], rest[8:12], rest[12:16]
        adjoint, own, to_left, to_right = rest[16:20]
        buf, w_buf, a_buf, sems = rest[20:]

        def loads(j, s):
            k = (4 - j) % 4
            at = jnp.where(pos[s, 1] > RIM, HALF, 0)
            out = w_buf.at[j]
            return (
                pltpu.make_async_copy(inputs[j], buf.at[j, 0], sems.at[j, 0]),
                pltpu.make_async_copy(turned[j], buf.at[j, 1], sems.at[j, 1]),
                pltpu.make_async_copy(pure[k], out.at[:, :, aligned(at)], sems.at[j, 2]),
                pltpu.make_async_copy(mixed[k], out.at[:, :, aligned(HALF - at)], sems.at[j, 3]),
            )

        def store(j, s):
            return pltpu.make_async_copy(a_buf.at[j], adjoint.at[s], sems.at[j, 4])

        def begin(j, s):
            for copy in loads(j, s):
                copy.start()

        def work(j, s):
            for copy in loads(j, s):
                copy.wait()
            edge = pos[s, 1] - RIM

            @pl.when(lax.axis_index("cuts") == 0)
            def _():
                scale = jnp.where(s < counts[0], 1.0, 0.0)
                place_probe(probe, pos[s, 0], pos[s, 1], scale, buf.at[j, 0])

            ins, outs = buf.at[j, 0], buf.at[j, 1]
            rim_terms(ins, outs, edge, widths, to_left.at[s], to_right.at[s])
            for half, values in zip((LOW, HIGH), own_terms(ins, outs, edge)):
                for part, value in enumerate(values):
                    own[s, part, :, half] = value
            adjoint_of(outs, w_buf.at[j], pos, s, a_buf.at[j])
            store(j, s).start()

        each_owner(0, begin)
        each_owner(0, work)
        each_owner(0, lambda j, s: store(j, s).wait())

    strips = jax.ShapeDtypeStruct((4, 2, W, HALF), F32)
    return pl.pallas_call(
        kernel,
        out_shape=(
            jax.ShapeDtypeStruct((cap, 2, W, W), F32),
            jax.ShapeDtypeStruct((4, 2, W, W), F32),
            strips,
            strips,
        ),
        in_specs=[SMEM_SPEC] * 3 + [VMEM_SPEC] + [ANY_SPEC] * 16,
        out_specs=(ANY_SPEC, VMEM_SPEC, VMEM_SPEC, VMEM_SPEC),
        scratch_shapes=[
            pltpu.VMEM((4, 2, 2, W, W), F32),
            pltpu.VMEM((4, 2, W, W), F32),
            pltpu.VMEM((4, 2, W, W), F32),
            pltpu.SemaphoreType.DMA((4, 5)),
        ],
        compiler_params=params(),
        cost_estimate=cost(7),
        name="terms_first",
    )


def rims_second(count):
    def kernel(pos, counts, widths, probe, *rest):
        pairs, (to_left, to_right), (buf, sems) = rest[:4], rest[4:6], rest[6:]

        def load(j):
            return pltpu.make_async_copy(pairs[j], buf.at[j], sems.at[j])

        def work(j, s):
            load(j).wait()

            @pl.when(lax.axis_index("cuts") == 0)
            def _():
                scale = jnp.where(s < counts[0], 1.0, 0.0)
                place_probe(probe, pos[s, 0], pos[s, 1], scale, buf.at[j, 0])

            edge = pos[s, 1] - RIM
            at = s - 4
            rim_terms(buf.at[j, 0], buf.at[j, 1], edge, widths, to_left.at[at], to_right.at[at])

        each_owner(1, lambda j, s: load(j).start())
        each_owner(1, work)

    strips = jax.ShapeDtypeStruct((count, 2, W, HALF), F32)
    return pl.pallas_call(
        kernel,
        out_shape=(strips, strips),
        in_specs=[SMEM_SPEC] * 3 + [VMEM_SPEC] + [ANY_SPEC] * 4,
        out_specs=(VMEM_SPEC, VMEM_SPEC),
        scratch_shapes=[pltpu.VMEM((4, 2, 2, W, W), F32), pltpu.SemaphoreType.DMA((4,))],
        compiler_params=params(),
        cost_estimate=cost(3),
        name="rims_second",
    )


class AddInto:
    def __init__(self, grad, row, cols, buf, more_buf, sems):
        base, more, self.delta = row_base(row)
        self.buf, self.more_buf = buf, more_buf
        self.pairs = (
            (grad.at[:, pl.ds(base, W), cols], buf),
            (grad.at[:, pl.ds(more, 8), cols], more_buf),
        )
        self.sems = sems

    def copies(self, inward):
        return [
            pltpu.make_async_copy(
                pair[0 if inward else 1], pair[1 if inward else 0], self.sems.at[at]
            )
            for at, pair in enumerate(self.pairs)
        ]

    def start(self, inward):
        for copy in self.copies(inward):
            copy.start()

    def wait(self, inward):
        for copy in self.copies(inward):
            copy.wait()

    def add(self, part, half, value):
        below = rows_below(self.delta, value.shape)
        self.buf[part, :, half] += jnp.where(below, 0.0, value)
        few = rows_below(self.delta, value[:8].shape)
        self.more_buf[part, :, half] += jnp.where(few, value[:8], 0.0)


def add_rows(out, row, value, cols):
    base, more, delta = row_base(row)
    width = value[0].shape[-1]
    below = rows_below(delta, (W, width))
    few = rows_below(delta, (8, width))
    for part in range(2):
        out[part, pl.ds(base, W), cols] += jnp.where(below, 0.0, value[part])
        out[part, pl.ds(more, 8), cols] += jnp.where(few, value[part][:8], 0.0)


def finish(cap, rows):
    def kernel(pos, pos_left, pos_right, counts, probe, own, left, right, adjoint_in, *rest):
        pairs, full, (adjoint, grad) = rest[:4], rest[4:8], rest[8:10]
        buf, w_buf, a_buf, sems = rest[10:]

        def loads(j):
            return (
                pltpu.make_async_copy(pairs[j], buf.at[j], sems.at[j, 0]),
                pltpu.make_async_copy(full[(4 - j) % 4], w_buf.at[j], sems.at[j, 1]),
            )

        def store(j, s):
            return pltpu.make_async_copy(a_buf.at[j], adjoint.at[s], sems.at[j, 2])

        def begin(j, s):
            for copy in loads(j):
                copy.start()

        def work(j, s):
            for copy in loads(j):
                copy.wait()

            @pl.when(lax.axis_index("cuts") == 0)
            def _():
                scale = jnp.where(s < counts[0], 1.0, 0.0)
                place_probe(probe, pos[s, 0], pos[s, 1], scale, buf.at[j, 0])

            adjoint_of(buf.at[j, 1], w_buf.at[j], pos, s, a_buf.at[j])
            store(j, s).start()
            terms = own_terms(buf.at[j, 0], buf.at[j, 1], pos[s, 1] - RIM)
            for half, values in zip((LOW, HIGH), terms):
                add_rows(grad, pos[s, 0], values, half)

        each_owner(1, begin)
        grad[...] = jnp.zeros_like(grad)
        for s in range(4):
            add_rows(grad, pos[s, 0], own[s], slice(0, W))
            add_rows(grad, pos_left[s, 0], left[s], LOW)
            add_rows(grad, pos_right[s, 0], right[s], HIGH)
        each_owner(1, work)
        each_owner(1, lambda j, s: store(j, s).wait())

    return pl.pallas_call(
        kernel,
        out_shape=(
            jax.ShapeDtypeStruct((cap, 2, W, W), F32),
            jax.ShapeDtypeStruct((2, rows, W), F32),
        ),
        in_specs=[SMEM_SPEC] * 4 + [VMEM_SPEC] * 4 + [ANY_SPEC] * 9,
        out_specs=(ANY_SPEC, VMEM_SPEC),
        scratch_shapes=[
            pltpu.VMEM((4, 2, 2, W, W), F32),
            pltpu.VMEM((4, 2, W, W), F32),
            pltpu.VMEM((4, 2, W, W), F32),
            pltpu.SemaphoreType.DMA((4, 3)),
        ],
        input_output_aliases={8: 0},
        compiler_params=params(),
        cost_estimate=cost(9),
        name="finish",
    )


def add_rims(count, rows):
    def kernel(pos_left, pos_right, grad_in, left, right, grad, buf, more_buf, sems):
        for s in range(count):
            adders = [
                AddInto(
                    grad,
                    pos[4 + s, 0],
                    pl.ds(side * HALF, HALF),
                    buf.at[side],
                    more_buf.at[side],
                    sems.at[side],
                )
                for side, pos in enumerate((pos_left, pos_right))
            ]
            for add in adders:
                add.start(True)
            for add, values in zip(adders, (left, right)):
                add.wait(True)
                for part in range(2):
                    add.add(part, LOW, values[s, part])
                add.start(False)
            for add in adders:
                add.wait(False)

    return pl.pallas_call(
        kernel,
        out_shape=jax.ShapeDtypeStruct((2, rows, W), F32),
        in_specs=[SMEM_SPEC] * 2 + [ANY_SPEC] + [VMEM_SPEC] * 2,
        out_specs=ANY_SPEC,
        scratch_shapes=[
            pltpu.VMEM((2, 2, W, HALF), F32),
            pltpu.VMEM((2, 2, 8, HALF), F32),
            pltpu.SemaphoreType.DMA((2, 2)),
        ],
        input_output_aliases={2: 0},
        compiler_params=params(),
        cost_estimate=cost(4),
        name="add_rims",
    )


def after(value, *others):
    return lax.optimization_barrier((value, *others))[0]


def on_device(probe_wave, transmission, kernel_phase, measured, counts, positions, widths):
    groups, tiles = lax.axis_size("cuts"), lax.axis_size("tile")
    cap = positions.shape[1]
    rows = transmission.shape[2]
    image, pos = transmission[0], positions[0]
    up = [(i, i + 1) for i in range(tiles - 1)]
    down = [(i + 1, i) for i in range(tiles - 1)]

    def to_up(value):
        return lax.ppermute(value, "tile", up)

    def to_down(value):
        return lax.ppermute(value, "tile", down)

    def shift(value, by, keep):
        pairs = [
            (g * tiles + t, (g + by) % groups * tiles + t)
            for g in range(groups)
            for t in range(tiles)
            if keep(g, (g + by) % groups, t % 2)
        ]
        return lax.ppermute(value, ("cuts", "tile"), pairs)

    def shifted(values, keep):
        moved = {k: shift(values[k], k, keep) for k in (1, 3, 2)}
        return [values[0], moved[1], moved[2], moved[3]]

    every = lambda src, dst, parity: True
    to_owner = lambda src, dst, parity: dst % 2 == parity
    inner = lambda src, dst, parity: dst != 0
    owned = lambda src, dst, parity: src % 2 == parity

    order = jnp.asarray(ORDER)
    exact = lax.Precision.HIGHEST
    phase = jnp.dot(jnp.dot(order, kernel_phase, precision=exact), order.T, precision=exact)
    kern = jnp.stack([jnp.cos(phase), jnp.sin(phase)])
    tab = jnp.asarray(TABLES)
    hot, hot_t = order.astype(BF16), order.T.astype(BF16)

    pos_left, pos_right = to_up(pos), to_down(pos)
    pure1 = pure_halves()(pos, image)
    got_pure1 = shifted(pure1, every)
    edge_left, edge_right = cut_rims(cap)(pos_left, pos_right, image)
    rim_right, rim_left = to_down(edge_left), to_up(edge_right)
    rim_left = after(rim_left, kern, *got_pure1[1:])

    made = mixed_windows()(pos, widths, image, rim_left, rim_right)
    mixed1, full2 = made[:4], made[4:]
    got_mixed1 = shifted(mixed1, every)
    got_full2 = shifted([after(value, *got_mixed1[1:]) for value in full2], to_owner)

    wide = (probe_wave, measured[0], kern, tab, hot, hot_t)
    *in1, back1 = forward_first()(pos, counts, *wide, *got_pure1, *got_mixed1)
    got_in1 = shifted(in1, inner)
    back1 = after(back1, *got_full2[1:])
    turned1 = backward_first()(pos, back1, kern, tab, *got_pure1, *got_mixed1)
    got_turned1 = shifted(turned1, every)
    got_full2[0] = after(got_full2[0], turned1[1], got_in1[1])
    pairs2 = both_ways(1)(pos, counts, *wide, *got_full2)
    got_pairs2 = shifted(pairs2, owned)

    adjoint, own1, left1, right1 = terms_first(cap)(
        pos, counts, widths, probe_wave, *got_in1, *got_turned1, *pure1, *mixed1
    )
    right1, left1 = to_down(left1), to_up(right1)
    left2, right2 = rims_second(cap - 4)(pos, counts, widths, probe_wave, *got_pairs2)
    own1 = after(own1, left2)
    right2, left2 = to_down(left2), to_up(right2)
    adjoint, grad = finish(cap, rows)(
        pos, pos_left, pos_right, counts, probe_wave, own1, left1, right1, adjoint,
        *got_pairs2, *full2
    )
    grad = add_rims(cap - 4, rows)(pos_left, pos_right, grad, left2, right2)
    return adjoint[None, None], grad[None]


def solution(mesh):
    return jax.shard_map(
        on_device,
        mesh=mesh,
        in_specs=(
            P(),
            P("cuts", None, None, "tile"),
            P(),
            P("tile", None, None, None),
            P("tile"),
            P("tile", None, None),
            P("tile", None),
        ),
        out_specs=(P("cuts", "tile", None, None, None, None), P("cuts", None, None, "tile")),
        check_vma=False,
    )
```

time: 212 us -> 192 us (0.906)
  the two profiles are of different devices: /device:TPU:57 before, /device:TPU:1 now
where the time goes in v2:
time: 192 us; the launch traced here: 191 us
  starting transfers between devices  62.2 us (32%)
  Pallas kernels  60 us (31%)
  waiting for transfers between devices  56.2 us (29%)
  local copies, waits for them, and re-layouts  7.51 us (4%)
  matrix products  2.07 us (1%)
  between operations  2 us (1%)
    ppermute x18, waiting for transfers between devices, shift(): return lax.ppermute(value, ('cuts', 'tile'), pairs)  54.2 us
    ppermute x18, starting transfers between devices, shift(): return lax.ppermute(value, ('cuts', 'tile'), pairs)  34.1 us
    ppermute x4, starting transfers between devices, to_up(): return lax.ppermute(value, 'tile', up)  18.9 us
    pallas_call x1, Pallas kernels, on_device(): *in1, back1 = forward_first()(pos, counts, *wide, *got_pure1, *got_mixed1)  10.6 us
    pallas_call x1, Pallas kernels, on_device(): finish(cap, rows)  9.78 us
    pallas_call x1, Pallas kernels, on_device(): turned1 = backward_first()(pos, back1, kern, tab, *got_pure1, *got_mixed1)  9.5 us
    ppermute x4, starting transfers between devices, to_down(): return lax.ppermute(value, 'tile', down)  9.21 us
    pallas_call x1, Pallas kernels, on_device(): terms_first(cap)  8.7 us
  transfers between devices with their start and end apart: 26, of which 9 were waited for; matrix products, arithmetic and copies ran while one was open for 2% of the time, Pallas kernels for 25%

profile of v2, /device:TPU:1, one launch (start us, length us, event | category | flops | bytes accessed | tf_op | source)
XLA Modules:
  0.0 190.9 jit_solution(14353094363497170269)
XLA Ops:
  1.5 3.3 %collective-permute-start.1 = (s32[6,2]{1,0:T(8,128)S(1)}, s32[6,2]{1,0:T(8,128)S(1)}, u32[]{:S(2)}, u32[]{:S(2)}) collective-permute-start(s32[6,2]{1,0:T(8,128)S(1)} %copy.22.pos), channel_id=1, source_target_pairs={{1,0},{2,1},{3,2},{4,3},{5,4},{6,5},{7,6},{8,7},{9,8},{10,9},{11,1... | collective-permute-start | bytes 152 | tf_op jit(solution)/shard_map/ppermute | solution.py:899
  4.8 3.2 %collective-permute-start = (s32[6,2]{1,0:T(8,128)S(1)}, s32[6,2]{1,0:T(8,128)S(1)}, u32[]{:S(2)}, u32[]{:S(2)}) collective-permute-start(s32[6,2]{1,0:T(8,128)S(1)} %copy.22.pos), channel_id=1, source_target_pairs={{0,1},{1,2},{2,3},{3,4},{4,5},{5,6},{6,7},{7,8},{8,9},{9,10},{10,1... | collective-permute-start | bytes 152 | tf_op jit(solution)/shard_map/ppermute | solution.py:896
  9.3 4.1 %cut_rims.1 = (f32[6,2,256,128]{3,2,1,0:T(8,128)}, f32[6,2,256,128]{3,2,1,0:T(8,128)}) custom-call(s32[6,2]{1,0:T(8,128)} %copy-done.28, s32[6,2]{1,0:T(8,128)} %copy-done.27, f32[2,4096,256]{2,1,0:T(8,128)} %bitcast.13), custom_call_target="tpu_custom_call" | custom-call | bytes 13200000 | tf_op jit(solution)/shard_map/cut_rims/pallas_call | solution.py:929
  13.4 4.2 %collective-permute-start.5 = (f32[6,2,256,128]{3,2,1,0:T(8,128)}, f32[6,2,256,128]{3,2,1,0:T(8,128)S(1)}, u32[]{:S(2)}, u32[]{:S(2)}) collective-permute-start(f32[6,2,256,128]{3,2,1,0:T(8,128)} %get-tuple-element.49), channel_id=1, source_target_pairs={{0,1},{1,2},{2,3},{3,4},{4,5},{5,6},{6,7},{7,8},{8,9},{9,10},{10,1... | collective-permute-start | bytes 4718600 | tf_op jit(solution)/shard_map/ppermute | solution.py:896
  17.6 2.1 %collective-permute-start.6 = (f32[6,2,256,128]{3,2,1,0:T(8,128)}, f32[6,2,256,128]{3,2,1,0:T(8,128)S(1)}, u32[]{:S(2)}, u32[]{:S(2)}) collective-permute-start(f32[6,2,256,128]{3,2,1,0:T(8,128)} %get-tuple-element.51), channel_id=1, source_target_pairs={{1,0},{2,1},{3,2},{4,3},{5,4},{6,5},{7,6},{8,7},{9,8},{10,9},{11,1... | collective-permute-start | bytes 4718600 | tf_op jit(solution)/shard_map/ppermute | solution.py:899
  19.7 3.1 %pure_halves.1 = (f32[2,256,128]{2,1,0:T(8,128)}, f32[2,256,128]{2,1,0:T(8,128)}, f32[2,256,128]{2,1,0:T(8,128)}, f32[2,256,128]{2,1,0:T(8,128)}) custom-call(s32[6,2]{1,0:T(8,128)} %copy-done.26, f32[2,4096,256]{2,1,0:T(8,128)} %bitcast.14), custom_call_target="tpu_custom_call" | custom-call | bytes 9900000 | tf_op jit(solution)/shard_map/pure_halves/pallas_call | solution.py:927
  22.8 1.7 collective-permute-start.2
  24.5 3.3 %collective-permute-start.3 = (f32[2,256,128]{2,1,0:T(8,128)}, f32[2,256,128]{2,1,0:T(8,128)S(1)}, u32[]{:S(2)}, u32[]{:S(2)}) collective-permute-start(f32[2,256,128]{2,1,0:T(8,128)} %get-tuple-element.47.rest_10_), channel_id=1, source_target_pairs={{0,64},{1,65},{2,66},{3,67},{4,68},{5,69},{6,70},{7,71},{8,72},{9,... | collective-permute-start | bytes 786440 | tf_op jit(solution)/shard_map/ppermute | solution.py:908
  28.9 1.7 cosine_bitcast_fusion
  32.0 6.3 %collective-permute-done.3.rest_2_ = f32[2,256,128]{2,1,0:T(8,128)S(1)} collective-permute-done((f32[2,256,128]{2,1,0:T(8,128)}, f32[2,256,128]{2,1,0:T(8,128)S(1)}, u32[]{:S(2)}, u32[]{:S(2)}) %collective-permute-start.3) | collective-permute-done | bytes 262176 | tf_op jit(solution)/shard_map/ppermute | solution.py:908
  40.8 4.1 %mixed_windows.1 = (f32[2,256,128]{2,1,0:T(8,128)}, f32[2,256,128]{2,1,0:T(8,128)}, f32[2,256,128]{2,1,0:T(8,128)}, f32[2,256,128]{2,1,0:T(8,128)}, f32[2,256,25...) custom-call(s32[6,2]{1,0:T(8,128)} %copy-done.26, s32[1,2]{1,0:T(1,128)} %widths.5, ...), custom_call_target="tpu_custom_call" | custom-call | bytes 16500000 | tf_op jit(solution)/shard_map/mixed_windows/pallas_call | solution.py:933
  44.9 1.7 collective-permute-start.7
  46.6 3.3 %collective-permute-start.8 = (f32[2,256,128]{2,1,0:T(8,128)}, f32[2,256,128]{2,1,0:T(8,128)S(1)}, u32[]{:S(2)}, u32[]{:S(2)}) collective-permute-start(f32[2,256,128]{2,1,0:T(8,128)} %get-tuple-element.54.rest_14_), channel_id=1, source_target_pairs={{0,64},{1,65},{2,66},{3,67},{4,68},{5,69},{6,70},{7,71},{8,72},{9,... | collective-permute-start | bytes 786440 | tf_op jit(solution)/shard_map/ppermute | solution.py:908
  50.6 3.6 %collective-permute-done.7.rest_5_ = f32[2,256,128]{2,1,0:T(8,128)S(1)} collective-permute-done((f32[2,256,128]{2,1,0:T(8,128)}, f32[2,256,128]{2,1,0:T(8,128)S(1)}, u32[]{:S(2)}, u32[]{:S(2)}) %collective-permute-start.7) | collective-permute-done | bytes 262176 | tf_op jit(solution)/shard_map/ppermute | solution.py:908
  54.3 7.1 %collective-permute-done.8.rest_6_ = f32[2,256,128]{2,1,0:T(8,128)S(1)} collective-permute-done((f32[2,256,128]{2,1,0:T(8,128)}, f32[2,256,128]{2,1,0:T(8,128)S(1)}, u32[]{:S(2)}, u32[]{:S(2)}) %collective-permute-start.8) | collective-permute-done | bytes 262176 | tf_op jit(solution)/shard_map/ppermute | solution.py:908
  61.3 3.0 %collective-permute-start.13 = (f32[2,256,256]{2,1,0:T(8,128)}, f32[2,256,256]{2,1,0:T(8,128)S(1)}, u32[]{:S(2)}, u32[]{:S(2)}) collective-permute-start(f32[2,256,256]{2,1,0:T(8,128)} %get-tuple-element.62.rest_5_), channel_id=1, source_target_pairs={{1,33},{3,35},{5,37},{7,39},{9,41},{11,43},{13,45},{15,47},{17,49}... | collective-permute-start | bytes 1572872 | tf_op jit(solution)/shard_map/ppermute | solution.py:908
  65.0 4.9 %collective-permute-start.15 = (f32[2,256,256]{2,1,0:T(8,128)}, f32[2,256,256]{2,1,0:T(8,128)S(1)}, u32[]{:S(2)}, u32[]{:S(2)}) collective-permute-start(f32[2,256,256]{2,1,0:T(8,128)} %get-tuple-element.66.rest_7_), channel_id=1, source_target_pairs={{1,97},{3,99},{5,101},{7,103},{9,105},{11,107},{13,109},{15,111},{... | collective-permute-start | bytes 1572872 | tf_op jit(solution)/shard_map/ppermute | solution.py:908
  70.6 10.6 %forward_first.1 = (f32[2,256,256]{2,1,0:T(8,128)}, f32[2,256,256]{2,1,0:T(8,128)}, f32[2,256,256]{2,1,0:T(8,128)}, f32[2,256,256]{2,1,0:T(8,128)}, f32[2,256,256]{2,1,0:T(8,128)}) custom-call(s32[6,2]{1,0:T(8,128)} %copy-done.26, s32[1]{0:T(128)S(6)} %copy.25.counts, f32[2,256,256]{2,1,0:T(8,128)} %probe.9, bf16[6,256,256]{2,1,0:T(8,128)(2,1)} %bitcast.17, ...), custom_call_target="tpu_custom_call" | custom-call | bytes 29700000 | tf_op jit(solution)/shard_map/forward_first/pallas_call | solution.py:939
  82.6 3.9 %collective-permute-start.11 = (f32[2,256,256]{2,1,0:T(8,128)}, f32[2,256,256]{2,1,0:T(8,128)S(1)}, u32[]{:S(2)}, u32[]{:S(2)}) collective-permute-start(f32[2,256,256]{2,1,0:T(8,128)} %get-tuple-element.58), channel_id=1, source_target_pairs={{0,64},{1,65},{2,66},{3,67},{4,68},{5,69},{6,70},{7,71},{8,72},{9,... | collective-permute-start | bytes 1572872 | tf_op jit(solution)/shard_map/ppermute | solution.py:908
  86.5 4.0 %collective-permute-start.12 = (f32[2,256,256]{2,1,0:T(8,128)}, f32[2,256,256]{2,1,0:T(8,128)S(1)}, u32[]{:S(2)}, u32[]{:S(2)}) collective-permute-start(f32[2,256,256]{2,1,0:T(8,128)} %get-tuple-element.59), channel_id=1, source_target_pairs={{0,96},{1,97},{2,98},{3,99},{4,100},{5,101},{6,102},{7,103},{8,104... | collective-permute-start | bytes 1572872 | tf_op jit(solution)/shard_map/ppermute | solution.py:908
  90.5 9.5 %backward_first.1 = (f32[2,256,256]{2,1,0:T(8,128)}, f32[2,256,256]{2,1,0:T(8,128)}, f32[2,256,256]{2,1,0:T(8,128)}, f32[2,256,256]{2,1,0:T(8,128)}) custom-call(s32[6,2]{1,0:T(8,128)} %copy-done.26, f32[2,256,256]{2,1,0:T(8,128)} %get-tuple-element.67.back, f32[2,256,256]{2,1,0:T(8,128)} %pad_maximum_fusion.kern, bf16[8,256,256]{2,1,0:T(8,128)(2,1)} %constant.5.clone.tab, ...), custom_call_target="tpu_custom_call" | custom-call | bytes 23100000 | tf_op jit(solution)/shard_map/backward_first/pallas_call | solution.py:942
  102.8 1.8 collective-permute-done.11.rest_2_
  105.9 14.4 %collective-permute-done.12.rest_3_ = f32[2,256,256]{2,1,0:T(8,128)S(1)} collective-permute-done((f32[2,256,256]{2,1,0:T(8,128)}, f32[2,256,256]{2,1,0:T(8,128)S(1)}, u32[]{:S(2)}, u32[]{:S(2)}) %collective-permute-start.12) | collective-permute-done | bytes 524320 | tf_op jit(solution)/shard_map/ppermute | solution.py:908
  122.4 20.4 %collective-permute-done.18.rest_7_ = f32[2,256,256]{2,1,0:T(8,128)S(1)} collective-permute-done((f32[2,256,256]{2,1,0:T(8,128)}, f32[2,256,256]{2,1,0:T(8,128)S(1)}, u32[]{:S(2)}, u32[]{:S(2)}) %collective-permute-start.18) | collective-permute-done | bytes 524320 | tf_op jit(solution)/shard_map/ppermute | solution.py:908
  143.8 8.7 %terms_first.1 = (f32[6,2,256,256]{3,2,1,0:T(8,128)}, f32[4,2,256,256]{3,2,1,0:T(8,128)}, f32[4,2,256,128]{3,2,1,0:T(8,128)}, f32[4,2,256,128]{3,2,1,0:T(8,128)}) custom-call(s32[6,2]{1,0:T(8,128)} %copy-done.26, s32[1]{0:T(128)S(6)} %copy.25.counts, s32[1,2]{1,0:T(1,128)} %widths.5, f32[2,256,256]{2,1,0:T(8,128)} %probe.9, ...), custom_call_target="tpu_custom_call" | custom-call | bytes 23100000 | tf_op jit(solution)/shard_map/terms_first/pallas_call | solution.py:948
  152.5 2.7 %collective-permute-start.22 = (f32[4,2,256,128]{3,2,1,0:T(8,128)}, f32[4,2,256,128]{3,2,1,0:T(8,128)S(1)}, u32[]{:S(2)}, u32[]{:S(2)}) collective-permute-start(f32[4,2,256,128]{3,2,1,0:T(8,128)} %get-tuple-element.82), channel_id=1, source_target_pairs={{0,1},{1,2},{2,3},{3,4},{4,5},{5,6},{6,7},{7,8},{8,9},{9,10},{10,1... | collective-permute-start | bytes 3145736 | tf_op jit(solution)/shard_map/ppermute | solution.py:896
  155.2 1.9 %collective-permute-start.23 = (f32[4,2,256,128]{3,2,1,0:T(8,128)}, f32[4,2,256,128]{3,2,1,0:T(8,128)S(1)}, u32[]{:S(2)}, u32[]{:S(2)}) collective-permute-start(f32[4,2,256,128]{3,2,1,0:T(8,128)} %get-tuple-element.83), channel_id=1, source_target_pairs={{1,0},{2,1},{3,2},{4,3},{5,4},{6,5},{7,6},{8,7},{9,8},{10,9},{11,1... | collective-permute-start | bytes 3145736 | tf_op jit(solution)/shard_map/ppermute | solution.py:899
  158.8 4.1 %rims_second.1 = (f32[2,2,256,128]{3,2,1,0:T(8,128)}, f32[2,2,256,128]{3,2,1,0:T(8,128)}) custom-call(s32[6,2]{1,0:T(8,128)} %copy-done.26, s32[1]{0:T(128)S(6)} %copy.25.counts, s32[1,2]{1,0:T(1,128)} %widths.5, f32[2,256,256]{2,1,0:T(8,128)} %probe.9, f32[2,2,256,256]{3,2,1,0:T(8,128)} %get-tuple-element.76.rest_0_, f32[2,2,256,256]{3,2,1,0:T(8,128)} %copy-done.1, ...), custom_call_target="tpu_custom_call" | custom-call | bytes 9900000 | tf_op jit(solution)/shard_map/rims_second/pallas_call | solution.py:952
  162.9 8.8 %collective-permute-start.24 = (f32[2,2,256,128]{3,2,1,0:T(8,128)}, f32[2,2,256,128]{3,2,1,0:T(8,128)S(1)}, u32[]{:S(2)}, u32[]{:S(2)}) collective-permute-start(f32[2,2,256,128]{3,2,1,0:T(8,128)} %get-tuple-element.87), channel_id=1, source_target_pairs={{0,1},{1,2},{2,3},{3,4},{4,5},{5,6},{6,7},{7,8},{8,9},{9,10},{10,1... | collective-permute-start | bytes 1572872 | tf_op jit(solution)/shard_map/ppermute | solution.py:896
  171.7 1.9 %collective-permute-start.25 = (f32[2,2,256,128]{3,2,1,0:T(8,128)}, f32[2,2,256,128]{3,2,1,0:T(8,128)S(1)}, u32[]{:S(2)}, u32[]{:S(2)}) collective-permute-start(f32[2,2,256,128]{3,2,1,0:T(8,128)} %get-tuple-element.80), channel_id=1, source_target_pairs={{1,0},{2,1},{3,2},{4,3},{5,4},{6,5},{7,6},{8,7},{9,8},{10,9},{11,1... | collective-permute-start | bytes 1572872 | tf_op jit(solution)/shard_map/ppermute | solution.py:899
  175.1 9.8 %finish.1 = (f32[6,2,256,256]{3,2,1,0:T(8,128)}, f32[2,4096,256]{2,1,0:T(8,128)}) custom-call(s32[6,2]{1,0:T(8,128)} %copy-done.26, s32[6,2]{1,0:T(8,128)} %copy-done.28, s32[6,2]{1,0:T(8,128)} %copy-done.27, s32[1]{0:T(128)S(6)} %copy.25.counts, f32[2,256,256]{2,1,0:T(8,128)} %probe.9, ...), custom_call_target="tpu_custom_call", output_to_operand_aliasing={{0}: (8, {})} | custom-call | bytes 29700000 | tf_op jit(solution)/shard_map/finish/pallas_call | solution.py:955
  185.9 4.8 %add_rims.1 = f32[2,4096,256]{2,1,0:T(8,128)} custom-call(s32[6,2]{1,0:T(8,128)} %copy-done.28, s32[6,2]{1,0:T(8,128)} %copy-done.27, f32[2,4096,256]{2,1,0:T(8,128)} %get-tuple-element.86.grad_in, f32[2,2,256,128]{3,2,1,0:T(8,128)} %copy-done.24, f32[2,2,256,128]{3,2,1,0:T(8,128)} %copy-done.25), custom_call_target="tpu_custom_call", output_to_operand_aliasing={{}: (2, {})} | custom-call | bytes 13200000 | tf_op jit(solution)/shard_map/add_rims/pallas_call | solution.py:959
  (92 shorter events, 20.8 us)
Async XLA Ops:
  0.6 27.9 %copy-start = (f32[256,256]{1,0:T(8,128)S(1)}, f32[256,256]{1,0:T(8,128)}, u32[]{:S(2)}) copy-start(f32[256,256]{1,0:T(8,128)} %param.11) | copy-start | bytes 786436
  1.5 6.5 %collective-permute-start.1 = (s32[6,2]{1,0:T(8,128)S(1)}, s32[6,2]{1,0:T(8,128)S(1)}, u32[]{:S(2)}, u32[]{:S(2)}) collective-permute-start(s32[6,2]{1,0:T(8,128)S(1)} %copy.22.pos), channel_id=1, source_target_pairs={{1,0},{2,1},{3,2},{4,3},{5,4},{6,5},{7,6},{8,7},{9,8},{10,9},{11,1... | collective-permute-start | bytes 152 | tf_op jit(solution)/shard_map/ppermute | solution.py:899
  4.8 3.9 %collective-permute-start = (s32[6,2]{1,0:T(8,128)S(1)}, s32[6,2]{1,0:T(8,128)S(1)}, u32[]{:S(2)}, u32[]{:S(2)}) collective-permute-start(s32[6,2]{1,0:T(8,128)S(1)} %copy.22.pos), channel_id=1, source_target_pairs={{0,1},{1,2},{2,3},{3,4},{4,5},{5,6},{6,7},{7,8},{8,9},{9,10},{10,1... | collective-permute-start | bytes 152 | tf_op jit(solution)/shard_map/ppermute | solution.py:896
  13.4 25.0 %collective-permute-start.5 = (f32[6,2,256,128]{3,2,1,0:T(8,128)}, f32[6,2,256,128]{3,2,1,0:T(8,128)S(1)}, u32[]{:S(2)}, u32[]{:S(2)}) collective-permute-start(f32[6,2,256,128]{3,2,1,0:T(8,128)} %get-tuple-element.49), channel_id=1, source_target_pairs={{0,1},{1,2},{2,3},{3,4},{4,5},{5,6},{6,7},{7,8},{8,9},{9,10},{10,1... | collective-permute-start | bytes 4718600 | tf_op jit(solution)/shard_map/ppermute | solution.py:896
  17.6 22.1 %collective-permute-start.6 = (f32[6,2,256,128]{3,2,1,0:T(8,128)}, f32[6,2,256,128]{3,2,1,0:T(8,128)S(1)}, u32[]{:S(2)}, u32[]{:S(2)}) collective-permute-start(f32[6,2,256,128]{3,2,1,0:T(8,128)} %get-tuple-element.51), channel_id=1, source_target_pairs={{1,0},{2,1},{3,2},{4,3},{5,4},{6,5},{7,6},{8,7},{9,8},{10,9},{11,1... | collective-permute-start | bytes 4718600 | tf_op jit(solution)/shard_map/ppermute | solution.py:899
  22.8 9.2 %collective-permute-start.2 = (f32[2,256,128]{2,1,0:T(8,128)}, f32[2,256,128]{2,1,0:T(8,128)S(1)}, u32[]{:S(2)}, u32[]{:S(2)}) collective-permute-start(f32[2,256,128]{2,1,0:T(8,128)} %get-tuple-element.46.rest_9_), channel_id=1, source_target_pairs={{0,32},{1,33},{2,34},{3,35},{4,36},{5,37},{6,38},{7,39},{8,40},{9,... | collective-permute-start | bytes 786440 | tf_op jit(solution)/shard_map/ppermute | solution.py:908
  24.5 13.9 %collective-permute-start.3 = (f32[2,256,128]{2,1,0:T(8,128)}, f32[2,256,128]{2,1,0:T(8,128)S(1)}, u32[]{:S(2)}, u32[]{:S(2)}) collective-permute-start(f32[2,256,128]{2,1,0:T(8,128)} %get-tuple-element.47.rest_10_), channel_id=1, source_target_pairs={{0,64},{1,65},{2,66},{3,67},{4,68},{5,69},{6,70},{7,71},{8,72},{9,... | collective-permute-start | bytes 786440 | tf_op jit(solution)/shard_map/ppermute | solution.py:908
  27.8 10.6 %collective-permute-start.4 = (f32[2,256,128]{2,1,0:T(8,128)}, f32[2,256,128]{2,1,0:T(8,128)S(1)}, u32[]{:S(2)}, u32[]{:S(2)}) collective-permute-start(f32[2,256,128]{2,1,0:T(8,128)} %get-tuple-element.48.rest_11_), channel_id=1, source_target_pairs={{0,96},{1,97},{2,98},{3,99},{4,100},{5,101},{6,102},{7,103},{8,104... | collective-permute-start | bytes 786440 | tf_op jit(solution)/shard_map/ppermute | solution.py:908
  32.0 38.5 %copy-start.8 = (f32[2,256,128]{2,1,0:T(8,128)}, f32[2,256,128]{2,1,0:T(8,128)S(1)}, u32[]{:S(2)}) copy-start(f32[2,256,128]{2,1,0:T(8,128)S(1)} %collective-permute-done.2.rest_1_) | copy-start | bytes 786436
  38.4 32.2 %copy-start.9 = (f32[2,256,128]{2,1,0:T(8,128)}, f32[2,256,128]{2,1,0:T(8,128)S(1)}, u32[]{:S(2)}) copy-start(f32[2,256,128]{2,1,0:T(8,128)S(1)} %collective-permute-done.3.rest_2_) | copy-start | bytes 786436
  38.4 32.2 %copy-start.10 = (f32[2,256,128]{2,1,0:T(8,128)}, f32[2,256,128]{2,1,0:T(8,128)S(1)}, u32[]{:S(2)}) copy-start(f32[2,256,128]{2,1,0:T(8,128)S(1)} %collective-permute-done.4.rest_3_) | copy-start | bytes 786436
  44.9 9.3 %collective-permute-start.7 = (f32[2,256,128]{2,1,0:T(8,128)}, f32[2,256,128]{2,1,0:T(8,128)S(1)}, u32[]{:S(2)}, u32[]{:S(2)}) collective-permute-start(f32[2,256,128]{2,1,0:T(8,128)} %get-tuple-element.53.rest_13_), channel_id=1, source_target_pairs={{0,32},{1,33},{2,34},{3,35},{4,36},{5,37},{6,38},{7,39},{8,40},{9,... | collective-permute-start | bytes 786440 | tf_op jit(solution)/shard_map/ppermute | solution.py:908
  46.6 14.7 %collective-permute-start.8 = (f32[2,256,128]{2,1,0:T(8,128)}, f32[2,256,128]{2,1,0:T(8,128)S(1)}, u32[]{:S(2)}, u32[]{:S(2)}) collective-permute-start(f32[2,256,128]{2,1,0:T(8,128)} %get-tuple-element.54.rest_14_), channel_id=1, source_target_pairs={{0,64},{1,65},{2,66},{3,67},{4,68},{5,69},{6,70},{7,71},{8,72},{9,... | collective-permute-start | bytes 786440 | tf_op jit(solution)/shard_map/ppermute | solution.py:908
  49.9 11.4 %collective-permute-start.9 = (f32[2,256,128]{2,1,0:T(8,128)}, f32[2,256,128]{2,1,0:T(8,128)S(1)}, u32[]{:S(2)}, u32[]{:S(2)}) collective-permute-start(f32[2,256,128]{2,1,0:T(8,128)} %get-tuple-element.55.rest_15_), channel_id=1, source_target_pairs={{0,96},{1,97},{2,98},{3,99},{4,100},{5,101},{6,102},{7,103},{8,104... | collective-permute-start | bytes 786440 | tf_op jit(solution)/shard_map/ppermute | solution.py:908
  61.3 25.2 %collective-permute-start.13 = (f32[2,256,256]{2,1,0:T(8,128)}, f32[2,256,256]{2,1,0:T(8,128)S(1)}, u32[]{:S(2)}, u32[]{:S(2)}) collective-permute-start(f32[2,256,256]{2,1,0:T(8,128)} %get-tuple-element.62.rest_5_), channel_id=1, source_target_pairs={{1,33},{3,35},{5,37},{7,39},{9,41},{11,43},{13,45},{15,47},{17,49}... | collective-permute-start | bytes 1572872 | tf_op jit(solution)/shard_map/ppermute | solution.py:908
  64.3 26.2 %collective-permute-start.14 = (f32[2,256,256]{2,1,0:T(8,128)}, f32[2,256,256]{2,1,0:T(8,128)S(1)}, u32[]{:S(2)}, u32[]{:S(2)}) collective-permute-start(f32[2,256,256]{2,1,0:T(8,128)} %get-tuple-element.64.rest_6_), channel_id=1, source_target_pairs={{0,64},{2,66},{4,68},{6,70},{8,72},{10,74},{12,76},{14,78},{16,80}... | collective-permute-start | bytes 1572872 | tf_op jit(solution)/shard_map/ppermute | solution.py:908
  65.0 25.5 %collective-permute-start.15 = (f32[2,256,256]{2,1,0:T(8,128)}, f32[2,256,256]{2,1,0:T(8,128)S(1)}, u32[]{:S(2)}, u32[]{:S(2)}) collective-permute-start(f32[2,256,256]{2,1,0:T(8,128)} %get-tuple-element.66.rest_7_), channel_id=1, source_target_pairs={{1,97},{3,99},{5,101},{7,103},{9,105},{11,107},{13,109},{15,111},{... | collective-permute-start | bytes 1572872 | tf_op jit(solution)/shard_map/ppermute | solution.py:908
  81.3 19.0 %collective-permute-start.10 = (f32[2,256,256]{2,1,0:T(8,128)}, f32[2,256,256]{2,1,0:T(8,128)S(1)}, u32[]{:S(2)}, u32[]{:S(2)}) collective-permute-start(f32[2,256,256]{2,1,0:T(8,128)} %get-tuple-element.57), channel_id=1, source_target_pairs={{0,32},{1,33},{2,34},{3,35},{4,36},{5,37},{6,38},{7,39},{8,40},{9,... | collective-permute-start | bytes 1572872 | tf_op jit(solution)/shard_map/ppermute | solution.py:908
  82.6 22.1 %collective-permute-start.11 = (f32[2,256,256]{2,1,0:T(8,128)}, f32[2,256,256]{2,1,0:T(8,128)S(1)}, u32[]{:S(2)}, u32[]{:S(2)}) collective-permute-start(f32[2,256,256]{2,1,0:T(8,128)} %get-tuple-element.58), channel_id=1, source_target_pairs={{0,64},{1,65},{2,66},{3,67},{4,68},{5,69},{6,70},{7,71},{8,72},{9,... | collective-permute-start | bytes 1572872 | tf_op jit(solution)/shard_map/ppermute | solution.py:908
  86.5 33.9 %collective-permute-start.12 = (f32[2,256,256]{2,1,0:T(8,128)}, f32[2,256,256]{2,1,0:T(8,128)S(1)}, u32[]{:S(2)}, u32[]{:S(2)}) collective-permute-start(f32[2,256,256]{2,1,0:T(8,128)} %get-tuple-element.59), channel_id=1, source_target_pairs={{0,96},{1,97},{2,98},{3,99},{4,100},{5,101},{6,102},{7,103},{8,104... | collective-permute-start | bytes 1572872 | tf_op jit(solution)/shard_map/ppermute | solution.py:908
  100.0 21.1 %collective-permute-start.17 = (f32[2,256,256]{2,1,0:T(8,128)}, f32[2,256,256]{2,1,0:T(8,128)S(1)}, u32[]{:S(2)}, u32[]{:S(2)}) collective-permute-start(f32[2,256,256]{2,1,0:T(8,128)} %get-tuple-element.70), channel_id=1, source_target_pairs={{0,64},{1,65},{2,66},{3,67},{4,68},{5,69},{6,70},{7,71},{8,72},{9,... | collective-permute-start | bytes 1572872 | tf_op jit(solution)/shard_map/ppermute | solution.py:908
  100.1 42.7 %collective-permute-start.18 = (f32[2,256,256]{2,1,0:T(8,128)}, f32[2,256,256]{2,1,0:T(8,128)S(1)}, u32[]{:S(2)}, u32[]{:S(2)}) collective-permute-start(f32[2,256,256]{2,1,0:T(8,128)} %get-tuple-element.71), channel_id=1, source_target_pairs={{0,96},{1,97},{2,98},{3,99},{4,100},{5,101},{6,102},{7,103},{8,104... | collective-permute-start | bytes 1572872 | tf_op jit(solution)/shard_map/ppermute | solution.py:908
  100.2 42.6 %copy-start.15 = (f32[2,256,256]{2,1,0:T(8,128)}, f32[2,256,256]{2,1,0:T(8,128)S(1)}, u32[]{:S(2)}) copy-start(f32[2,256,256]{2,1,0:T(8,128)S(1)} %collective-permute-done.10.rest_1_) | copy-start | bytes 1572868
  100.2 42.6 %collective-permute-start.16 = (f32[2,256,256]{2,1,0:T(8,128)}, f32[2,256,256]{2,1,0:T(8,128)S(1)}, u32[]{:S(2)}, u32[]{:S(2)}) collective-permute-start(f32[2,256,256]{2,1,0:T(8,128)} %get-tuple-element.69), channel_id=1, source_target_pairs={{0,32},{1,33},{2,34},{3,35},{4,36},{5,37},{6,38},{7,39},{8,40},{9,... | collective-permute-start | bytes 1572872 | tf_op jit(solution)/shard_map/ppermute | solution.py:908
  104.6 38.2 %copy-start.16 = (f32[2,256,256]{2,1,0:T(8,128)}, f32[2,256,256]{2,1,0:T(8,128)S(1)}, u32[]{:S(2)}) copy-start(f32[2,256,256]{2,1,0:T(8,128)S(1)} %collective-permute-done.11.rest_2_) | copy-start | bytes 1572868
  104.6 52.5 %collective-permute-start.19 = (f32[2,2,256,256]{3,2,1,0:T(8,128)}, f32[2,2,256,256]{3,2,1,0:T(8,128)S(1)}, u32[]{:S(2)}, u32[]{:S(2)}) collective-permute-start(f32[2,2,256,256]{3,2,1,0:T(8,128)} %get-tuple-element.77), channel_id=1, source_target_pairs={{0,32},{2,34},{4,36},{6,38},{8,40},{10,42},{12,44},{14,46},{16,48}... | collective-permute-start | bytes 3145736 | tf_op jit(solution)/shard_map/ppermute | solution.py:908
  120.4 36.8 %collective-permute-start.20 = (f32[2,2,256,256]{3,2,1,0:T(8,128)}, f32[2,2,256,256]{3,2,1,0:T(8,128)S(1)}, u32[]{:S(2)}, u32[]{:S(2)}) collective-permute-start(f32[2,2,256,256]{3,2,1,0:T(8,128)} %get-tuple-element.78), channel_id=1, source_target_pairs={{0,64},{2,66},{4,68},{6,70},{8,72},{10,74},{12,76},{14,78},{16,80}... | collective-permute-start | bytes 3145736 | tf_op jit(solution)/shard_map/ppermute | solution.py:908
  121.1 36.1 %collective-permute-start.21 = (f32[2,2,256,256]{3,2,1,0:T(8,128)}, f32[2,2,256,256]{3,2,1,0:T(8,128)S(1)}, u32[]{:S(2)}, u32[]{:S(2)}) collective-permute-start(f32[2,2,256,256]{3,2,1,0:T(8,128)} %get-tuple-element.79), channel_id=1, source_target_pairs={{0,96},{2,98},{4,100},{6,102},{8,104},{10,106},{12,108},{14,110},{... | collective-permute-start | bytes 3145736 | tf_op jit(solution)/shard_map/ppermute | solution.py:908
  152.5 21.2 %collective-permute-start.22 = (f32[4,2,256,128]{3,2,1,0:T(8,128)}, f32[4,2,256,128]{3,2,1,0:T(8,128)S(1)}, u32[]{:S(2)}, u32[]{:S(2)}) collective-permute-start(f32[4,2,256,128]{3,2,1,0:T(8,128)} %get-tuple-element.82), channel_id=1, source_target_pairs={{0,1},{1,2},{2,3},{3,4},{4,5},{5,6},{6,7},{7,8},{8,9},{9,10},{10,1... | collective-permute-start | bytes 3145736 | tf_op jit(solution)/shard_map/ppermute | solution.py:896
  155.2 18.5 %collective-permute-start.23 = (f32[4,2,256,128]{3,2,1,0:T(8,128)}, f32[4,2,256,128]{3,2,1,0:T(8,128)S(1)}, u32[]{:S(2)}, u32[]{:S(2)}) collective-permute-start(f32[4,2,256,128]{3,2,1,0:T(8,128)} %get-tuple-element.83), channel_id=1, source_target_pairs={{1,0},{2,1},{3,2},{4,3},{5,4},{6,5},{7,6},{8,7},{9,8},{10,9},{11,1... | collective-permute-start | bytes 3145736 | tf_op jit(solution)/shard_map/ppermute | solution.py:899
  162.9 22.0 %collective-permute-start.24 = (f32[2,2,256,128]{3,2,1,0:T(8,128)}, f32[2,2,256,128]{3,2,1,0:T(8,128)S(1)}, u32[]{:S(2)}, u32[]{:S(2)}) collective-permute-start(f32[2,2,256,128]{3,2,1,0:T(8,128)} %get-tuple-element.87), channel_id=1, source_target_pairs={{0,1},{1,2},{2,3},{3,4},{4,5},{5,6},{6,7},{7,8},{8,9},{9,10},{10,1... | collective-permute-start | bytes 1572872 | tf_op jit(solution)/shard_map/ppermute | solution.py:896
  171.7 13.1 %collective-permute-start.25 = (f32[2,2,256,128]{3,2,1,0:T(8,128)}, f32[2,2,256,128]{3,2,1,0:T(8,128)S(1)}, u32[]{:S(2)}, u32[]{:S(2)}) collective-permute-start(f32[2,2,256,128]{3,2,1,0:T(8,128)} %get-tuple-element.80), channel_id=1, source_target_pairs={{1,0},{2,1},{3,2},{4,3},{5,4},{6,5},{7,6},{8,7},{9,8},{10,9},{11,1... | collective-permute-start | bytes 1572872 | tf_op jit(solution)/shard_map/ppermute | solution.py:899
  (23 other events, 153.2 us)

commit v3 on v2

--- a/solution.py
+++ b/solution.py
@@ -338,10 +338,14 @@
             pltpu.make_async_copy(mixed, out.at[:, :, aligned(HALF - self.at)], self.sems.at[n, 1]),
         ]
 
-    def start(self):
+    def start(self, first):
         for k in range(4):
-            for copy in self.copies(k, (lax.axis_index("cuts") - k) % 4):
-                copy.start()
+            n = (lax.axis_index("cuts") - k) % 4
+
+            @pl.when((n == 0) if first else (n != 0))
+            def _(k=k, n=n):
+                for copy in self.copies(k, n):
+                    copy.start()
 
     def wait(self, n):
         for copy in self.copies(0, n):
@@ -406,7 +410,7 @@
     back[1] = im
 
 
-def backward_steps(wins, turned_buf, back, kern, tab, store):
+def backward_steps(wins, turned_buf, back, kern, tab, store, fresh):
     def step(at, carry):
         n = 3 - at
         re, im = propagate(back[0], back[1], kern, tab, -1.0)
@@ -414,6 +418,8 @@
         turned_buf[n, 1] = im
         for k in range(4):
             pl.when((lax.axis_index("cuts") + k) % 4 == n)(lambda k=k: store(k, n).start())
+        if fresh:
+            wins.wait(n)
         wr, wi = wins.buf[n, 0], wins.buf[n, 1]
         back[0] = wr * re + wi * im
         back[1] = wr * im - wi * re
@@ -432,12 +438,13 @@
         consts = Loads((probe, tab, kern, order, order_t), bufs, const_sems)
         probe, tab, kern, order, order_t = bufs
         wins = Windows(refs, win_buf, pos[s, 1] > RIM, load_sems)
-        wins.start()
+        wins.start(True)
         seeing = pltpu.make_async_copy(measured.at[s], seen, sems.at[4])
         seeing.start()
         consts.wait(0)
         place_probe(probe, pos[s, 0], pos[s, 1], jnp.where(s < counts[0], 1.0, 0.0), in_buf.at[0])
         consts.wait(1, 2)
+        wins.start(False)
         forward_steps(wins, in_buf, kern, tab)
         stores = [
             pltpu.make_async_copy(in_buf.at[(group + k) % 4], inputs[k], sems.at[k])
@@ -479,16 +486,15 @@
         consts = Loads((back, tab, kern), (back_buf, *bufs), const_sems)
         tab, kern = bufs
         wins = Windows(refs, win_buf, pos[s, 1] > RIM, load_sems)
-        wins.start()
         consts.wait(0, 1, 2)
+        wins.start(True)
+        wins.start(False)
 
 
         def store(k, n):
             return pltpu.make_async_copy(turned_buf.at[n], turned[k], sems.at[k])
 
-        for n in range(4):
-            wins.wait(n)
-        backward_steps(wins, turned_buf, back_buf, kern, tab, store)
+        backward_steps(wins, turned_buf, back_buf, kern, tab, store, True)
         for k in range(4):
             store(k, 0).wait()
 
@@ -531,13 +537,14 @@
             consts = Loads((probe, tab, kern, order, order_t), bufs, const_sems)
             probe_buf, tab_buf, kern_buf, order_buf, order_t_buf = bufs
             wins = Windows(refs, win_buf, pos[s, 1] > RIM, load_sems)
-            wins.start()
+            wins.start(True)
             seeing = pltpu.make_async_copy(measured.at[s], seen, sems.at[8])
             seeing.start()
             scale = jnp.where(s < counts[0], 1.0, 0.0)
             consts.wait(0)
             place_probe(probe_buf, pos[s, 0], pos[s, 1], scale, in_buf.at[0])
             consts.wait(1, 2)
+            wins.start(False)
             forward_steps(wins, in_buf, kern_buf, tab_buf)
             stores = [
                 pltpu.make_async_copy(in_buf.at[(group + k) % 4], outs[k].at[0], sems.at[k])
@@ -548,7 +555,7 @@
             seeing.wait()
             consts.wait(3, 4)
             far_step(in_buf, seen, order_buf, order_t_buf, tab_buf, back_buf)
-            backward_steps(wins, turned_buf, back_buf, kern_buf, tab_buf, store)
+            backward_steps(wins, turned_buf, back_buf, kern_buf, tab_buf, store, False)
             for copy in stores:
                 copy.wait()
             for k in range(4):
@@ -841,27 +848,40 @@
 
 def add_rims(count, rows):
     def kernel(pos_left, pos_right, grad_in, left, right, grad, buf, more_buf, sems):
-        for s in range(count):
-            adders = [
-                AddInto(
-                    grad,
-                    pos[4 + s, 0],
-                    pl.ds(side * HALF, HALF),
-                    buf.at[side],
-                    more_buf.at[side],
-                    sems.at[side],
-                )
-                for side, pos in enumerate((pos_left, pos_right))
-            ]
-            for add in adders:
+        sides = ((pos_left, left), (pos_right, right))
+
+        def adder(s, side):
+            row, cols = sides[side][0][4 + s, 0], pl.ds(side * HALF, HALF)
+            return AddInto(
+                grad, row, cols, buf.at[s, side], more_buf.at[s, side], sems.at[s, side]
+            )
+
+        def add_slots(slots):
+            adders = [(s, side, adder(s, side)) for s in slots for side in range(2)]
+            for _, _, add in adders:
                 add.start(True)
-            for add, values in zip(adders, (left, right)):
+            for s, side, add in adders:
                 add.wait(True)
                 for part in range(2):
-                    add.add(part, LOW, values[s, part])
+                    add.add(part, LOW, sides[side][1][s, part])
                 add.start(False)
-            for add in adders:
+            for _, _, add in adders:
                 add.wait(False)
+
+        apart = jnp.bool_(True)
+        for pos, _ in sides:
+            for one in range(count):
+                for two in range(one):
+                    apart &= jnp.abs(pos[4 + one, 0] - pos[4 + two, 0]) >= W + 32
+
+        @pl.when(apart)
+        def _():
+            add_slots(range(count))
+
+        @pl.when(jnp.logical_not(apart))
+        def _():
+            for s in range(count):
+                add_slots([s])
 
     return pl.pallas_call(
         kernel,
@@ -869,9 +889,9 @@
         in_specs=[SMEM_SPEC] * 2 + [ANY_SPEC] + [VMEM_SPEC] * 2,
         out_specs=ANY_SPEC,
         scratch_shapes=[
-            pltpu.VMEM((2, 2, W, HALF), F32),
-            pltpu.VMEM((2, 2, 8, HALF), F32),
-            pltpu.SemaphoreType.DMA((2, 2)),
+            pltpu.VMEM((count, 2, 2, W, HALF), F32),
+            pltpu.VMEM((count, 2, 2, 8, HALF), F32),
+            pltpu.SemaphoreType.DMA((count, 2, 2)),
         ],
         input_output_aliases={2: 0},
         compiler_params=params(),

time: 192 us -> 191 us (level)
  transfers between devices with their start and end apart: 26 -> 26, of which waited for: 9 -> 9; matrix products, arithmetic and copies ran while one was open for 2% -> 2% of each run, Pallas kernels for 25% -> 24%
where the time goes in v3:
time: 191 us
  starting transfers between devices  62.2 us (33%)
  Pallas kernels  59.5 us (31%)
  waiting for transfers between devices  56.6 us (30%)
  local copies, waits for them, and re-layouts  7.51 us (4%)
  matrix products  2.08 us (1%)
  between operations  1.99 us (1%)
    ppermute x18, waiting for transfers between devices, shift(): return lax.ppermute(value, ('cuts', 'tile'), pairs)  54.6 us
    ppermute x18, starting transfers between devices, shift(): return lax.ppermute(value, ('cuts', 'tile'), pairs)  33.8 us
    ppermute x4, starting transfers between devices, to_up(): return lax.ppermute(value, 'tile', up)  19.1 us
    pallas_call x1, Pallas kernels, on_device(): *in1, back1 = forward_first()(pos, counts, *wide, *got_pure1, *got_mixed1)  10.6 us
    pallas_call x1, Pallas kernels, on_device(): finish(cap, rows)  9.78 us
    ppermute x4, starting transfers between devices, to_down(): return lax.ppermute(value, 'tile', down)  9.21 us
    pallas_call x1, Pallas kernels, on_device(): turned1 = backward_first()(pos, back1, kern, tab, *got_pure1, *got_mixed1)  8.97 us
    pallas_call x1, Pallas kernels, on_device(): terms_first(cap)  8.71 us
  transfers between devices with their start and end apart: 26, of which 9 were waited for; matrix products, arithmetic and copies ran while one was open for 2% of the time, Pallas kernels for 24%

profile of v3, /device:TPU:1, one launch (start us, length us, event | category | flops | bytes accessed | tf_op | source)
XLA Modules:
  0.0 190.7 jit_solution(2200060421284212748)
XLA Ops:
  1.5 3.3 %collective-permute-start.1 = (s32[6,2]{1,0:T(8,128)S(1)}, s32[6,2]{1,0:T(8,128)S(1)}, u32[]{:S(2)}, u32[]{:S(2)}) collective-permute-start(s32[6,2]{1,0:T(8,128)S(1)} %copy.22.pos), channel_id=1, source_target_pairs={{1,0},{2,1},{3,2},{4,3},{5,4},{6,5},{7,6},{8,7},{9,8},{10,9},{11,1... | collective-permute-start | bytes 152 | tf_op jit(solution)/shard_map/ppermute | solution.py:919
  4.8 3.2 %collective-permute-start = (s32[6,2]{1,0:T(8,128)S(1)}, s32[6,2]{1,0:T(8,128)S(1)}, u32[]{:S(2)}, u32[]{:S(2)}) collective-permute-start(s32[6,2]{1,0:T(8,128)S(1)} %copy.22.pos), channel_id=1, source_target_pairs={{0,1},{1,2},{2,3},{3,4},{4,5},{5,6},{6,7},{7,8},{8,9},{9,10},{10,1... | collective-permute-start | bytes 152 | tf_op jit(solution)/shard_map/ppermute | solution.py:916
  9.3 4.1 %cut_rims.1 = (f32[6,2,256,128]{3,2,1,0:T(8,128)}, f32[6,2,256,128]{3,2,1,0:T(8,128)}) custom-call(s32[6,2]{1,0:T(8,128)} %copy-done.28, s32[6,2]{1,0:T(8,128)} %copy-done.27, f32[2,4096,256]{2,1,0:T(8,128)} %bitcast.13), custom_call_target="tpu_custom_call" | custom-call | bytes 13200000 | tf_op jit(solution)/shard_map/cut_rims/pallas_call | solution.py:949
  13.4 4.2 %collective-permute-start.5 = (f32[6,2,256,128]{3,2,1,0:T(8,128)}, f32[6,2,256,128]{3,2,1,0:T(8,128)S(1)}, u32[]{:S(2)}, u32[]{:S(2)}) collective-permute-start(f32[6,2,256,128]{3,2,1,0:T(8,128)} %get-tuple-element.49), channel_id=1, source_target_pairs={{0,1},{1,2},{2,3},{3,4},{4,5},{5,6},{6,7},{7,8},{8,9},{9,10},{10,1... | collective-permute-start | bytes 4718600 | tf_op jit(solution)/shard_map/ppermute | solution.py:916
  17.6 2.1 %collective-permute-start.6 = (f32[6,2,256,128]{3,2,1,0:T(8,128)}, f32[6,2,256,128]{3,2,1,0:T(8,128)S(1)}, u32[]{:S(2)}, u32[]{:S(2)}) collective-permute-start(f32[6,2,256,128]{3,2,1,0:T(8,128)} %get-tuple-element.51), channel_id=1, source_target_pairs={{1,0},{2,1},{3,2},{4,3},{5,4},{6,5},{7,6},{8,7},{9,8},{10,9},{11,1... | collective-permute-start | bytes 4718600 | tf_op jit(solution)/shard_map/ppermute | solution.py:919
  19.7 3.1 %pure_halves.1 = (f32[2,256,128]{2,1,0:T(8,128)}, f32[2,256,128]{2,1,0:T(8,128)}, f32[2,256,128]{2,1,0:T(8,128)}, f32[2,256,128]{2,1,0:T(8,128)}) custom-call(s32[6,2]{1,0:T(8,128)} %copy-done.26, f32[2,4096,256]{2,1,0:T(8,128)} %bitcast.14), custom_call_target="tpu_custom_call" | custom-call | bytes 9900000 | tf_op jit(solution)/shard_map/pure_halves/pallas_call | solution.py:947
  22.8 1.7 collective-permute-start.2
  24.5 3.3 %collective-permute-start.3 = (f32[2,256,128]{2,1,0:T(8,128)}, f32[2,256,128]{2,1,0:T(8,128)S(1)}, u32[]{:S(2)}, u32[]{:S(2)}) collective-permute-start(f32[2,256,128]{2,1,0:T(8,128)} %get-tuple-element.47.rest_10_), channel_id=1, source_target_pairs={{0,64},{1,65},{2,66},{3,67},{4,68},{5,69},{6,70},{7,71},{8,72},{9,... | collective-permute-start | bytes 786440 | tf_op jit(solution)/shard_map/ppermute | solution.py:928
  28.9 1.7 cosine_bitcast_fusion
  32.0 6.3 %collective-permute-done.3.rest_2_ = f32[2,256,128]{2,1,0:T(8,128)S(1)} collective-permute-done((f32[2,256,128]{2,1,0:T(8,128)}, f32[2,256,128]{2,1,0:T(8,128)S(1)}, u32[]{:S(2)}, u32[]{:S(2)}) %collective-permute-start.3) | collective-permute-done | bytes 262176 | tf_op jit(solution)/shard_map/ppermute | solution.py:928
  40.8 4.1 %mixed_windows.1 = (f32[2,256,128]{2,1,0:T(8,128)}, f32[2,256,128]{2,1,0:T(8,128)}, f32[2,256,128]{2,1,0:T(8,128)}, f32[2,256,128]{2,1,0:T(8,128)}, f32[2,256,25...) custom-call(s32[6,2]{1,0:T(8,128)} %copy-done.26, s32[1,2]{1,0:T(1,128)} %widths.5, ...), custom_call_target="tpu_custom_call" | custom-call | bytes 16500000 | tf_op jit(solution)/shard_map/mixed_windows/pallas_call | solution.py:953
  44.9 1.7 collective-permute-start.7
  46.6 3.3 %collective-permute-start.8 = (f32[2,256,128]{2,1,0:T(8,128)}, f32[2,256,128]{2,1,0:T(8,128)S(1)}, u32[]{:S(2)}, u32[]{:S(2)}) collective-permute-start(f32[2,256,128]{2,1,0:T(8,128)} %get-tuple-element.54.rest_14_), channel_id=1, source_target_pairs={{0,64},{1,65},{2,66},{3,67},{4,68},{5,69},{6,70},{7,71},{8,72},{9,... | collective-permute-start | bytes 786440 | tf_op jit(solution)/shard_map/ppermute | solution.py:928
  50.6 3.6 %collective-permute-done.7.rest_5_ = f32[2,256,128]{2,1,0:T(8,128)S(1)} collective-permute-done((f32[2,256,128]{2,1,0:T(8,128)}, f32[2,256,128]{2,1,0:T(8,128)S(1)}, u32[]{:S(2)}, u32[]{:S(2)}) %collective-permute-start.7) | collective-permute-done | bytes 262176 | tf_op jit(solution)/shard_map/ppermute | solution.py:928
  54.3 7.1 %collective-permute-done.8.rest_6_ = f32[2,256,128]{2,1,0:T(8,128)S(1)} collective-permute-done((f32[2,256,128]{2,1,0:T(8,128)}, f32[2,256,128]{2,1,0:T(8,128)S(1)}, u32[]{:S(2)}, u32[]{:S(2)}) %collective-permute-start.8) | collective-permute-done | bytes 262176 | tf_op jit(solution)/shard_map/ppermute | solution.py:928
  61.3 3.0 %collective-permute-start.13 = (f32[2,256,256]{2,1,0:T(8,128)}, f32[2,256,256]{2,1,0:T(8,128)S(1)}, u32[]{:S(2)}, u32[]{:S(2)}) collective-permute-start(f32[2,256,256]{2,1,0:T(8,128)} %get-tuple-element.62.rest_5_), channel_id=1, source_target_pairs={{1,33},{3,35},{5,37},{7,39},{9,41},{11,43},{13,45},{15,47},{17,49}... | collective-permute-start | bytes 1572872 | tf_op jit(solution)/shard_map/ppermute | solution.py:928
  65.0 4.9 %collective-permute-start.15 = (f32[2,256,256]{2,1,0:T(8,128)}, f32[2,256,256]{2,1,0:T(8,128)S(1)}, u32[]{:S(2)}, u32[]{:S(2)}) collective-permute-start(f32[2,256,256]{2,1,0:T(8,128)} %get-tuple-element.66.rest_7_), channel_id=1, source_target_pairs={{1,97},{3,99},{5,101},{7,103},{9,105},{11,107},{13,109},{15,111},{... | collective-permute-start | bytes 1572872 | tf_op jit(solution)/shard_map/ppermute | solution.py:928
  70.6 10.6 %forward_first.1 = (f32[2,256,256]{2,1,0:T(8,128)}, f32[2,256,256]{2,1,0:T(8,128)}, f32[2,256,256]{2,1,0:T(8,128)}, f32[2,256,256]{2,1,0:T(8,128)}, f32[2,256,256]{2,1,0:T(8,128)}) custom-call(s32[6,2]{1,0:T(8,128)} %copy-done.26, s32[1]{0:T(128)S(6)} %copy.25.counts, f32[2,256,256]{2,1,0:T(8,128)} %probe.9, bf16[6,256,256]{2,1,0:T(8,128)(2,1)} %bitcast.17, ...), custom_call_target="tpu_custom_call" | custom-call | bytes 29700000 | tf_op jit(solution)/shard_map/forward_first/pallas_call | solution.py:959
  82.6 3.6 %collective-permute-start.11 = (f32[2,256,256]{2,1,0:T(8,128)}, f32[2,256,256]{2,1,0:T(8,128)S(1)}, u32[]{:S(2)}, u32[]{:S(2)}) collective-permute-start(f32[2,256,256]{2,1,0:T(8,128)} %get-tuple-element.58), channel_id=1, source_target_pairs={{0,64},{1,65},{2,66},{3,67},{4,68},{5,69},{6,70},{7,71},{8,72},{9,... | collective-permute-start | bytes 1572872 | tf_op jit(solution)/shard_map/ppermute | solution.py:928
  86.2 4.0 %collective-permute-start.12 = (f32[2,256,256]{2,1,0:T(8,128)}, f32[2,256,256]{2,1,0:T(8,128)S(1)}, u32[]{:S(2)}, u32[]{:S(2)}) collective-permute-start(f32[2,256,256]{2,1,0:T(8,128)} %get-tuple-element.59), channel_id=1, source_target_pairs={{0,96},{1,97},{2,98},{3,99},{4,100},{5,101},{6,102},{7,103},{8,104... | collective-permute-start | bytes 1572872 | tf_op jit(solution)/shard_map/ppermute | solution.py:928
  90.2 9.0 %backward_first.1 = (f32[2,256,256]{2,1,0:T(8,128)}, f32[2,256,256]{2,1,0:T(8,128)}, f32[2,256,256]{2,1,0:T(8,128)}, f32[2,256,256]{2,1,0:T(8,128)}) custom-call(s32[6,2]{1,0:T(8,128)} %copy-done.26, f32[2,256,256]{2,1,0:T(8,128)} %get-tuple-element.67.back, f32[2,256,256]{2,1,0:T(8,128)} %pad_maximum_fusion.kern, bf16[8,256,256]{2,1,0:T(8,128)(2,1)} %constant.5.clone.tab, ...), custom_call_target="tpu_custom_call" | custom-call | bytes 23100000 | tf_op jit(solution)/shard_map/backward_first/pallas_call | solution.py:962
  102.0 2.8 %collective-permute-done.11.rest_2_ = f32[2,256,256]{2,1,0:T(8,128)S(1)} collective-permute-done((f32[2,256,256]{2,1,0:T(8,128)}, f32[2,256,256]{2,1,0:T(8,128)S(1)}, u32[]{:S(2)}, u32[]{:S(2)}) %collective-permute-start.11) | collective-permute-done | bytes 524320 | tf_op jit(solution)/shard_map/ppermute | solution.py:928
  106.1 13.8 %collective-permute-done.12.rest_3_ = f32[2,256,256]{2,1,0:T(8,128)S(1)} collective-permute-done((f32[2,256,256]{2,1,0:T(8,128)}, f32[2,256,256]{2,1,0:T(8,128)S(1)}, u32[]{:S(2)}, u32[]{:S(2)}) %collective-permute-start.12) | collective-permute-done | bytes 524320 | tf_op jit(solution)/shard_map/ppermute | solution.py:928
  121.9 20.4 %collective-permute-done.18.rest_7_ = f32[2,256,256]{2,1,0:T(8,128)S(1)} collective-permute-done((f32[2,256,256]{2,1,0:T(8,128)}, f32[2,256,256]{2,1,0:T(8,128)S(1)}, u32[]{:S(2)}, u32[]{:S(2)}) %collective-permute-start.18) | collective-permute-done | bytes 524320 | tf_op jit(solution)/shard_map/ppermute | solution.py:928
  143.3 8.7 %terms_first.1 = (f32[6,2,256,256]{3,2,1,0:T(8,128)}, f32[4,2,256,256]{3,2,1,0:T(8,128)}, f32[4,2,256,128]{3,2,1,0:T(8,128)}, f32[4,2,256,128]{3,2,1,0:T(8,128)}) custom-call(s32[6,2]{1,0:T(8,128)} %copy-done.26, s32[1]{0:T(128)S(6)} %copy.25.counts, s32[1,2]{1,0:T(1,128)} %widths.5, f32[2,256,256]{2,1,0:T(8,128)} %probe.9, ...), custom_call_target="tpu_custom_call" | custom-call | bytes 23100000 | tf_op jit(solution)/shard_map/terms_first/pallas_call | solution.py:968
  152.1 4.6 %collective-permute-start.22 = (f32[4,2,256,128]{3,2,1,0:T(8,128)}, f32[4,2,256,128]{3,2,1,0:T(8,128)S(1)}, u32[]{:S(2)}, u32[]{:S(2)}) collective-permute-start(f32[4,2,256,128]{3,2,1,0:T(8,128)} %get-tuple-element.82), channel_id=1, source_target_pairs={{0,1},{1,2},{2,3},{3,4},{4,5},{5,6},{6,7},{7,8},{8,9},{9,10},{10,1... | collective-permute-start | bytes 3145736 | tf_op jit(solution)/shard_map/ppermute | solution.py:916
  156.7 1.9 %collective-permute-start.23 = (f32[4,2,256,128]{3,2,1,0:T(8,128)}, f32[4,2,256,128]{3,2,1,0:T(8,128)S(1)}, u32[]{:S(2)}, u32[]{:S(2)}) collective-permute-start(f32[4,2,256,128]{3,2,1,0:T(8,128)} %get-tuple-element.83), channel_id=1, source_target_pairs={{1,0},{2,1},{3,2},{4,3},{5,4},{6,5},{7,6},{8,7},{9,8},{10,9},{11,1... | collective-permute-start | bytes 3145736 | tf_op jit(solution)/shard_map/ppermute | solution.py:919
  160.3 4.1 %rims_second.1 = (f32[2,2,256,128]{3,2,1,0:T(8,128)}, f32[2,2,256,128]{3,2,1,0:T(8,128)}) custom-call(s32[6,2]{1,0:T(8,128)} %copy-done.26, s32[1]{0:T(128)S(6)} %copy.25.counts, s32[1,2]{1,0:T(1,128)} %widths.5, f32[2,256,256]{2,1,0:T(8,128)} %probe.9, f32[2,2,256,256]{3,2,1,0:T(8,128)} %get-tuple-element.76.rest_0_, f32[2,2,256,256]{3,2,1,0:T(8,128)} %copy-done.1, ...), custom_call_target="tpu_custom_call" | custom-call | bytes 9900000 | tf_op jit(solution)/shard_map/rims_second/pallas_call | solution.py:972
  164.4 7.1 %collective-permute-start.24 = (f32[2,2,256,128]{3,2,1,0:T(8,128)}, f32[2,2,256,128]{3,2,1,0:T(8,128)S(1)}, u32[]{:S(2)}, u32[]{:S(2)}) collective-permute-start(f32[2,2,256,128]{3,2,1,0:T(8,128)} %get-tuple-element.87), channel_id=1, source_target_pairs={{0,1},{1,2},{2,3},{3,4},{4,5},{5,6},{6,7},{7,8},{8,9},{9,10},{10,1... | collective-permute-start | bytes 1572872 | tf_op jit(solution)/shard_map/ppermute | solution.py:916
  171.5 1.9 %collective-permute-start.25 = (f32[2,2,256,128]{3,2,1,0:T(8,128)}, f32[2,2,256,128]{3,2,1,0:T(8,128)S(1)}, u32[]{:S(2)}, u32[]{:S(2)}) collective-permute-start(f32[2,2,256,128]{3,2,1,0:T(8,128)} %get-tuple-element.80), channel_id=1, source_target_pairs={{1,0},{2,1},{3,2},{4,3},{5,4},{6,5},{7,6},{8,7},{9,8},{10,9},{11,1... | collective-permute-start | bytes 1572872 | tf_op jit(solution)/shard_map/ppermute | solution.py:919
  174.8 9.8 %finish.1 = (f32[6,2,256,256]{3,2,1,0:T(8,128)}, f32[2,4096,256]{2,1,0:T(8,128)}) custom-call(s32[6,2]{1,0:T(8,128)} %copy-done.26, s32[6,2]{1,0:T(8,128)} %copy-done.28, s32[6,2]{1,0:T(8,128)} %copy-done.27, s32[1]{0:T(128)S(6)} %copy.25.counts, f32[2,256,256]{2,1,0:T(8,128)} %probe.9, ...), custom_call_target="tpu_custom_call", output_to_operand_aliasing={{0}: (8, {})} | custom-call | bytes 29700000 | tf_op jit(solution)/shard_map/finish/pallas_call | solution.py:975
  185.7 4.9 %add_rims.1 = f32[2,4096,256]{2,1,0:T(8,128)} custom-call(s32[6,2]{1,0:T(8,128)} %copy-done.28, s32[6,2]{1,0:T(8,128)} %copy-done.27, f32[2,4096,256]{2,1,0:T(8,128)} %get-tuple-element.86.grad_in, f32[2,2,256,128]{3,2,1,0:T(8,128)} %copy-done.24, f32[2,2,256,128]{3,2,1,0:T(8,128)} %copy-done.25), custom_call_target="tpu_custom_call", output_to_operand_aliasing={{}: (2, {})} | custom-call | bytes 13200000 | tf_op jit(solution)/shard_map/add_rims/pallas_call | solution.py:979
  (92 shorter events, 20.8 us)
Async XLA Ops:
  0.6 27.9 %copy-start = (f32[256,256]{1,0:T(8,128)S(1)}, f32[256,256]{1,0:T(8,128)}, u32[]{:S(2)}) copy-start(f32[256,256]{1,0:T(8,128)} %param.11) | copy-start | bytes 786436
  1.5 6.5 %collective-permute-start.1 = (s32[6,2]{1,0:T(8,128)S(1)}, s32[6,2]{1,0:T(8,128)S(1)}, u32[]{:S(2)}, u32[]{:S(2)}) collective-permute-start(s32[6,2]{1,0:T(8,128)S(1)} %copy.22.pos), channel_id=1, source_target_pairs={{1,0},{2,1},{3,2},{4,3},{5,4},{6,5},{7,6},{8,7},{9,8},{10,9},{11,1... | collective-permute-start | bytes 152 | tf_op jit(solution)/shard_map/ppermute | solution.py:919
  4.8 3.9 %collective-permute-start = (s32[6,2]{1,0:T(8,128)S(1)}, s32[6,2]{1,0:T(8,128)S(1)}, u32[]{:S(2)}, u32[]{:S(2)}) collective-permute-start(s32[6,2]{1,0:T(8,128)S(1)} %copy.22.pos), channel_id=1, source_target_pairs={{0,1},{1,2},{2,3},{3,4},{4,5},{5,6},{6,7},{7,8},{8,9},{9,10},{10,1... | collective-permute-start | bytes 152 | tf_op jit(solution)/shard_map/ppermute | solution.py:916
  13.4 25.0 %collective-permute-start.5 = (f32[6,2,256,128]{3,2,1,0:T(8,128)}, f32[6,2,256,128]{3,2,1,0:T(8,128)S(1)}, u32[]{:S(2)}, u32[]{:S(2)}) collective-permute-start(f32[6,2,256,128]{3,2,1,0:T(8,128)} %get-tuple-element.49), channel_id=1, source_target_pairs={{0,1},{1,2},{2,3},{3,4},{4,5},{5,6},{6,7},{7,8},{8,9},{9,10},{10,1... | collective-permute-start | bytes 4718600 | tf_op jit(solution)/shard_map/ppermute | solution.py:916
  17.6 22.1 %collective-permute-start.6 = (f32[6,2,256,128]{3,2,1,0:T(8,128)}, f32[6,2,256,128]{3,2,1,0:T(8,128)S(1)}, u32[]{:S(2)}, u32[]{:S(2)}) collective-permute-start(f32[6,2,256,128]{3,2,1,0:T(8,128)} %get-tuple-element.51), channel_id=1, source_target_pairs={{1,0},{2,1},{3,2},{4,3},{5,4},{6,5},{7,6},{8,7},{9,8},{10,9},{11,1... | collective-permute-start | bytes 4718600 | tf_op jit(solution)/shard_map/ppermute | solution.py:919
  22.8 9.2 %collective-permute-start.2 = (f32[2,256,128]{2,1,0:T(8,128)}, f32[2,256,128]{2,1,0:T(8,128)S(1)}, u32[]{:S(2)}, u32[]{:S(2)}) collective-permute-start(f32[2,256,128]{2,1,0:T(8,128)} %get-tuple-element.46.rest_9_), channel_id=1, source_target_pairs={{0,32},{1,33},{2,34},{3,35},{4,36},{5,37},{6,38},{7,39},{8,40},{9,... | collective-permute-start | bytes 786440 | tf_op jit(solution)/shard_map/ppermute | solution.py:928
  24.5 13.9 %collective-permute-start.3 = (f32[2,256,128]{2,1,0:T(8,128)}, f32[2,256,128]{2,1,0:T(8,128)S(1)}, u32[]{:S(2)}, u32[]{:S(2)}) collective-permute-start(f32[2,256,128]{2,1,0:T(8,128)} %get-tuple-element.47.rest_10_), channel_id=1, source_target_pairs={{0,64},{1,65},{2,66},{3,67},{4,68},{5,69},{6,70},{7,71},{8,72},{9,... | collective-permute-start | bytes 786440 | tf_op jit(solution)/shard_map/ppermute | solution.py:928
  27.8 10.6 %collective-permute-start.4 = (f32[2,256,128]{2,1,0:T(8,128)}, f32[2,256,128]{2,1,0:T(8,128)S(1)}, u32[]{:S(2)}, u32[]{:S(2)}) collective-permute-start(f32[2,256,128]{2,1,0:T(8,128)} %get-tuple-element.48.rest_11_), channel_id=1, source_target_pairs={{0,96},{1,97},{2,98},{3,99},{4,100},{5,101},{6,102},{7,103},{8,104... | collective-permute-start | bytes 786440 | tf_op jit(solution)/shard_map/ppermute | solution.py:928
  32.0 38.5 %copy-start.8 = (f32[2,256,128]{2,1,0:T(8,128)}, f32[2,256,128]{2,1,0:T(8,128)S(1)}, u32[]{:S(2)}) copy-start(f32[2,256,128]{2,1,0:T(8,128)S(1)} %collective-permute-done.2.rest_1_) | copy-start | bytes 786436
  38.4 32.2 %copy-start.9 = (f32[2,256,128]{2,1,0:T(8,128)}, f32[2,256,128]{2,1,0:T(8,128)S(1)}, u32[]{:S(2)}) copy-start(f32[2,256,128]{2,1,0:T(8,128)S(1)} %collective-permute-done.3.rest_2_) | copy-start | bytes 786436
  38.4 32.2 %copy-start.10 = (f32[2,256,128]{2,1,0:T(8,128)}, f32[2,256,128]{2,1,0:T(8,128)S(1)}, u32[]{:S(2)}) copy-start(f32[2,256,128]{2,1,0:T(8,128)S(1)} %collective-permute-done.4.rest_3_) | copy-start | bytes 786436
  44.9 9.3 %collective-permute-start.7 = (f32[2,256,128]{2,1,0:T(8,128)}, f32[2,256,128]{2,1,0:T(8,128)S(1)}, u32[]{:S(2)}, u32[]{:S(2)}) collective-permute-start(f32[2,256,128]{2,1,0:T(8,128)} %get-tuple-element.53.rest_13_), channel_id=1, source_target_pairs={{0,32},{1,33},{2,34},{3,35},{4,36},{5,37},{6,38},{7,39},{8,40},{9,... | collective-permute-start | bytes 786440 | tf_op jit(solution)/shard_map/ppermute | solution.py:928
  46.6 14.7 %collective-permute-start.8 = (f32[2,256,128]{2,1,0:T(8,128)}, f32[2,256,128]{2,1,0:T(8,128)S(1)}, u32[]{:S(2)}, u32[]{:S(2)}) collective-permute-start(f32[2,256,128]{2,1,0:T(8,128)} %get-tuple-element.54.rest_14_), channel_id=1, source_target_pairs={{0,64},{1,65},{2,66},{3,67},{4,68},{5,69},{6,70},{7,71},{8,72},{9,... | collective-permute-start | bytes 786440 | tf_op jit(solution)/shard_map/ppermute | solution.py:928
  49.9 11.4 %collective-permute-start.9 = (f32[2,256,128]{2,1,0:T(8,128)}, f32[2,256,128]{2,1,0:T(8,128)S(1)}, u32[]{:S(2)}, u32[]{:S(2)}) collective-permute-start(f32[2,256,128]{2,1,0:T(8,128)} %get-tuple-element.55.rest_15_), channel_id=1, source_target_pairs={{0,96},{1,97},{2,98},{3,99},{4,100},{5,101},{6,102},{7,103},{8,104... | collective-permute-start | bytes 786440 | tf_op jit(solution)/shard_map/ppermute | solution.py:928
  61.3 24.9 %collective-permute-start.13 = (f32[2,256,256]{2,1,0:T(8,128)}, f32[2,256,256]{2,1,0:T(8,128)S(1)}, u32[]{:S(2)}, u32[]{:S(2)}) collective-permute-start(f32[2,256,256]{2,1,0:T(8,128)} %get-tuple-element.62.rest_5_), channel_id=1, source_target_pairs={{1,33},{3,35},{5,37},{7,39},{9,41},{11,43},{13,45},{15,47},{17,49}... | collective-permute-start | bytes 1572872 | tf_op jit(solution)/shard_map/ppermute | solution.py:928
  64.3 25.9 %collective-permute-start.14 = (f32[2,256,256]{2,1,0:T(8,128)}, f32[2,256,256]{2,1,0:T(8,128)S(1)}, u32[]{:S(2)}, u32[]{:S(2)}) collective-permute-start(f32[2,256,256]{2,1,0:T(8,128)} %get-tuple-element.64.rest_6_), channel_id=1, source_target_pairs={{0,64},{2,66},{4,68},{6,70},{8,72},{10,74},{12,76},{14,78},{16,80}... | collective-permute-start | bytes 1572872 | tf_op jit(solution)/shard_map/ppermute | solution.py:928
  65.0 25.2 %collective-permute-start.15 = (f32[2,256,256]{2,1,0:T(8,128)}, f32[2,256,256]{2,1,0:T(8,128)S(1)}, u32[]{:S(2)}, u32[]{:S(2)}) collective-permute-start(f32[2,256,256]{2,1,0:T(8,128)} %get-tuple-element.66.rest_7_), channel_id=1, source_target_pairs={{1,97},{3,99},{5,101},{7,103},{9,105},{11,107},{13,109},{15,111},{... | collective-permute-start | bytes 1572872 | tf_op jit(solution)/shard_map/ppermute | solution.py:928
  81.3 18.1 %collective-permute-start.10 = (f32[2,256,256]{2,1,0:T(8,128)}, f32[2,256,256]{2,1,0:T(8,128)S(1)}, u32[]{:S(2)}, u32[]{:S(2)}) collective-permute-start(f32[2,256,256]{2,1,0:T(8,128)} %get-tuple-element.57), channel_id=1, source_target_pairs={{0,32},{1,33},{2,34},{3,35},{4,36},{5,37},{6,38},{7,39},{8,40},{9,... | collective-permute-start | bytes 1572872 | tf_op jit(solution)/shard_map/ppermute | solution.py:928
  82.6 22.2 %collective-permute-start.11 = (f32[2,256,256]{2,1,0:T(8,128)}, f32[2,256,256]{2,1,0:T(8,128)S(1)}, u32[]{:S(2)}, u32[]{:S(2)}) collective-permute-start(f32[2,256,256]{2,1,0:T(8,128)} %get-tuple-element.58), channel_id=1, source_target_pairs={{0,64},{1,65},{2,66},{3,67},{4,68},{5,69},{6,70},{7,71},{8,72},{9,... | collective-permute-start | bytes 1572872 | tf_op jit(solution)/shard_map/ppermute | solution.py:928
  86.2 33.7 %collective-permute-start.12 = (f32[2,256,256]{2,1,0:T(8,128)}, f32[2,256,256]{2,1,0:T(8,128)S(1)}, u32[]{:S(2)}, u32[]{:S(2)}) collective-permute-start(f32[2,256,256]{2,1,0:T(8,128)} %get-tuple-element.59), channel_id=1, source_target_pairs={{0,96},{1,97},{2,98},{3,99},{4,100},{5,101},{6,102},{7,103},{8,104... | collective-permute-start | bytes 1572872 | tf_op jit(solution)/shard_map/ppermute | solution.py:928
  99.2 21.4 %collective-permute-start.17 = (f32[2,256,256]{2,1,0:T(8,128)}, f32[2,256,256]{2,1,0:T(8,128)S(1)}, u32[]{:S(2)}, u32[]{:S(2)}) collective-permute-start(f32[2,256,256]{2,1,0:T(8,128)} %get-tuple-element.70), channel_id=1, source_target_pairs={{0,64},{1,65},{2,66},{3,67},{4,68},{5,69},{6,70},{7,71},{8,72},{9,... | collective-permute-start | bytes 1572872 | tf_op jit(solution)/shard_map/ppermute | solution.py:928
  99.3 43.1 %collective-permute-start.18 = (f32[2,256,256]{2,1,0:T(8,128)}, f32[2,256,256]{2,1,0:T(8,128)S(1)}, u32[]{:S(2)}, u32[]{:S(2)}) collective-permute-start(f32[2,256,256]{2,1,0:T(8,128)} %get-tuple-element.71), channel_id=1, source_target_pairs={{0,96},{1,97},{2,98},{3,99},{4,100},{5,101},{6,102},{7,103},{8,104... | collective-permute-start | bytes 1572872 | tf_op jit(solution)/shard_map/ppermute | solution.py:928
  99.4 43.0 %copy-start.15 = (f32[2,256,256]{2,1,0:T(8,128)}, f32[2,256,256]{2,1,0:T(8,128)S(1)}, u32[]{:S(2)}) copy-start(f32[2,256,256]{2,1,0:T(8,128)S(1)} %collective-permute-done.10.rest_1_) | copy-start | bytes 1572868
  99.4 43.0 %collective-permute-start.16 = (f32[2,256,256]{2,1,0:T(8,128)}, f32[2,256,256]{2,1,0:T(8,128)S(1)}, u32[]{:S(2)}, u32[]{:S(2)}) collective-permute-start(f32[2,256,256]{2,1,0:T(8,128)} %get-tuple-element.69), channel_id=1, source_target_pairs={{0,32},{1,33},{2,34},{3,35},{4,36},{5,37},{6,38},{7,39},{8,40},{9,... | collective-permute-start | bytes 1572872 | tf_op jit(solution)/shard_map/ppermute | solution.py:928
  104.8 37.6 %copy-start.16 = (f32[2,256,256]{2,1,0:T(8,128)}, f32[2,256,256]{2,1,0:T(8,128)S(1)}, u32[]{:S(2)}) copy-start(f32[2,256,256]{2,1,0:T(8,128)S(1)} %collective-permute-done.11.rest_2_) | copy-start | bytes 1572868
  104.8 53.8 %collective-permute-start.19 = (f32[2,2,256,256]{3,2,1,0:T(8,128)}, f32[2,2,256,256]{3,2,1,0:T(8,128)S(1)}, u32[]{:S(2)}, u32[]{:S(2)}) collective-permute-start(f32[2,2,256,256]{3,2,1,0:T(8,128)} %get-tuple-element.77), channel_id=1, source_target_pairs={{0,32},{2,34},{4,36},{6,38},{8,40},{10,42},{12,44},{14,46},{16,48}... | collective-permute-start | bytes 3145736 | tf_op jit(solution)/shard_map/ppermute | solution.py:928
  119.9 38.8 %collective-permute-start.20 = (f32[2,2,256,256]{3,2,1,0:T(8,128)}, f32[2,2,256,256]{3,2,1,0:T(8,128)S(1)}, u32[]{:S(2)}, u32[]{:S(2)}) collective-permute-start(f32[2,2,256,256]{3,2,1,0:T(8,128)} %get-tuple-element.78), channel_id=1, source_target_pairs={{0,64},{2,66},{4,68},{6,70},{8,72},{10,74},{12,76},{14,78},{16,80}... | collective-permute-start | bytes 3145736 | tf_op jit(solution)/shard_map/ppermute | solution.py:928
  120.6 38.0 %collective-permute-start.21 = (f32[2,2,256,256]{3,2,1,0:T(8,128)}, f32[2,2,256,256]{3,2,1,0:T(8,128)S(1)}, u32[]{:S(2)}, u32[]{:S(2)}) collective-permute-start(f32[2,2,256,256]{3,2,1,0:T(8,128)} %get-tuple-element.79), channel_id=1, source_target_pairs={{0,96},{2,98},{4,100},{6,102},{8,104},{10,106},{12,108},{14,110},{... | collective-permute-start | bytes 3145736 | tf_op jit(solution)/shard_map/ppermute | solution.py:928
  152.1 21.4 %collective-permute-start.22 = (f32[4,2,256,128]{3,2,1,0:T(8,128)}, f32[4,2,256,128]{3,2,1,0:T(8,128)S(1)}, u32[]{:S(2)}, u32[]{:S(2)}) collective-permute-start(f32[4,2,256,128]{3,2,1,0:T(8,128)} %get-tuple-element.82), channel_id=1, source_target_pairs={{0,1},{1,2},{2,3},{3,4},{4,5},{5,6},{6,7},{7,8},{8,9},{9,10},{10,1... | collective-permute-start | bytes 3145736 | tf_op jit(solution)/shard_map/ppermute | solution.py:916
  156.7 16.8 %collective-permute-start.23 = (f32[4,2,256,128]{3,2,1,0:T(8,128)}, f32[4,2,256,128]{3,2,1,0:T(8,128)S(1)}, u32[]{:S(2)}, u32[]{:S(2)}) collective-permute-start(f32[4,2,256,128]{3,2,1,0:T(8,128)} %get-tuple-element.83), channel_id=1, source_target_pairs={{1,0},{2,1},{3,2},{4,3},{5,4},{6,5},{7,6},{8,7},{9,8},{10,9},{11,1... | collective-permute-start | bytes 3145736 | tf_op jit(solution)/shard_map/ppermute | solution.py:919
  164.4 20.3 %collective-permute-start.24 = (f32[2,2,256,128]{3,2,1,0:T(8,128)}, f32[2,2,256,128]{3,2,1,0:T(8,128)S(1)}, u32[]{:S(2)}, u32[]{:S(2)}) collective-permute-start(f32[2,2,256,128]{3,2,1,0:T(8,128)} %get-tuple-element.87), channel_id=1, source_target_pairs={{0,1},{1,2},{2,3},{3,4},{4,5},{5,6},{6,7},{7,8},{8,9},{9,10},{10,1... | collective-permute-start | bytes 1572872 | tf_op jit(solution)/shard_map/ppermute | solution.py:916
  171.5 13.1 %collective-permute-start.25 = (f32[2,2,256,128]{3,2,1,0:T(8,128)}, f32[2,2,256,128]{3,2,1,0:T(8,128)S(1)}, u32[]{:S(2)}, u32[]{:S(2)}) collective-permute-start(f32[2,2,256,128]{3,2,1,0:T(8,128)} %get-tuple-element.80), channel_id=1, source_target_pairs={{1,0},{2,1},{3,2},{4,3},{5,4},{6,5},{7,6},{8,7},{9,8},{10,9},{11,1... | collective-permute-start | bytes 1572872 | tf_op jit(solution)/shard_map/ppermute | solution.py:919
  (23 other events, 151.6 us)
